TPU v7x, 128 devices: a whole 4x4x4 slice. The times are simulated.
128 devices in a mesh: fsdp: 2 (over y_hi), tile: 32 (over z, x, core), scan: 2 (over y_lo).
Axes of the slice: x: 4, y: 4 (y_hi: 2, y_lo: 2; y = y_hi * 2 + y_lo), z: 4, core: 2. Of those that a mesh axis runs over, the one named last changes fastest.
Arguments:
- acts: bfloat16 [2, 2, 16, 64, 64, 512], P('scan', 'fsdp', None, 'tile'), may hold values from -6 to 6
- spatial_weight: bfloat16 [9, 512, 512], P(None, None, 'fsdp'), may hold values from -0.09375 to 0.09375
- temporal_weight: bfloat16 [3, 512, 512], P(None, None, 'fsdp'), may hold values from -0.15625 to 0.15625
- readout_weight: bfloat16 [2, 4096, 512], P('scan', 'tile'), may hold values from -0.25 to 0.25
- readout_bias: bfloat16 [2, 4096], P('scan', 'tile'), may hold values from -1.5 to 0.5
- tile_of: int32 [2, 4096, 1], P('scan', 'tile'), may hold values from 0 to 31; in each aligned block of 128 rows (0 to 127, 128 to 255, ..., all dimensions but the last counted through in order) at most 10 rows name the same one
- row_of: int32 [2, 4096], P('scan', 'tile'), may hold values from 0 to 1
- column_of: int32 [2, 4096], P('scan', 'tile'), may hold values from 0 to 63
- spikes: int32 [2, 2, 16, 4096], P('scan', 'fsdp', None, 'tile'), may hold values from 0 to 5
Outputs:
- spatial_grad: float32 [9, 512, 512], P(None, None, 'fsdp')
- temporal_grad: float32 [3, 512, 512], P(None, None, 'fsdp')
- readout_grad: float32 [2, 4096, 512], P('scan', 'tile')
- bias_grad: float32 [2, 4096], P('scan', 'tile')
Inputs may be any that keep to these rules, and one draw needn't show every extreme that they name: `tile_of`: among the 128 neurons of one index of tile (aligned blocks of a scan's neurons), at most 10 read one tile.
All inputs are finite; a program needn't handle non-finite values.
Results may differ from a plain program's by a relative error of at most 0.006.
Values may be sent and summed in bfloat16 or wider, within the bound.
No kernel may reach another device: no remote copies, remote signals or barrier semaphores. Data moves between devices by JAX's collectives and lax.ppermute only.
A program may use at most 192 MiB of HBM per device.

v0:
```python
import jax
import jax.numpy as jnp
from jax import lax
from jax.sharding import Mesh, PartitionSpec as P


BF = jnp.bfloat16
F32 = jnp.float32
TILE = ("z", "x", "core")
PACK = 640


def contract_rows(left, right):
    return lax.dot_general(left, right, (((0,), (0,)), ((), ())), preferred_element_type=F32)


def swap(value, axis, kind):
    if axis == "core":
        pairs = ((0, 1),)
    elif kind == 0:
        pairs = ((0, 1), (2, 3))
    else:
        pairs = ((1, 2), (3, 0))
    name = ("fsdp", "scan") if axis == "y" else axis
    perm = [pair for a, b in pairs for pair in ((a, b), (b, a))]
    return lax.ppermute(value, name, perm)


def bit(axis, kind):
    if axis == "core":
        return lax.axis_index("core")
    if axis == "y":
        place = lax.axis_index("fsdp") * 2 + lax.axis_index("scan")
    else:
        place = lax.axis_index(axis)
    return place >> 1 if kind else (place ^ (place >> 1)) & 1


def halve(value, axis, kind, flip=0):
    size = value.shape[0] // 2
    mine = bit(axis, kind) ^ flip
    sent = lax.dynamic_slice_in_dim(value, (1 - mine) * size, size, 0)
    kept = lax.dynamic_slice_in_dim(value, mine * size, size, 0)
    return kept.astype(F32) + swap(sent.astype(BF), axis, kind).astype(F32)


def own_columns(value):
    cols = value.shape[1] // 6
    own, far = (
        jnp.concatenate([value[:, (2 * g + h) * cols :][:, :cols] for g in range(3)], axis=1)
        for h in range(2)
    )
    return own.astype(F32) + swap(far.astype(BF), "y", 1).astype(F32)


def share(value, axis, kind):
    value = value.astype(BF)
    return value.astype(F32) + swap(value, axis, kind).astype(F32)


def double(value, axis, kind, dim):
    other = swap(value, axis, kind)
    first = bit(axis, kind) == 0
    return jnp.concatenate(
        [jnp.where(first, value, other), jnp.where(first, other, value)], axis=dim
    )


def blocks_of(spatial, temporal):
    color = bit("x", 0) ^ (bit("x", 1) * 2) ^ (bit("z", 0) * 3)
    rows, cols = spatial.shape[1] // 2, spatial.shape[2]
    core = lax.axis_index("core")
    start = core * rows
    taps = lax.dynamic_slice(spatial, (3 * jnp.minimum(color, 2), start, 0), (3, rows, cols))
    lags = lax.dynamic_slice_in_dim(temporal, start, rows, 1)
    part = jnp.where(color == 3, lags, taps)
    part = jnp.concatenate([part[0], part[1], part[2]], axis=1)
    part = swap(part, "y", 1)
    parts = [part, swap(part, "x", 0), swap(part, "x", 1), swap(part, "z", 0)]
    mine = jnp.stack(parts)
    other = swap(mine, "core", 0)
    both = jnp.stack([mine, other])

    def block(half, group):
        index = (half ^ core, group ^ color, 0, 0)
        return lax.dynamic_slice(both, index, (1, 1, rows, 3 * cols))[0, 0]

    return block


def edges(block):
    count = 1
    for axis in TILE:
        count *= lax.axis_size(axis)
    forward = [(i, i + 1) for i in range(count - 1)]
    backward = [(b, a) for a, b in forward]
    low = lax.ppermute(block[:, -1:], TILE, forward)
    high = lax.ppermute(block[:, :1], TILE, backward)
    return low, high


def shift(value, step):
    if step == 0:
        return value
    zeros = jnp.zeros_like(value[:, :, :1])
    if step > 0:
        return jnp.concatenate([value[:, :, 1:], zeros], axis=2)
    return jnp.concatenate([zeros, value[:, :, :-1]], axis=2)


def compute(
    acts,
    spatial_weight,
    temporal_weight,
    readout_weight,
    readout_bias,
    tile_of,
    row_of,
    column_of,
    spikes,
):
    fsdp = lax.axis_index("fsdp")
    block = blocks_of(spatial_weight, temporal_weight)
    frames_in = acts[0, 0]
    frames, rows, width, channels = frames_in.shape
    half = channels // 2
    cells = rows * width
    tile_count = lax.axis_size("z") * lax.axis_size("x") * lax.axis_size("core")
    rep_count = lax.axis_size("fsdp")
    neurons = readout_weight.shape[1]
    capacity = max(2, 5 * neurons // (2 * tile_count))
    slot_count = tile_count * capacity
    scale_factor = 1.0 / (rep_count * frames)
    low, high = edges(frames_in)

    def local(value):
        return jnp.where(
            fsdp == 0, value, jnp.concatenate([value[:, half:], value[:, :half]], axis=1)
        )

    tile_ids = tile_of[0, :, 0]
    cell_ids = row_of[0] * width + column_of[0]
    same_tile = tile_ids[:, None] == tile_ids[None, :]
    order = jnp.arange(neurons)
    rank_ids = jnp.sum((same_tile & (order[None, :] < order[:, None])).astype(jnp.int32), axis=1)
    slot_ids = tile_ids * capacity + rank_ids
    selector = (slot_ids[None, :] == jnp.arange(slot_count)[:, None]).astype(BF)
    table = jnp.concatenate(
        [
            local(readout_weight[0]),
            readout_bias[0][:, None],
            cell_ids.astype(BF)[:, None],
            jnp.ones((neurons, 1), BF),
            spikes[0, 0].T.astype(BF),
            jnp.zeros((neurons, PACK - channels - 3 - frames), BF),
        ],
        axis=1,
    )
    packed = jnp.dot(selector, table, preferred_element_type=F32).astype(BF)
    held = lax.all_to_all(
        packed.reshape(tile_count, capacity, PACK),
        TILE,
        split_axis=0,
        concat_axis=0,
        tiled=True,
    ).reshape(slot_count, PACK)
    slot_weight = held[:, :channels]
    extras = held[:, channels : channels + 3 + frames].astype(F32)
    slot_bias = extras[:, 0]
    slot_cell = jnp.where(extras[:, 2] > 0.5, extras[:, 1].astype(jnp.int32), cells)
    slot_spikes = extras[:, 3:].T

    shifted_rows = [
        jnp.concatenate([low, frames_in[:, :1]], axis=1).reshape(-1, channels),
        frames_in.reshape(-1, channels),
        jnp.concatenate([frames_in[:, 1:], high], axis=1).reshape(-1, channels),
    ]
    taller = jnp.concatenate(shifted_rows, axis=1)

    def convolve(weights):
        sums = jnp.dot(taller, weights, preferred_element_type=F32)
        sums = sums.reshape(frames, rows, width, 3 * half)
        total = (
            shift(sums[..., :half], -1)
            + sums[..., half : 2 * half]
            + shift(sums[..., 2 * half :], 1)
        )
        return total.astype(BF).reshape(frames, cells, half)

    near_weights = jnp.concatenate(
        [
            jnp.concatenate([spatial_weight[3 * a + b] for b in range(3)], axis=1)
            for a in range(3)
        ]
    )
    near_out = convolve(near_weights)
    far_out = convolve(jnp.concatenate([block(h, g) for g in range(3) for h in range(2)]))
    spatial_out = jnp.concatenate([near_out, far_out], axis=2)

    lag_blocks = [block(q ^ fsdp, 3) for q in range(2)]
    temporal = [
        jnp.concatenate(
            [
                jnp.concatenate(
                    [
                        lax.dynamic_slice_in_dim(temporal_weight[lag], (q ^ fsdp) * half, half, 0),
                        lag_blocks[q][:, lag * half : (lag + 1) * half],
                    ],
                    axis=1,
                )
                for q in range(2)
            ]
        )
        for lag in range(3)
    ]
    causal = jnp.pad(spatial_out, ((2, 0), (0, 0), (0, 0)))
    mixed = jnp.zeros((frames * cells, channels), F32)
    for lag in range(3):
        mixed = mixed + jnp.dot(
            causal[2 - lag : 2 - lag + frames].reshape(-1, channels),
            temporal[lag],
            preferred_element_type=F32,
        )
    features = jax.nn.elu(mixed).astype(BF)

    here = jnp.arange(cells)[:, None] == slot_cell[None, :]
    scores = lax.dot_general(
        features, slot_weight, (((1,), (1,)), ((), ())), preferred_element_type=F32
    ).reshape(frames, cells, slot_count)
    logits = jnp.sum(jnp.where(here[None], scores, 0.0), axis=1) + slot_bias[None, :]
    delta = (jnp.exp(logits) - slot_spikes) * scale_factor
    spread = jnp.where(here[None], delta[:, None, :], 0.0).astype(BF).reshape(-1, slot_count)
    feature_grad = jnp.dot(spread, slot_weight, preferred_element_type=F32)
    slope = jnp.where(mixed > 0, 1.0, jnp.exp(jnp.minimum(mixed, 0.0)))
    mixed_grad = (feature_grad * slope).astype(BF)
    back_pad = jnp.pad(mixed_grad.reshape(frames, cells, channels), ((0, 2), (0, 0), (0, 0)))
    later = jnp.concatenate(
        [back_pad[lag : lag + frames].reshape(-1, channels) for lag in range(3)], axis=1
    )
    grad_t = contract_rows(spatial_out.reshape(-1, channels), later)
    part_t = halve(grad_t, "core", 0, fsdp)

    slot_grad = contract_rows(spread, features)
    slot_bias_grad = jnp.sum(delta, axis=0)
    back = jnp.concatenate(
        [slot_grad, slot_bias_grad[:, None], jnp.zeros((slot_count, PACK - channels - 1), F32)],
        axis=1,
    ).astype(BF)

    spatial_back = lax.dot_general(
        later,
        jnp.concatenate(temporal, axis=1),
        (((1,), (1,)), ((), ())),
        preferred_element_type=F32,
    )
    spatial_back = spatial_back.reshape(frames, rows, width, channels)
    wider = jnp.concatenate(
        [shift(spatial_back, 1 - b).astype(BF).reshape(-1, channels) for b in range(3)], axis=1
    )
    part_t = halve(part_t, "x", 0)
    grad_0 = contract_rows(shifted_rows[0], wider)
    part_0 = halve(grad_0, "core", 0)
    grad_1 = contract_rows(shifted_rows[1], wider)
    part_1 = halve(grad_1, "core", 0)
    part_0 = own_columns(part_0)
    grad_2 = contract_rows(shifted_rows[2], wider)
    part_2 = halve(grad_2, "core", 0)
    part_t = halve(part_t, "y", 0)
    part_1 = halve(part_1, "x", 0)
    part_2 = own_columns(part_2)
    part_t = halve(part_t, "z", 0)
    part_0 = halve(part_0, "x", 1)
    part_1 = halve(part_1, "y", 0)
    part_0 = halve(part_0, "z", 1)
    part_2 = halve(part_2, "x", 1)
    part_1 = halve(part_1, "z", 0)
    part_2 = halve(part_2, "z", 1)

    returned = lax.all_to_all(
        back.reshape(tile_count, capacity, PACK), TILE, split_axis=0, concat_axis=0, tiled=True
    ).reshape(slot_count, PACK)
    mine = contract_rows(selector, returned)
    mine = jnp.concatenate([local(mine[:, :channels]), mine[:, channels:]], axis=1).astype(BF)
    other = lax.ppermute(mine, "fsdp", [(0, 1), (1, 0)])
    summed = mine.astype(F32) + other.astype(F32)
    weight_grad = summed[:, :channels]
    bias_grad = summed[:, channels]

    odd = jnp.concatenate([part_t, part_1])
    even = jnp.concatenate([part_0, part_2])
    odd = own_columns(odd)
    even = share(even, "x", 0)
    odd = share(odd, "x", 1)
    even = share(even, "y", 0)
    odd = share(odd, "z", 1)
    even = share(even, "z", 0)
    odd = odd.astype(BF).reshape(2, -1, odd.shape[1])
    even = even.astype(BF).reshape(2, -1, even.shape[1])
    odd = double(odd, "z", 0, 1)
    even = double(even, "z", 1, 1)
    odd = double(odd, "y", 0, 1)
    even = double(even, "x", 1, 1)
    odd = double(odd, "x", 0, 1)
    even = double(even, "core", 0, 1)
    odd = double(odd, "core", 0, 1)

    def taps(value):
        return [value[:, b * half : (b + 1) * half].astype(F32) for b in range(3)]

    total_temporal = jnp.stack(taps(odd[0]))
    total_spatial = jnp.stack(taps(even[0]) + taps(odd[1]) + taps(even[1]))
    return (total_spatial, total_temporal, weight_grad[None], bias_grad[None])


def solution(mesh):
    shape = mesh.devices.shape
    split = Mesh(
        mesh.devices.reshape(shape[0], 4, 4, 2, shape[2]), ("fsdp", "z", "x", "core", "scan")
    )
    return jax.shard_map(
        compute,
        mesh=split,
        in_specs=(
            P("scan", "fsdp", None, TILE, None, None),
            P(None, None, "fsdp"),
            P(None, None, "fsdp"),
            P("scan", TILE, None),
            P("scan", TILE),
            P("scan", TILE, None),
            P("scan", TILE),
            P("scan", TILE),
            P("scan", "fsdp", None, TILE),
        ),
        out_specs=(
            P(None, None, "fsdp"),
            P(None, None, "fsdp"),
            P("scan", TILE, None),
            P("scan", TILE),
        ),
        check_vma=False,
    )
```

profile of v0, /device:TPU:1, one launch (start us, length us, event | category | flops | bytes accessed | tf_op | source)
XLA Modules:
  0.0 234.3 jit_solution(11692610636235411789)
XLA Ops:
  7.9 9.4 %all-to-all-start = ((bf16[32,10,640]{2,1,0:T(8,128)(2,1)}), bf16[32,10,640]{2,1,0:T(8,128)(2,1)S(1)}, u32[]{:S(2)}, u32[]{:S(2)}) async-start(bf16[32,10,640]{2,1,0:T(8,128)(2,1)} %reshape.177), calls=%async_computation | async-start | bytes 1310720 | tf_op jit(solution)/shard_map/all_to_all | solution.py:160
  19.3 2.7 %collective-permute-start.2 = (bf16[256,768]{1,0:T(8,128)(2,1)}, bf16[256,768]{1,0:T(8,128)(2,1)}, u32[]{:S(2)}, u32[]{:S(2)}) collective-permute-start(bf16[256,768]{1,0:T(8,128)(2,1)} %pad_maximum_fusion.18), channel_id=1, source_target_pairs={{1,64},{64,1},{65,0},{0,65},{3,66},{66,3},{67,2},{2,67},{5,68},{68... | collective-permute-start | bytes 1179656 | tf_op jit(solution)/shard_map/ppermute | solution.py:26
  22.0 1.7 fusion.150
  23.7 3.8 %collective-permute-start = (bf16[16,1,64,512]{3,2,1,0:T(8,128)(2,1)S(1)}, bf16[16,1,64,512]{3,2,1,0:T(8,128)(2,1)}, u32[]{:S(2)}, u32[]{:S(2)}) collective-permute-start(bf16[16,1,64,512]{3,2,1,0:T(8,128)(2,1)S(1)} %get-tuple-element.31), channel_id=1, source_target_pairs={{0,2},{2,4},{4,6},{6,8},{8,10},{10,12},{12,14},{14,16},{16,18},{18... | collective-permute-start | bytes 3145736 | tf_op jit(solution)/shard_map/ppermute | solution.py:97
  27.5 1.9 collective-permute-start.1
  29.5 3.0 %slice_bitcast_fusion.21 = (bf16[512,256]{1,0:T(8,128)(2,1)}, bf16[512,256]{1,0:T(8,128)(2,1)}, bf16[512,256]{1,0:T(8,128)(2,1)}, bf16[512,256]{1,0:T(8,128)(2,1...) fusion(bf16[9,512,256]{2,1,0:T(8,128)(2,1)} %param.10), kind=kLoop, calls=%fused_computation.236 | loop fusion | bytes 4718592 | tf_op jit(solution)/shard_map/squeeze | solution.py:192
  35.8 2.4 %collective-permute-start.4 = (bf16[256,768]{1,0:T(8,128)(2,1)}, bf16[256,768]{1,0:T(8,128)(2,1)}, u32[]{:S(2)}, u32[]{:S(2)}) collective-permute-start(bf16[256,768]{1,0:T(8,128)(2,1)} %collective-permute-done.2), channel_id=1, source_target_pairs={{4,8},{8,4},{12,0},{0,12},{5,9},{9,5},{13,1},{1,13},{6,10},{10,6},... | collective-permute-start | bytes 1179656 | tf_op jit(solution)/shard_map/ppermute | solution.py:26
  40.1 9.7 %collective-permute-done.5 = bf16[256,768]{1,0:T(8,128)(2,1)} collective-permute-done((bf16[256,768]{1,0:T(8,128)(2,1)}, bf16[256,768]{1,0:T(8,128)(2,1)}, u32[]{:S(2)}, u32[]{:S(2)}) %collective-permute-start.5) | collective-permute-done | bytes 393248 | tf_op jit(solution)/shard_map/ppermute | solution.py:26
  49.9 2.7 %fusion.141 = (bf16[1,4,256,768]{3,2,1,0:T(8,128)(2,1)S(1)}, bf16[4,256,768]{2,1,0:T(8,128)(2,1)}) fusion(bf16[1,256,768]{2,1,0:T(8,128)(2,1)} %bitcast.27, bf16[1,256,768]{2,1,0:T(8,128)(2,1)} %bitcast.26, bf16[1,256,768]{2,1,0:T(8,128)(2,1)} %bitcast.25, bf16[1,256,768]{2,1,0:T(8,128)(2,1)} %bitcast.24), kind=kLoop, calls=%fused_computation.304 | loop fusion | flops 2359296 | bytes 4718592 | tf_op jit(solution)/shard_map/stack | solution.py:82
  52.7 3.1 %collective-permute-start.6 = (bf16[4,256,768]{2,1,0:T(8,128)(2,1)}, bf16[4,256,768]{2,1,0:T(8,128)(2,1)S(1)}, u32[]{:S(2)}, u32[]{:S(2)}) collective-permute-start(bf16[4,256,768]{2,1,0:T(8,128)(2,1)} %get-tuple-element.48), channel_id=1, source_target_pairs={{0,2},{2,0},{1,3},{3,1},{4,6},{6,4},{5,7},{7,5},{8,10},{10,8},{9,1... | collective-permute-start | bytes 4718600 | tf_op jit(solution)/shard_map/ppermute | solution.py:26
  57.3 2.2 pad_maximum_fusion.8
  60.4 6.1 %fusion.7 = f32[2048,768]{1,0:T(8,128)S(1)} fusion(bf16[2048,512]{1,0:T(8,128)(2,1)S(1)} %bitcast.219, bf16[2048,512]{1,0:T(8,128)(2,1)S(1)} %bitcast.213, bf16[2048,512]{1,0:T(8,128)(2,1)S(1)} %bitcast.216, bf16[512,256]{1,0:T(8,128)(2,1)} %get-tuple-element.26, bf16[512,256]{1,0:T(8,128)(2,1)S(1)} %copy-done.13, bf16[512,256]{1,0:T(8,128)(2,1)S(1)} %copy-done.14, ...), kind=kOutput, calls=%fused_computation.34 | convolution fusion | flops 4871946240 | bytes 14942208 | tf_op jit(solution)/shard_map/dot_general | solution.py:181
  70.1 5.1 %fusion.6 = f32[2048,768]{1,0:T(8,128)S(1)} fusion(bf16[1536,768]{1,0:T(8,128)(2,1)S(1)} %bitcast_dynamic-update-slice_fusion, bf16[2048,512]{1,0:T(8,128)(2,1)S(1)} %bitcast.220, bf16[2048,512]{1,0:T(8,128)(2,1)S(1)} %bitcast.214, bf16[2048,512]{1,0:T(8,128)(2,1)S(1)} %bitcast.217), kind=kOutput, calls=%fused_computation.33 | convolution fusion | flops 4850712576 | bytes 14942208 | tf_op jit(solution)/shard_map/dot_general | solution.py:181
  81.0 1.5 add_add_fusion
  82.6 2.0 convolution_bitcast_fusion
  88.1 1.9 fusion.5
  90.5 3.5 %convolution_convert_fusion = bf16[2048,512]{1,0:T(8,128)(2,1)S(1)} fusion(bf16[2048,512]{1,0:T(8,128)(2,1)S(1)} %bitcast.210, bf16[2048,512]{1,0:T(8,128)(2,1)S(1)} %bitcast.208, bf16[2048,512]{1,0:T(8,128)(2,1)S(1)} %fusion.5, bf16[256,256]{1,0:T(8,128)(2,1)S(1)} %get-tuple-element.98, bf16[256,256]{1,0:T(8,128)(2,1)S(1)} %get-tuple-element.82, ...), kind=kOutput, calls=%fused_computation.30 | convolution fusion | flops 3260022784 | bytes 9961472 | tf_op jit(solution)/shard_map/dot_general | solution.py:250
  94.0 5.2 %fusion.8 = f32[512,1536]{1,0:T(8,128)} fusion(bf16[2048,512]{1,0:T(8,128)(2,1)S(1)} %bitcast.211, bf16[2048,512]{1,0:T(8,128)(2,1)S(1)} %bitcast.209, bf16[2048,512]{1,0:T(8,128)(2,1)S(1)} %fusion.5, bf16[2048,256]{1,0:T(8,128)(2,1)S(1)} %bitcast.206, bf16[2048,256]{1,0:T(8,128)(2,1)S(1)} %bitcast.203), kind=kOutput, calls=%fused_computation.35 | convolution fusion | flops 3244294144 | bytes 11534336 | tf_op jit(solution)/shard_map/dot_general | solution.py:14
  102.1 5.5 %fusion.139 = f32[512,1536]{1,0:T(8,128)} fusion(bf16[2048,512]{1,0:T(8,128)(2,1)S(1)} %bitcast.221, bf16[2048,512]{1,0:T(8,128)(2,1)S(1)} %bitcast.225, bf16[2048,512]{1,0:T(8,128)(2,1)S(1)} %convolution_convert_fusion, bf16[2048,512]{1,0:T(8,128)(2,1)S(1)} %bitcast.222), kind=kOutput, calls=%fused_computation.302 | convolution fusion | flops 3240099840 | bytes 11534336 | tf_op jit(solution)/shard_map/dot_general | solution.py:14
  107.6 5.3 %fusion.140 = f32[512,1536]{1,0:T(8,128)} fusion(bf16[2048,512]{1,0:T(8,128)(2,1)S(1)} %bitcast.218, bf16[2048,512]{1,0:T(8,128)(2,1)S(1)} %bitcast.226, bf16[2048,512]{1,0:T(8,128)(2,1)S(1)} %convolution_convert_fusion, bf16[2048,512]{1,0:T(8,128)(2,1)S(1)} %bitcast.223), kind=kOutput, calls=%fused_computation.303 | convolution fusion | flops 3240099840 | bytes 11534336 | tf_op jit(solution)/shard_map/dot_general | solution.py:14
  113.0 5.9 %fusion.138 = f32[1536,512]{0,1:T(8,128)} fusion(bf16[2048,512]{1,0:T(8,128)(2,1)S(1)} %bitcast.215, bf16[2048,512]{1,0:T(8,128)(2,1)S(1)} %bitcast.227, bf16[2048,512]{1,0:T(8,128)(2,1)S(1)} %convolution_convert_fusion, bf16[2048,512]{1,0:T(8,128)(2,1)S(1)} %bitcast.224), kind=kOutput, calls=%fused_computation.301 | convolution fusion | flops 3240099840 | bytes 11534336 | tf_op jit(solution)/shard_map/dot_general | solution.py:14
  119.8 4.5 %fusion.59 = bf16[32,10,512]{2,0,1:T(8,128)(2,1)S(1)} fusion(bf16[32,10,2048]{2,1,0:T(8,128)(2,1)S(1)} %dot_general.63, f32[2048,512]{1,0:T(8,128)} %copy-done), kind=kOutput, calls=%fused_computation.109 | convolution fusion | flops 675446784 | bytes 5832704 | tf_op jit(solution)/shard_map/dot_general | solution.py:14
  125.4 8.5 %all-to-all-start.1 = ((bf16[32,10,640]{2,1,0:T(8,128)(2,1)}), bf16[32,10,640]{2,1,0:T(8,128)(2,1)S(1)}, u32[]{:S(2)}, u32[]{:S(2)}) async-start(bf16[32,10,640]{2,1,0:T(8,128)(2,1)} %copy.33), calls=%async_computation.1 | async-start | bytes 1310720 | tf_op jit(solution)/shard_map/all_to_all | solution.py:279
  133.9 2.4 %dynamic-slice_convert_fusion.1 = bf16[256,1536]{1,0:T(8,128)(2,1)} fusion(f32[512,1536]{1,0:T(8,128)} %fusion.8, s32[]{:T(128)S(6)} %select_n.276), kind=kLoop, calls=%fused_computation.99 | loop fusion | bytes 1572868 | tf_op jit(solution)/shard_map/convert_element_type | solution.py:44
  136.5 2.4 %dynamic-slice_convert_fusion.2 = bf16[256,1536]{1,0:T(8,128)(2,1)} fusion(f32[512,1536]{1,0:T(8,128)} %fusion.139, s32[]{:T(128)S(6)} %select_n.261), kind=kLoop, calls=%fused_computation.101 | loop fusion | bytes 1572868 | tf_op jit(solution)/shard_map/convert_element_type | solution.py:44
  140.7 2.4 %dynamic-slice_convert_fusion.3 = bf16[256,1536]{1,0:T(8,128)(2,1)} fusion(f32[512,1536]{1,0:T(8,128)} %fusion.140, s32[]{:T(128)S(6)} %select_n.261), kind=kLoop, calls=%fused_computation.103 | loop fusion | bytes 1572868 | tf_op jit(solution)/shard_map/convert_element_type | solution.py:44
  143.5 3.2 %all-to-all-done.1 = bf16[32,10,640]{2,1,0:T(8,128)(2,1)S(1)} async-done(((bf16[32,10,640]{2,1,0:T(8,128)(2,1)}), bf16[32,10,640]{2,1,0:T(8,128)(2,1)S(1)}, u32[]{:S(2)}, u32[]{:S(2)}) %all-to-all-start.1) | async-done | bytes 409632 | tf_op jit(solution)/shard_map/all_to_all | solution.py:279
  147.3 2.0 convert_add_fusion
  151.8 2.1 collective-permute-start.8
  156.4 3.5 %collective-permute-done.22 = bf16[128,1536]{1,0:T(8,128)(2,1)S(1)} collective-permute-done((bf16[128,1536]{1,0:T(8,128)(2,1)S(1)}, bf16[128,1536]{1,0:T(8,128)(2,1)S(1)}, u32[]{:S(2)}, u32[]{:S(2)}) %collective-permute-start.22) | collective-permute-done | bytes 393248 | tf_op jit(solution)/shard_map/ppermute | solution.py:26
  160.1 2.1 collective-permute-done.12
  163.4 7.3 %collective-permute-done.8 = bf16[256,768]{1,0:T(8,128)(2,1)S(1)} collective-permute-done((bf16[256,768]{1,0:T(8,128)(2,1)S(1)}, bf16[256,768]{1,0:T(8,128)(2,1)S(1)}, u32[]{:S(2)}, u32[]{:S(2)}) %collective-permute-start.8) | collective-permute-done | bytes 393248 | tf_op jit(solution)/shard_map/ppermute | solution.py:26
  173.5 3.8 %collective-permute-done.9 = bf16[128,768]{1,0:T(8,128)(2,1)S(1)} collective-permute-done((bf16[128,768]{1,0:T(8,128)(2,1)S(1)}, bf16[128,768]{1,0:T(8,128)(2,1)S(1)}, u32[]{:S(2)}, u32[]{:S(2)}) %collective-permute-start.9) | collective-permute-done | bytes 196640 | tf_op jit(solution)/shard_map/ppermute | solution.py:26
  177.4 1.6 collective-permute-start.10
  179.7 2.9 %collective-permute-done.28 = bf16[32,1536]{1,0:T(8,128)(2,1)S(1)} collective-permute-done((bf16[32,1536]{1,0:T(8,128)(2,1)S(1)}, bf16[32,1536]{1,0:T(8,128)(2,1)S(1)}, u32[]{:S(2)}, u32[]{:S(2)}) %collective-permute-start.28) | collective-permute-done | bytes 98336 | tf_op jit(solution)/shard_map/ppermute | solution.py:26
  183.0 4.4 %collective-permute-done.29 = bf16[64,768]{1,0:T(8,128)(2,1)S(1)} collective-permute-done((bf16[64,768]{1,0:T(8,128)(2,1)S(1)}, bf16[64,768]{1,0:T(8,128)(2,1)S(1)}, u32[]{:S(2)}, u32[]{:S(2)}) %collective-permute-start.29) | collective-permute-done | bytes 98336 | tf_op jit(solution)/shard_map/ppermute | solution.py:26
  188.0 4.2 %collective-permute-done.30 = bf16[64,768]{1,0:T(8,128)(2,1)S(1)} collective-permute-done((bf16[64,768]{1,0:T(8,128)(2,1)S(1)}, bf16[64,768]{1,0:T(8,128)(2,1)S(1)}, u32[]{:S(2)}, u32[]{:S(2)}) %collective-permute-start.30) | collective-permute-done | bytes 98336 | tf_op jit(solution)/shard_map/ppermute | solution.py:26
  193.6 3.7 %collective-permute-done.31 = bf16[64,768]{1,0:T(8,128)(2,1)S(1)} collective-permute-done((bf16[64,768]{1,0:T(8,128)(2,1)S(1)}, bf16[64,768]{1,0:T(8,128)(2,1)S(1)}, u32[]{:S(2)}, u32[]{:S(2)}) %collective-permute-start.31) | collective-permute-done | bytes 98336 | tf_op jit(solution)/shard_map/ppermute | solution.py:26
  199.3 1.6 collective-permute-done.32
  201.0 2.3 collective-permute-done.17
  203.3 1.7 collective-permute-start.18
  205.0 2.1 collective-permute-done.33
  207.4 1.7 collective-permute-done.18
  209.2 1.5 collective-permute-start.19
  210.7 3.2 %collective-permute-done.34 = bf16[2,128,768]{2,1,0:T(8,128)(2,1)S(1)} collective-permute-done((bf16[2,128,768]{2,1,0:T(8,128)(2,1)S(1)}, bf16[2,128,768]{2,1,0:T(8,128)(2,1)S(1)}, u32[]{:S(2)}, u32[]{:S(2)}) %collective-permute-start.34) | collective-permute-done | bytes 393248 | tf_op jit(solution)/shard_map/ppermute | solution.py:26
  214.1 8.3 %collective-permute-start.35 = (bf16[2,256,768]{2,1,0:T(8,128)(2,1)S(1)}, bf16[2,256,768]{2,1,0:T(8,128)(2,1)S(1)}, u32[]{:S(2)}, u32[]{:S(2)}) collective-permute-start(bf16[2,256,768]{2,1,0:T(8,128)(2,1)S(1)} %pad_maximum_fusion.16), channel_id=1, source_target_pairs={{0,2},{2,0},{1,3},{3,1},{4,6},{6,4},{5,7},{7,5},{8,10},{10,8},{9,1... | collective-permute-start | bytes 2359304 | tf_op jit(solution)/shard_map/ppermute | solution.py:26
  224.0 4.9 %collective-permute-start.20 = (bf16[2,256,768]{2,1,0:T(8,128)(2,1)S(1)}, bf16[2,256,768]{2,1,0:T(8,128)(2,1)S(1)}, u32[]{:S(2)}, u32[]{:S(2)}) collective-permute-start(bf16[2,256,768]{2,1,0:T(8,128)(2,1)S(1)} %pad_maximum_fusion.15), channel_id=1, source_target_pairs={{0,2},{2,0},{1,3},{3,1},{4,6},{6,4},{5,7},{7,5},{8,10},{10,8},{9,1... | collective-permute-start | bytes 2359304 | tf_op jit(solution)/shard_map/ppermute | solution.py:26
  231.5 2.6 %stack.102 = f32[9,512,256]{2,1,0:T(8,128)} convert(bf16[9,512,256]{2,1,0:T(8,128)(2,1)S(1)} %fusion.108) | non-fusion elementwise | flops 1179648 | bytes 7077888 | tf_op jit(solution)/shard_map/stack | solution.py:311
  (237 shorter events, 56.5 us)
Async XLA Ops:
  0.6 16.7 %copy-start.8 = (bf16[3,512,256]{2,1,0:T(8,128)(2,1)S(1)}, bf16[3,512,256]{2,1,0:T(8,128)(2,1)}, u32[]{:S(2)}) copy-start(bf16[3,512,256]{2,1,0:T(8,128)(2,1)} %param.11) | copy-start | bytes 2359300
  2.2 5.6 %copy-start.24 = (s32[128]{0:T(128)}, s32[128]{0:T(128)S(1)}, u32[]{:S(2)}) copy-start(s32[128]{0:T(128)S(1)} %multiply_add_fusion) | copy-start | bytes 1540
  7.9 30.3 %all-to-all-start = ((bf16[32,10,640]{2,1,0:T(8,128)(2,1)}), bf16[32,10,640]{2,1,0:T(8,128)(2,1)S(1)}, u32[]{:S(2)}, u32[]{:S(2)}) async-start(bf16[32,10,640]{2,1,0:T(8,128)(2,1)} %reshape.177), calls=%async_computation | async-start | bytes 1310720 | tf_op jit(solution)/shard_map/all_to_all | solution.py:160
  19.3 15.4 %collective-permute-start.2 = (bf16[256,768]{1,0:T(8,128)(2,1)}, bf16[256,768]{1,0:T(8,128)(2,1)}, u32[]{:S(2)}, u32[]{:S(2)}) collective-permute-start(bf16[256,768]{1,0:T(8,128)(2,1)} %pad_maximum_fusion.18), channel_id=1, source_target_pairs={{1,64},{64,1},{65,0},{0,65},{3,66},{66,3},{67,2},{2,67},{5,68},{68... | collective-permute-start | bytes 1179656 | tf_op jit(solution)/shard_map/ppermute | solution.py:26
  23.7 32.1 %collective-permute-start = (bf16[16,1,64,512]{3,2,1,0:T(8,128)(2,1)S(1)}, bf16[16,1,64,512]{3,2,1,0:T(8,128)(2,1)}, u32[]{:S(2)}, u32[]{:S(2)}) collective-permute-start(bf16[16,1,64,512]{3,2,1,0:T(8,128)(2,1)S(1)} %get-tuple-element.31), channel_id=1, source_target_pairs={{0,2},{2,4},{4,6},{6,8},{8,10},{10,12},{12,14},{14,16},{16,18},{18... | collective-permute-start | bytes 3145736 | tf_op jit(solution)/shard_map/ppermute | solution.py:97
  27.5 29.8 %collective-permute-start.1 = (bf16[16,1,64,512]{3,2,1,0:T(8,128)(2,1)S(1)}, bf16[16,1,64,512]{3,2,1,0:T(8,128)(2,1)}, u32[]{:S(2)}, u32[]{:S(2)}) collective-permute-start(bf16[16,1,64,512]{3,2,1,0:T(8,128)(2,1)S(1)} %get-tuple-element.32), channel_id=1, source_target_pairs={{2,0},{4,2},{6,4},{8,6},{10,8},{12,10},{14,12},{16,14},{18,16},{20... | collective-permute-start | bytes 3145736 | tf_op jit(solution)/shard_map/ppermute | solution.py:98
  34.6 15.2 %collective-permute-start.5 = (bf16[256,768]{1,0:T(8,128)(2,1)}, bf16[256,768]{1,0:T(8,128)(2,1)}, u32[]{:S(2)}, u32[]{:S(2)}) collective-permute-start(bf16[256,768]{1,0:T(8,128)(2,1)} %collective-permute-done.2), channel_id=1, source_target_pairs={{0,16},{16,0},{32,48},{48,32},{1,17},{17,1},{33,49},{49,33},{2,18}... | collective-permute-start | bytes 1179656 | tf_op jit(solution)/shard_map/ppermute | solution.py:26
  35.8 14.1 %collective-permute-start.4 = (bf16[256,768]{1,0:T(8,128)(2,1)}, bf16[256,768]{1,0:T(8,128)(2,1)}, u32[]{:S(2)}, u32[]{:S(2)}) collective-permute-start(bf16[256,768]{1,0:T(8,128)(2,1)} %collective-permute-done.2), channel_id=1, source_target_pairs={{4,8},{8,4},{12,0},{0,12},{5,9},{9,5},{13,1},{1,13},{6,10},{10,6},... | collective-permute-start | bytes 1179656 | tf_op jit(solution)/shard_map/ppermute | solution.py:26
  38.2 11.7 %collective-permute-start.3 = (bf16[256,768]{1,0:T(8,128)(2,1)}, bf16[256,768]{1,0:T(8,128)(2,1)}, u32[]{:S(2)}, u32[]{:S(2)}) collective-permute-start(bf16[256,768]{1,0:T(8,128)(2,1)} %collective-permute-done.2), channel_id=1, source_target_pairs={{0,4},{4,0},{8,12},{12,8},{1,5},{5,1},{9,13},{13,9},{2,6},{6,2},{1... | collective-permute-start | bytes 1179656 | tf_op jit(solution)/shard_map/ppermute | solution.py:26
  52.7 15.0 %collective-permute-start.6 = (bf16[4,256,768]{2,1,0:T(8,128)(2,1)}, bf16[4,256,768]{2,1,0:T(8,128)(2,1)S(1)}, u32[]{:S(2)}, u32[]{:S(2)}) collective-permute-start(bf16[4,256,768]{2,1,0:T(8,128)(2,1)} %get-tuple-element.48), channel_id=1, source_target_pairs={{0,2},{2,0},{1,3},{3,1},{4,6},{6,4},{5,7},{7,5},{8,10},{10,8},{9,1... | collective-permute-start | bytes 4718600 | tf_op jit(solution)/shard_map/ppermute | solution.py:26
  57.2 11.5 %copy-start.2 = (bf16[16,2,64,512]{3,2,1,0:T(8,128)(2,1)}, bf16[16,2,64,512]{3,2,1,0:T(8,128)(2,1)S(1)}, u32[]{:S(2)}) copy-start(bf16[16,2,64,512]{3,2,1,0:T(8,128)(2,1)S(1)} %pad_maximum_fusion.7) | copy-start | bytes 6291460
  59.5 6.9 %copy-start.4 = (bf16[16,2,64,512]{3,2,1,0:T(8,128)(2,1)}, bf16[16,2,64,512]{3,2,1,0:T(8,128)(2,1)S(1)}, u32[]{:S(2)}) copy-start(bf16[16,2,64,512]{3,2,1,0:T(8,128)(2,1)S(1)} %pad_maximum_fusion.8) | copy-start | bytes 6291460
  82.6 5.5 %copy-start = (f32[2048,512]{1,0:T(8,128)}, f32[2048,512]{1,0:T(8,128)S(1)}, u32[]{:S(2)}) copy-start(f32[2048,512]{1,0:T(8,128)S(1)} %add_add_fusion) | copy-start | bytes 12582916
  102.1 5.5 %copy-start.3 = (bf16[16,2,64,512]{3,2,1,0:T(8,128)(2,1)S(1)}, bf16[16,2,64,512]{3,2,1,0:T(8,128)(2,1)}, u32[]{:S(2)}) copy-start(bf16[16,2,64,512]{3,2,1,0:T(8,128)(2,1)} %copy-done.2) | copy-start | bytes 6291460
  119.8 4.5 %copy-start.22 = (bf16[640]{0:T(1024)(128)(2,1)S(1)}, bf16[640]{0:T(1024)(128)(2,1)}, u32[]{:S(2)}) copy-start(bf16[640]{0:T(1024)(128)(2,1)} %pad.24.clone) | copy-start | bytes 3844
  125.4 21.3 %all-to-all-start.1 = ((bf16[32,10,640]{2,1,0:T(8,128)(2,1)}), bf16[32,10,640]{2,1,0:T(8,128)(2,1)S(1)}, u32[]{:S(2)}, u32[]{:S(2)}) async-start(bf16[32,10,640]{2,1,0:T(8,128)(2,1)} %copy.33), calls=%async_computation.1 | async-start | bytes 1310720 | tf_op jit(solution)/shard_map/all_to_all | solution.py:279
  136.3 11.0 %collective-permute-start.21 = (bf16[256,1536]{1,0:T(8,128)(2,1)}, bf16[256,1536]{1,0:T(8,128)(2,1)}, u32[]{:S(2)}, u32[]{:S(2)}) collective-permute-start(bf16[256,1536]{1,0:T(8,128)(2,1)} %dynamic-slice_convert_fusion.1), channel_id=1, source_target_pairs={{0,2},{2,0},{1,3},{3,1},{4,6},{6,4},{5,7},{7,5},{8,10},{10,8},{9,1... | collective-permute-start | bytes 2359304 | tf_op jit(solution)/shard_map/ppermute | solution.py:26
  138.9 8.0 %copy-start.25 = (s32[128]{0:T(128)S(1)}, s32[128]{0:T(128)}, u32[]{:S(2)}) copy-start(s32[128]{0:T(128)} %copy-done.24) | copy-start | bytes 1540
  138.9 11.4 %collective-permute-start.11 = (bf16[256,1536]{1,0:T(8,128)(2,1)}, bf16[256,1536]{1,0:T(8,128)(2,1)S(1)}, u32[]{:S(2)}, u32[]{:S(2)}) collective-permute-start(bf16[256,1536]{1,0:T(8,128)(2,1)} %dynamic-slice_convert_fusion.2), channel_id=1, source_target_pairs={{0,2},{2,0},{1,3},{3,1},{4,6},{6,4},{5,7},{7,5},{8,10},{10,8},{9,1... | collective-permute-start | bytes 2359304 | tf_op jit(solution)/shard_map/ppermute | solution.py:26
  143.0 7.7 %collective-permute-start.7 = (bf16[256,1536]{1,0:T(8,128)(2,1)}, bf16[256,1536]{1,0:T(8,128)(2,1)S(1)}, u32[]{:S(2)}, u32[]{:S(2)}) collective-permute-start(bf16[256,1536]{1,0:T(8,128)(2,1)} %dynamic-slice_convert_fusion.3), channel_id=1, source_target_pairs={{0,2},{2,0},{1,3},{3,1},{4,6},{6,4},{5,7},{7,5},{8,10},{10,8},{9,1... | collective-permute-start | bytes 2359304 | tf_op jit(solution)/shard_map/ppermute | solution.py:26
  143.3 10.6 %collective-permute-start.25 = (bf16[256,1536]{1,0:T(8,128)(2,1)S(1)}, bf16[256,1536]{1,0:T(8,128)(2,1)}, u32[]{:S(2)}, u32[]{:S(2)}) collective-permute-start(bf16[256,1536]{1,0:T(8,128)(2,1)S(1)} %fusion.65), channel_id=1, source_target_pairs={{0,2},{2,0},{1,3},{3,1},{4,6},{6,4},{5,7},{7,5},{8,10},{10,8},{9,1... | collective-permute-start | bytes 2359304 | tf_op jit(solution)/shard_map/ppermute | solution.py:26
  149.4 10.5 %collective-permute-start.22 = (bf16[128,1536]{1,0:T(8,128)(2,1)S(1)}, bf16[128,1536]{1,0:T(8,128)(2,1)S(1)}, u32[]{:S(2)}, u32[]{:S(2)}) collective-permute-start(bf16[128,1536]{1,0:T(8,128)(2,1)S(1)} %dynamic-slice_convert_fusion.5), channel_id=1, source_target_pairs={{0,4},{4,0},{8,12},{12,8},{1,5},{5,1},{9,13},{13,9},{2,6},{6,2},{1... | collective-permute-start | bytes 1179656 | tf_op jit(solution)/shard_map/ppermute | solution.py:26
  150.6 3.2 %copy-start.9 = (f32[1536,512]{0,1:T(8,128)S(1)}, f32[1536,512]{0,1:T(8,128)}, u32[]{:S(2)}) copy-start(f32[1536,512]{0,1:T(8,128)} %fusion.138) | copy-start | bytes 9437188
  150.6 11.6 %collective-permute-start.12 = (bf16[256,768]{1,0:T(8,128)(2,1)S(1)}, bf16[256,768]{1,0:T(8,128)(2,1)S(1)}, u32[]{:S(2)}, u32[]{:S(2)}) collective-permute-start(bf16[256,768]{1,0:T(8,128)(2,1)S(1)} %pad_maximum_fusion.20), channel_id=1, source_target_pairs={{1,64},{64,1},{65,0},{0,65},{3,66},{66,3},{67,2},{2,67},{5,68},{68... | collective-permute-start | bytes 1179656 | tf_op jit(solution)/shard_map/ppermute | solution.py:26
  151.8 18.9 %collective-permute-start.8 = (bf16[256,768]{1,0:T(8,128)(2,1)S(1)}, bf16[256,768]{1,0:T(8,128)(2,1)S(1)}, u32[]{:S(2)}, u32[]{:S(2)}) collective-permute-start(bf16[256,768]{1,0:T(8,128)(2,1)S(1)} %pad_maximum_fusion.19), channel_id=1, source_target_pairs={{1,64},{64,1},{65,0},{0,65},{3,66},{66,3},{67,2},{2,67},{5,68},{68... | collective-permute-start | bytes 1179656 | tf_op jit(solution)/shard_map/ppermute | solution.py:26
  155.3 16.5 %collective-permute-start.26 = (bf16[128,1536]{1,0:T(8,128)(2,1)S(1)}, bf16[128,1536]{1,0:T(8,128)(2,1)S(1)}, u32[]{:S(2)}, u32[]{:S(2)}) collective-permute-start(bf16[128,1536]{1,0:T(8,128)(2,1)S(1)} %dynamic-slice_convert_fusion.4), channel_id=1, source_target_pairs={{0,4},{4,0},{8,12},{12,8},{1,5},{5,1},{9,13},{13,9},{2,6},{6,2},{1... | collective-permute-start | bytes 1179656 | tf_op jit(solution)/shard_map/ppermute | solution.py:26
  160.0 12.0 %collective-permute-start.23 = (bf16[64,1536]{1,0:T(8,128)(2,1)S(1)}, bf16[64,1536]{1,0:T(8,128)(2,1)S(1)}, u32[]{:S(2)}, u32[]{:S(2)}) collective-permute-start(bf16[64,1536]{1,0:T(8,128)(2,1)S(1)} %dynamic-slice_convert_fusion.7), channel_id=1, source_target_pairs={{0,1},{1,0},{64,65},{65,64},{2,3},{3,2},{66,67},{67,66},{4,5},{5,4... | collective-permute-start | bytes 589832 | tf_op jit(solution)/shard_map/ppermute | solution.py:26
  162.3 10.4 %collective-permute-start.13 = (bf16[128,768]{1,0:T(8,128)(2,1)S(1)}, bf16[128,768]{1,0:T(8,128)(2,1)S(1)}, u32[]{:S(2)}, u32[]{:S(2)}) collective-permute-start(bf16[128,768]{1,0:T(8,128)(2,1)S(1)} %dynamic-slice_convert_fusion.8), channel_id=1, source_target_pairs={{4,8},{8,4},{12,0},{0,12},{5,9},{9,5},{13,1},{1,13},{6,10},{10,6},... | collective-permute-start | bytes 589832 | tf_op jit(solution)/shard_map/ppermute | solution.py:26
  170.8 6.5 %collective-permute-start.9 = (bf16[128,768]{1,0:T(8,128)(2,1)S(1)}, bf16[128,768]{1,0:T(8,128)(2,1)S(1)}, u32[]{:S(2)}, u32[]{:S(2)}) collective-permute-start(bf16[128,768]{1,0:T(8,128)(2,1)S(1)} %dynamic-slice_convert_fusion.9), channel_id=1, source_target_pairs={{4,8},{8,4},{12,0},{0,12},{5,9},{9,5},{13,1},{1,13},{6,10},{10,6},... | collective-permute-start | bytes 589832 | tf_op jit(solution)/shard_map/ppermute | solution.py:26
  171.9 7.0 %collective-permute-start.27 = (bf16[64,1536]{1,0:T(8,128)(2,1)S(1)}, bf16[64,1536]{1,0:T(8,128)(2,1)S(1)}, u32[]{:S(2)}, u32[]{:S(2)}) collective-permute-start(bf16[64,1536]{1,0:T(8,128)(2,1)S(1)} %dynamic-slice_convert_fusion.6), channel_id=1, source_target_pairs={{0,1},{1,0},{64,65},{65,64},{2,3},{3,2},{66,67},{67,66},{4,5},{5,4... | collective-permute-start | bytes 589832 | tf_op jit(solution)/shard_map/ppermute | solution.py:26
  172.1 7.5 %collective-permute-start.24 = (bf16[32,1536]{1,0:T(8,128)(2,1)S(1)}, bf16[32,1536]{1,0:T(8,128)(2,1)S(1)}, u32[]{:S(2)}, u32[]{:S(2)}) collective-permute-start(bf16[32,1536]{1,0:T(8,128)(2,1)S(1)} %dynamic-slice_convert_fusion.11), channel_id=1, source_target_pairs={{0,16},{16,0},{32,48},{48,32},{1,17},{17,1},{33,49},{49,33},{2,18}... | collective-permute-start | bytes 294920 | tf_op jit(solution)/shard_map/ppermute | solution.py:26
  172.8 10.1 %collective-permute-start.14 = (bf16[64,768]{1,0:T(8,128)(2,1)S(1)}, bf16[64,768]{1,0:T(8,128)(2,1)S(1)}, u32[]{:S(2)}, u32[]{:S(2)}) collective-permute-start(bf16[64,768]{1,0:T(8,128)(2,1)S(1)} %dynamic-slice_convert_fusion.12), channel_id=1, source_target_pairs={{16,32},{32,16},{48,0},{0,48},{17,33},{33,17},{49,1},{1,49},{18,34... | collective-permute-start | bytes 294920 | tf_op jit(solution)/shard_map/ppermute | solution.py:26
  177.4 5.6 %collective-permute-start.10 = (bf16[64,768]{1,0:T(8,128)(2,1)S(1)}, bf16[64,768]{1,0:T(8,128)(2,1)S(1)}, u32[]{:S(2)}, u32[]{:S(2)}) collective-permute-start(bf16[64,768]{1,0:T(8,128)(2,1)S(1)} %dynamic-slice_convert_fusion.13), channel_id=1, source_target_pairs={{16,32},{32,16},{48,0},{0,48},{17,33},{33,17},{49,1},{1,49},{18,34... | collective-permute-start | bytes 294920 | tf_op jit(solution)/shard_map/ppermute | solution.py:26
  179.0 3.5 %collective-permute-start.28 = (bf16[32,1536]{1,0:T(8,128)(2,1)S(1)}, bf16[32,1536]{1,0:T(8,128)(2,1)S(1)}, u32[]{:S(2)}, u32[]{:S(2)}) collective-permute-start(bf16[32,1536]{1,0:T(8,128)(2,1)S(1)} %dynamic-slice_convert_fusion.10), channel_id=1, source_target_pairs={{0,16},{16,0},{32,48},{48,32},{1,17},{17,1},{33,49},{49,33},{2,18}... | collective-permute-start | bytes 294920 | tf_op jit(solution)/shard_map/ppermute | solution.py:26
  182.7 4.8 %collective-permute-start.29 = (bf16[64,768]{1,0:T(8,128)(2,1)S(1)}, bf16[64,768]{1,0:T(8,128)(2,1)S(1)}, u32[]{:S(2)}, u32[]{:S(2)}) collective-permute-start(bf16[64,768]{1,0:T(8,128)(2,1)S(1)} %pad_maximum_fusion.26), channel_id=1, source_target_pairs={{1,64},{64,1},{65,0},{0,65},{3,66},{66,3},{67,2},{2,67},{5,68},{68... | collective-permute-start | bytes 294920 | tf_op jit(solution)/shard_map/ppermute | solution.py:26
  187.5 4.8 %collective-permute-start.30 = (bf16[64,768]{1,0:T(8,128)(2,1)S(1)}, bf16[64,768]{1,0:T(8,128)(2,1)S(1)}, u32[]{:S(2)}, u32[]{:S(2)}) collective-permute-start(bf16[64,768]{1,0:T(8,128)(2,1)S(1)} %fusion.117), channel_id=1, source_target_pairs={{4,8},{8,4},{12,0},{0,12},{5,9},{9,5},{13,1},{1,13},{6,10},{10,6},... | collective-permute-start | bytes 294920 | tf_op jit(solution)/shard_map/ppermute | solution.py:26
  187.8 5.7 %collective-permute-start.15 = (bf16[128,768]{1,0:T(8,128)(2,1)S(1)}, bf16[128,768]{1,0:T(8,128)(2,1)S(1)}, u32[]{:S(2)}, u32[]{:S(2)}) collective-permute-start(bf16[128,768]{1,0:T(8,128)(2,1)S(1)} %pad_maximum_fusion.23), channel_id=1, source_target_pairs={{0,4},{4,0},{8,12},{12,8},{1,5},{5,1},{9,13},{13,9},{2,6},{6,2},{1... | collective-permute-start | bytes 589832 | tf_op jit(solution)/shard_map/ppermute | solution.py:26
  192.2 5.1 %collective-permute-start.31 = (bf16[64,768]{1,0:T(8,128)(2,1)S(1)}, bf16[64,768]{1,0:T(8,128)(2,1)S(1)}, u32[]{:S(2)}, u32[]{:S(2)}) collective-permute-start(bf16[64,768]{1,0:T(8,128)(2,1)S(1)} %add_convert_fusion.4), channel_id=1, source_target_pairs={{16,32},{32,16},{48,0},{0,48},{17,33},{33,17},{49,1},{1,49},{18,34... | collective-permute-start | bytes 294920 | tf_op jit(solution)/shard_map/ppermute | solution.py:26
  193.5 4.6 %collective-permute-start.16 = (bf16[128,768]{1,0:T(8,128)(2,1)S(1)}, bf16[128,768]{1,0:T(8,128)(2,1)S(1)}, u32[]{:S(2)}, u32[]{:S(2)}) collective-permute-start(bf16[128,768]{1,0:T(8,128)(2,1)S(1)} %add_convert_fusion.2), channel_id=1, source_target_pairs={{0,1},{1,0},{64,65},{65,64},{2,3},{3,2},{66,67},{67,66},{4,5},{5,4... | collective-permute-start | bytes 589832 | tf_op jit(solution)/shard_map/ppermute | solution.py:26
  197.3 3.5 %collective-permute-start.32 = (bf16[2,32,768]{2,1,0:T(8,128)(2,1)S(1)}, bf16[2,32,768]{2,1,0:T(8,128)(2,1)S(1)}, u32[]{:S(2)}, u32[]{:S(2)}) collective-permute-start(bf16[2,32,768]{2,1,0:T(8,128)(2,1)S(1)} %bitcast.231), channel_id=1, source_target_pairs={{0,16},{16,0},{32,48},{48,32},{1,17},{17,1},{33,49},{49,33},{2,18}... | collective-permute-start | bytes 294920 | tf_op jit(solution)/shard_map/ppermute | solution.py:26
  198.2 5.1 %collective-permute-start.17 = (bf16[128,768]{1,0:T(8,128)(2,1)S(1)}, bf16[128,768]{1,0:T(8,128)(2,1)S(1)}, u32[]{:S(2)}, u32[]{:S(2)}) collective-permute-start(bf16[128,768]{1,0:T(8,128)(2,1)S(1)} %add_convert_fusion.1), channel_id=1, source_target_pairs={{0,16},{16,0},{32,48},{48,32},{1,17},{17,1},{33,49},{49,33},{2,18}... | collective-permute-start | bytes 589832 | tf_op jit(solution)/shard_map/ppermute | solution.py:26
  200.9 6.2 %collective-permute-start.33 = (bf16[2,64,768]{2,1,0:T(8,128)(2,1)S(1)}, bf16[2,64,768]{2,1,0:T(8,128)(2,1)S(1)}, u32[]{:S(2)}, u32[]{:S(2)}) collective-permute-start(bf16[2,64,768]{2,1,0:T(8,128)(2,1)S(1)} %pad_maximum_fusion.24), channel_id=1, source_target_pairs={{0,1},{1,0},{64,65},{65,64},{2,3},{3,2},{66,67},{67,66},{4,5},{5,4... | collective-permute-start | bytes 589832 | tf_op jit(solution)/shard_map/ppermute | solution.py:26
  203.3 5.8 %collective-permute-start.18 = (bf16[2,64,768]{2,1,0:T(8,128)(2,1)S(1)}, bf16[2,64,768]{2,1,0:T(8,128)(2,1)S(1)}, u32[]{:S(2)}, u32[]{:S(2)}) collective-permute-start(bf16[2,64,768]{2,1,0:T(8,128)(2,1)S(1)} %bitcast.228), channel_id=1, source_target_pairs={{16,32},{32,16},{48,0},{0,48},{17,33},{33,17},{49,1},{1,49},{18,34... | collective-permute-start | bytes 589832 | tf_op jit(solution)/shard_map/ppermute | solution.py:26
  207.2 6.7 %collective-permute-start.34 = (bf16[2,128,768]{2,1,0:T(8,128)(2,1)S(1)}, bf16[2,128,768]{2,1,0:T(8,128)(2,1)S(1)}, u32[]{:S(2)}, u32[]{:S(2)}) collective-permute-start(bf16[2,128,768]{2,1,0:T(8,128)(2,1)S(1)} %pad_maximum_fusion.22), channel_id=1, source_target_pairs={{0,4},{4,0},{8,12},{12,8},{1,5},{5,1},{9,13},{13,9},{2,6},{6,2},{1... | collective-permute-start | bytes 1179656 | tf_op jit(solution)/shard_map/ppermute | solution.py:26
  207.3 15.1 %collective-permute-start.36 = (bf16[128,640]{1,0:T(8,128)(2,1)S(1)}, bf16[128,640]{1,0:T(8,128)(2,1)S(1)}, u32[]{:S(2)}, u32[]{:S(2)}) collective-permute-start(bf16[128,640]{1,0:T(8,128)(2,1)S(1)} %pad_maximum_fusion.25), channel_id=1, source_target_pairs={{0,64},{64,0},{1,65},{65,1},{2,66},{66,2},{3,67},{67,3},{4,68},{68... | collective-permute-start | bytes 491528 | tf_op jit(solution)/shard_map/ppermute | solution.py:284
  209.2 14.6 %collective-permute-start.19 = (bf16[2,128,768]{2,1,0:T(8,128)(2,1)S(1)}, bf16[2,128,768]{2,1,0:T(8,128)(2,1)S(1)}, u32[]{:S(2)}, u32[]{:S(2)}) collective-permute-start(bf16[2,128,768]{2,1,0:T(8,128)(2,1)S(1)} %pad_maximum_fusion.21), channel_id=1, source_target_pairs={{4,8},{8,4},{12,0},{0,12},{5,9},{9,5},{13,1},{1,13},{6,10},{10,6},... | collective-permute-start | bytes 1179656 | tf_op jit(solution)/shard_map/ppermute | solution.py:26
  214.1 14.8 %collective-permute-start.35 = (bf16[2,256,768]{2,1,0:T(8,128)(2,1)S(1)}, bf16[2,256,768]{2,1,0:T(8,128)(2,1)S(1)}, u32[]{:S(2)}, u32[]{:S(2)}) collective-permute-start(bf16[2,256,768]{2,1,0:T(8,128)(2,1)S(1)} %pad_maximum_fusion.16), channel_id=1, source_target_pairs={{0,2},{2,0},{1,3},{3,1},{4,6},{6,4},{5,7},{7,5},{8,10},{10,8},{9,1... | collective-permute-start | bytes 2359304 | tf_op jit(solution)/shard_map/ppermute | solution.py:26
  224.0 6.8 %collective-permute-start.20 = (bf16[2,256,768]{2,1,0:T(8,128)(2,1)S(1)}, bf16[2,256,768]{2,1,0:T(8,128)(2,1)S(1)}, u32[]{:S(2)}, u32[]{:S(2)}) collective-permute-start(bf16[2,256,768]{2,1,0:T(8,128)(2,1)S(1)} %pad_maximum_fusion.15), channel_id=1, source_target_pairs={{0,2},{2,0},{1,3},{3,1},{4,6},{6,4},{5,7},{7,5},{8,10},{10,8},{9,1... | collective-permute-start | bytes 2359304 | tf_op jit(solution)/shard_map/ppermute | solution.py:26
  (17 other events, 37.7 us)
where the time goes:
time: 239 us; the launch traced here: 234 us
  starting transfers between devices  63.7 us (27%)
  waiting for transfers between devices  56.8 us (24%)
  matrix products  49.7 us (21%)
  local copies, waits for them, and re-layouts  34 us (14%)
  other arithmetic  28 us (12%)
    ppermute x34, waiting for transfers between devices, swap(): return lax.ppermute(value, name, perm)  53.6 us
    ppermute x34, starting transfers between devices, swap(): return lax.ppermute(value, name, perm)  40 us
    dot_general x6, matrix products, contract_rows(): lax.dot_general(left, right, (((0,), (0,)), ((), ())), preferred_element_...  26.8 us
    dot_general x2, matrix products, convolve(): sums = jnp.dot(taller, weights, preferred_element_type=F32)  11.2 us
    all_to_all x1, starting transfers between devices, compute(): lax.all_to_all(packed.reshape(tile_count, capacity, PACK), TILE, split_ax...  9.42 us
    convert_element_type x14, local copies, waits for them, and re-layouts, halve(): return kept.astype(F32) + swap(sent.astype(BF), axis, kind).astype(F32)  8.93 us
    all_to_all x1, starting transfers between devices, compute(): lax.all_to_all(back.reshape(tile_count, capacity, PACK), TILE, split_axis...  8.48 us
    unnamed x63, local copies, waits for them, and re-layouts  5.55 us
  transfers between devices with their start and end apart: 39, of which 18 were waited for; matrix products, arithmetic and copies ran while one was open for 18% of the time, Pallas kernels for 0%

commit v1 on v0

--- a/solution.py
+++ b/solution.py
@@ -1,3 +1,5 @@
+import math
+
 import jax
 import jax.numpy as jnp
 from jax import lax
@@ -7,6 +9,7 @@
 BF = jnp.bfloat16
 F32 = jnp.float32
 TILE = ("z", "x", "core")
+ALL = ("fsdp", "z", "x", "core", "scan")
 PACK = 640
 
 
@@ -36,34 +39,94 @@
     return place >> 1 if kind else (place ^ (place >> 1)) & 1
 
 
-def halve(value, axis, kind, flip=0):
-    size = value.shape[0] // 2
-    mine = bit(axis, kind) ^ flip
-    sent = lax.dynamic_slice_in_dim(value, (1 - mine) * size, size, 0)
-    kept = lax.dynamic_slice_in_dim(value, mine * size, size, 0)
-    return kept.astype(F32) + swap(sent.astype(BF), axis, kind).astype(F32)
+def partner(dim, place):
+    _, kind = dim
+    if kind == 0:
+        return place ^ 1
+    return (place + (1 if place & 1 else -1)) % 4
+
+
+def swap_by_core(value, dims):
+    sizes = [lax.axis_size(name) for name in ALL]
+    perm = []
+    for index in range(math.prod(sizes)):
+        rest, spot = index, {}
+        for name, size in zip(reversed(ALL), reversed(sizes)):
+            spot[name] = rest % size
+            rest //= size
+        spot["y"] = spot["fsdp"] * 2 + spot["scan"]
+        dim = dims[spot["core"]]
+        spot[dim[0]] = partner(dim, spot[dim[0]])
+        spot["fsdp"], spot["scan"] = spot["y"] // 2, spot["y"] % 2
+        target = 0
+        for name, size in zip(ALL, sizes):
+            target = target * size + spot[name]
+        perm.append((index, target))
+    return lax.ppermute(value, ALL, perm)
+
+
+def bit_by_core(dims):
+    return jnp.where(lax.axis_index("core") == 0, bit(*dims[0]), bit(*dims[1]))
+
+
+def halve(value, dims):
+    size = value.shape[1] // 2
+    mine = bit_by_core(dims)
+    sent = lax.dynamic_slice_in_dim(value, (1 - mine) * size, size, 1)
+    kept = lax.dynamic_slice_in_dim(value, mine * size, size, 1)
+    return kept + swap_by_core(sent.astype(BF), dims).astype(F32)
 
 
 def own_columns(value):
-    cols = value.shape[1] // 6
+    cols = value.shape[2] // 6
     own, far = (
-        jnp.concatenate([value[:, (2 * g + h) * cols :][:, :cols] for g in range(3)], axis=1)
+        jnp.concatenate([value[:, :, (2 * g + h) * cols :][:, :, :cols] for g in range(3)], axis=2)
         for h in range(2)
     )
-    return own.astype(F32) + swap(far.astype(BF), "y", 1).astype(F32)
-
-
-def share(value, axis, kind):
+    return own + swap(far.astype(BF), "y", 1).astype(F32)
+
+
+def joined(value, other, mine):
+    first = mine == 0
+    return jnp.concatenate(
+        [jnp.where(first, value, other), jnp.where(first, other, value)], axis=1
+    )
+
+
+XA, XB, YA, ZA, ZB = ("x", 0), ("x", 1), ("y", 0), ("z", 0), ("z", 1)
+STEPS = {
+    "s1": ((XA, XB), (XB, XA), (YA, YA), (ZA, ZB), (ZB, ZA)),
+    "s2": ((ZA, ZB), (ZB, ZA), (YA, YA), (XA, XB), (XB, XA)),
+}
+
+
+def reduce_first(grads, flips):
+    core = lax.axis_index("core")
+    size = grads[0].shape[0] // 2
+    kept, sent = (
+        jnp.stack(
+            [
+                lax.dynamic_slice_in_dim(grad, (core ^ flip ^ far) * size, size, 0)
+                for grad, flip in zip(grads, flips)
+            ]
+        )
+        for far in range(2)
+    )
+    return kept + swap(sent.astype(BF), "core", 0).astype(F32)
+
+
+def reduce_rest(name, value):
+    steps = STEPS[name]
+    for index in range(3):
+        value = halve(value, steps[index])
+    value = own_columns(value)
+    for index in range(3, 5):
+        value = value + swap_by_core(value, steps[index])
     value = value.astype(BF)
-    return value.astype(F32) + swap(value, axis, kind).astype(F32)
-
-
-def double(value, axis, kind, dim):
-    other = swap(value, axis, kind)
-    first = bit(axis, kind) == 0
-    return jnp.concatenate(
-        [jnp.where(first, value, other), jnp.where(first, other, value)], axis=dim
-    )
+    for index in (2, 1, 0):
+        other = swap_by_core(value, steps[index])
+        value = joined(value, other, bit_by_core(steps[index]))
+    return joined(value, swap(value, "core", 0), lax.axis_index("core"))
 
 
 def blocks_of(spatial, temporal):
@@ -229,8 +292,18 @@
     ).reshape(frames, cells, slot_count)
     logits = jnp.sum(jnp.where(here[None], scores, 0.0), axis=1) + slot_bias[None, :]
     delta = (jnp.exp(logits) - slot_spikes) * scale_factor
-    spread = jnp.where(here[None], delta[:, None, :], 0.0).astype(BF).reshape(-1, slot_count)
-    feature_grad = jnp.dot(spread, slot_weight, preferred_element_type=F32)
+    coarse = lax.reduce_precision(delta, 8, 7)
+    pieces = jnp.concatenate([coarse, delta - coarse], axis=1).astype(BF)
+    here_twice = jnp.concatenate([here, here], axis=1)
+    spread_twice = jnp.where(here_twice[None], pieces[:, None, :], jnp.zeros((), BF)).reshape(
+        -1, 2 * slot_count
+    )
+    spread = spread_twice[:, :slot_count]
+    feature_grad = jnp.dot(
+        spread_twice,
+        jnp.concatenate([slot_weight, slot_weight]),
+        preferred_element_type=F32,
+    )
     slope = jnp.where(mixed > 0, 1.0, jnp.exp(jnp.minimum(mixed, 0.0)))
     mixed_grad = (feature_grad * slope).astype(BF)
     back_pad = jnp.pad(mixed_grad.reshape(frames, cells, channels), ((0, 2), (0, 0), (0, 0)))
@@ -238,14 +311,13 @@
         [back_pad[lag : lag + frames].reshape(-1, channels) for lag in range(3)], axis=1
     )
     grad_t = contract_rows(spatial_out.reshape(-1, channels), later)
-    part_t = halve(grad_t, "core", 0, fsdp)
-
     slot_grad = contract_rows(spread, features)
     slot_bias_grad = jnp.sum(delta, axis=0)
     back = jnp.concatenate(
         [slot_grad, slot_bias_grad[:, None], jnp.zeros((slot_count, PACK - channels - 1), F32)],
         axis=1,
     ).astype(BF)
+    back = lax.optimization_barrier(back)
 
     spatial_back = lax.dot_general(
         later,
@@ -257,24 +329,14 @@
     wider = jnp.concatenate(
         [shift(spatial_back, 1 - b).astype(BF).reshape(-1, channels) for b in range(3)], axis=1
     )
-    part_t = halve(part_t, "x", 0)
     grad_0 = contract_rows(shifted_rows[0], wider)
-    part_0 = halve(grad_0, "core", 0)
+    first_part = reduce_first((grad_t, grad_0), (fsdp, 0))
     grad_1 = contract_rows(shifted_rows[1], wider)
-    part_1 = halve(grad_1, "core", 0)
-    part_0 = own_columns(part_0)
+    first_part, wider = lax.optimization_barrier((first_part, wider))
     grad_2 = contract_rows(shifted_rows[2], wider)
-    part_2 = halve(grad_2, "core", 0)
-    part_t = halve(part_t, "y", 0)
-    part_1 = halve(part_1, "x", 0)
-    part_2 = own_columns(part_2)
-    part_t = halve(part_t, "z", 0)
-    part_0 = halve(part_0, "x", 1)
-    part_1 = halve(part_1, "y", 0)
-    part_0 = halve(part_0, "z", 1)
-    part_2 = halve(part_2, "x", 1)
-    part_1 = halve(part_1, "z", 0)
-    part_2 = halve(part_2, "z", 1)
+    second_part = reduce_first((grad_1, grad_2), (0, 0))
+    total_1 = reduce_rest("s1", first_part)
+    total_2 = reduce_rest("s2", second_part)
 
     returned = lax.all_to_all(
         back.reshape(tile_count, capacity, PACK), TILE, split_axis=0, concat_axis=0, tiled=True
@@ -286,29 +348,11 @@
     weight_grad = summed[:, :channels]
     bias_grad = summed[:, channels]
 
-    odd = jnp.concatenate([part_t, part_1])
-    even = jnp.concatenate([part_0, part_2])
-    odd = own_columns(odd)
-    even = share(even, "x", 0)
-    odd = share(odd, "x", 1)
-    even = share(even, "y", 0)
-    odd = share(odd, "z", 1)
-    even = share(even, "z", 0)
-    odd = odd.astype(BF).reshape(2, -1, odd.shape[1])
-    even = even.astype(BF).reshape(2, -1, even.shape[1])
-    odd = double(odd, "z", 0, 1)
-    even = double(even, "z", 1, 1)
-    odd = double(odd, "y", 0, 1)
-    even = double(even, "x", 1, 1)
-    odd = double(odd, "x", 0, 1)
-    even = double(even, "core", 0, 1)
-    odd = double(odd, "core", 0, 1)
-
     def taps(value):
         return [value[:, b * half : (b + 1) * half].astype(F32) for b in range(3)]
 
-    total_temporal = jnp.stack(taps(odd[0]))
-    total_spatial = jnp.stack(taps(even[0]) + taps(odd[1]) + taps(even[1]))
+    total_temporal = jnp.stack(taps(total_1[0]))
+    total_spatial = jnp.stack(taps(total_1[1]) + taps(total_2[0]) + taps(total_2[1]))
     return (total_spatial, total_temporal, weight_grad[None], bias_grad[None])
 
 

time: 239 us -> 254 us (1.063)
  waiting for transfers between devices: 56.8 us -> 85.4 us
  matrix products: 49.7 us -> 44.3 us
  other arithmetic: 28 us -> 25 us
  local copies, waits for them, and re-layouts: 34 us -> 31 us
  starting transfers between devices: 63.7 us -> 60.9 us
    ppermute x0 -> x16, waiting for transfers between devices: none -> 60.3 us  [swap_by_core(): return lax.ppermute(value, ALL, perm)]
    ppermute x34 -> x11, waiting for transfers between devices: 53.6 us -> 13 us  [swap(): return lax.ppermute(value, name, perm)]
    convert_element_type x14 -> x6, local copies, waits for them, and re-layouts: 8.93 us -> 0.35 us  [halve(): return kept + swap_by_core(sent.astype(BF), dims).astype(F32)]
    ppermute x0 -> x16, starting transfers between devices: none -> 8.42 us  [swap_by_core(): return lax.ppermute(value, ALL, perm)]
    ppermute x34 -> x11, starting transfers between devices: 40 us -> 32 us  [swap(): return lax.ppermute(value, name, perm)]
    dot_general x6, matrix products: 26.8 us -> 19.1 us  [contract_rows(): lax.dot_general(left, right, (((0,), (0,)), ((), ())), preferred_element_...]
    all_to_all x1, waiting for transfers between devices: 0.01 us -> 5.84 us  [compute(): lax.all_to_all(packed.reshape(tile_count, capacity, PACK), TILE, split_ax...]
    another operation x2 -> x10, local copies, waits for them, and re-layouts: 0.07 us -> 5.87 us  [the longest x8 5.8 us: reduce_first(): jnp.stack([lax.dynamic_slice_in_dim(grad, (core ^ flip ^ far) * size, siz...]
  transfers between devices with their start and end apart: 39 -> 32, of which waited for: 18 -> 20; matrix products, arithmetic and copies ran while one was open for 18% -> 17% of each run, Pallas kernels for 0% -> 0%
where the time goes in v1:
time: 254 us; the launch traced here: 249 us
  waiting for transfers between devices  85.4 us (34%)
  starting transfers between devices  60.9 us (24%)
  matrix products  44.3 us (17%)
  local copies, waits for them, and re-layouts  31 us (12%)
  other arithmetic  25 us (10%)
    ppermute x16, waiting for transfers between devices, swap_by_core(): return lax.ppermute(value, ALL, perm)  60.3 us
    ppermute x11, starting transfers between devices, swap(): return lax.ppermute(value, name, perm)  32 us
    dot_general x6, matrix products, contract_rows(): lax.dot_general(left, right, (((0,), (0,)), ((), ())), preferred_element_...  19.1 us
    ppermute x11, waiting for transfers between devices, swap(): return lax.ppermute(value, name, perm)  13 us
    dot_general x2, matrix products, convolve(): sums = jnp.dot(taller, weights, preferred_element_type=F32)  11.2 us
    all_to_all x1, starting transfers between devices, compute(): lax.all_to_all(packed.reshape(tile_count, capacity, PACK), TILE, split_ax...  9.41 us
    ppermute x16, starting transfers between devices, swap_by_core(): return lax.ppermute(value, ALL, perm)  8.42 us
    unnamed x133, local copies, waits for them, and re-layouts  7.57 us
  transfers between devices with their start and end apart: 32, of which 20 were waited for; matrix products, arithmetic and copies ran while one was open for 17% of the time, Pallas kernels for 0%

profile of v1, /device:TPU:1, one launch (start us, length us, event | category | flops | bytes accessed | tf_op | source)
XLA Modules:
  0.0 249.1 jit_solution(668513671387412491)
XLA Ops:
  2.9 3.6 %collective-permute-start.2 = (bf16[256,768]{1,0:T(8,128)(2,1)}, bf16[256,768]{1,0:T(8,128)(2,1)}, u32[]{:S(2)}, u32[]{:S(2)}) collective-permute-start(bf16[256,768]{1,0:T(8,128)(2,1)} %pad_maximum_fusion.19), channel_id=1, source_target_pairs={{1,64},{64,1},{65,0},{0,65},{3,66},{66,3},{67,2},{2,67},{5,68},{68... | collective-permute-start | bytes 1179656 | tf_op jit(solution)/shard_map/ppermute | solution.py:29
  6.7 2.9 %collective-permute-start.1 = (bf16[16,1,64,512]{3,2,1,0:T(8,128)(2,1)S(1)}, bf16[16,1,64,512]{3,2,1,0:T(8,128)(2,1)}, u32[]{:S(2)}, u32[]{:S(2)}) collective-permute-start(bf16[16,1,64,512]{3,2,1,0:T(8,128)(2,1)S(1)} %get-tuple-element.36), channel_id=1, source_target_pairs={{2,0},{4,2},{6,4},{8,6},{10,8},{12,10},{14,12},{16,14},{18,16},{20... | collective-permute-start | bytes 3145736 | tf_op jit(solution)/shard_map/ppermute | solution.py:161
  9.6 3.0 %collective-permute-start = (bf16[16,1,64,512]{3,2,1,0:T(8,128)(2,1)S(1)}, bf16[16,1,64,512]{3,2,1,0:T(8,128)(2,1)}, u32[]{:S(2)}, u32[]{:S(2)}) collective-permute-start(bf16[16,1,64,512]{3,2,1,0:T(8,128)(2,1)S(1)} %get-tuple-element.35), channel_id=1, source_target_pairs={{0,2},{2,4},{4,6},{6,8},{8,10},{10,12},{12,14},{14,16},{16,18},{18... | collective-permute-start | bytes 3145736 | tf_op jit(solution)/shard_map/ppermute | solution.py:160
  14.7 9.4 %all-to-all-start = ((bf16[32,10,640]{2,1,0:T(8,128)(2,1)}), bf16[32,10,640]{2,1,0:T(8,128)(2,1)S(1)}, u32[]{:S(2)}, u32[]{:S(2)}) async-start(bf16[32,10,640]{2,1,0:T(8,128)(2,1)} %reshape.184), calls=%async_computation | async-start | bytes 1310720 | tf_op jit(solution)/shard_map/all_to_all | solution.py:223
  24.2 3.1 %slice_bitcast_fusion.21 = (bf16[512,256]{1,0:T(8,128)(2,1)}, bf16[512,256]{1,0:T(8,128)(2,1)}, bf16[512,256]{1,0:T(8,128)(2,1)}, bf16[512,256]{1,0:T(8,128)(2,1...) fusion(bf16[9,512,256]{2,1,0:T(8,128)(2,1)} %param.10), kind=kLoop, calls=%fused_computation.226 | loop fusion | bytes 4718592 | tf_op jit(solution)/shard_map/squeeze | solution.py:255
  30.9 1.8 collective-permute-start.4
  33.9 5.8 %all-to-all-done = bf16[32,10,640]{2,1,0:T(8,128)(2,1)S(1)} async-done(((bf16[32,10,640]{2,1,0:T(8,128)(2,1)}), bf16[32,10,640]{2,1,0:T(8,128)(2,1)S(1)}, u32[]{:S(2)}, u32[]{:S(2)}) %all-to-all-start) | async-done | bytes 409632 | tf_op jit(solution)/shard_map/all_to_all | solution.py:223
  41.8 2.8 %collective-permute-done.4 = bf16[256,768]{1,0:T(8,128)(2,1)} collective-permute-done((bf16[256,768]{1,0:T(8,128)(2,1)}, bf16[256,768]{1,0:T(8,128)(2,1)}, u32[]{:S(2)}, u32[]{:S(2)}) %collective-permute-start.4) | collective-permute-done | bytes 393248 | tf_op jit(solution)/shard_map/ppermute | solution.py:29
  44.7 2.6 %fusion.134 = (bf16[1,4,256,768]{3,2,1,0:T(8,128)(2,1)S(1)}, bf16[4,256,768]{2,1,0:T(8,128)(2,1)}) fusion(bf16[1,256,768]{2,1,0:T(8,128)(2,1)} %bitcast.21, bf16[1,256,768]{2,1,0:T(8,128)(2,1)} %bitcast.20, bf16[1,256,768]{2,1,0:T(8,128)(2,1)S(1)} %bitcast.229, bf16[1,256,768]{2,1,0:T(8,128)(2,1)} %bitcast.18), kind=kLoop, calls=%fused_computation.287 | loop fusion | flops 2359296 | bytes 4718592 | tf_op jit(solution)/shard_map/stack | solution.py:145
  48.4 1.4 pad_maximum_fusion.8
  49.9 2.2 pad_maximum_fusion.7
  53.0 6.1 %fusion.7 = f32[2048,768]{1,0:T(8,128)S(1)} fusion(bf16[2048,512]{1,0:T(8,128)(2,1)S(1)} %bitcast.222, bf16[2048,512]{1,0:T(8,128)(2,1)S(1)} %bitcast.219, bf16[2048,512]{1,0:T(8,128)(2,1)S(1)} %bitcast.225, bf16[512,256]{1,0:T(8,128)(2,1)} %get-tuple-element.30, bf16[512,256]{1,0:T(8,128)(2,1)S(1)} %copy-done.33, bf16[512,256]{1,0:T(8,128)(2,1)S(1)} %copy-done.34, ...), kind=kOutput, calls=%fused_computation.36 | convolution fusion | flops 4871946240 | bytes 14942208 | tf_op jit(solution)/shard_map/dot_general | solution.py:244
  61.4 1.4 copy-done.8
  62.8 5.1 %fusion.6 = f32[2048,768]{1,0:T(8,128)S(1)} fusion(bf16[1536,768]{1,0:T(8,128)(2,1)S(1)} %bitcast_dynamic-update-slice_fusion, bf16[2048,512]{1,0:T(8,128)(2,1)S(1)} %bitcast.223, bf16[2048,512]{1,0:T(8,128)(2,1)S(1)} %bitcast.220, bf16[2048,512]{1,0:T(8,128)(2,1)S(1)} %bitcast.226), kind=kOutput, calls=%fused_computation.35 | convolution fusion | flops 4850712576 | bytes 14942208 | tf_op jit(solution)/shard_map/dot_general | solution.py:244
  74.0 1.4 add_add_fusion
  75.4 2.0 convolution_bitcast_fusion
  79.6 4.4 %fusion.5 = bf16[2048,512]{1,0:T(8,128)(2,1)S(1)} fusion(f32[2048,512]{1,0:T(8,128)} %copy-done, bf16[2048,640]{1,0:T(8,128)(2,1)S(1)} %bitcast.211, bf16[320,512]{1,0:T(8,128)(2,1)S(1)} %slice-done.2), kind=kOutput, calls=%fused_computation.28 | convolution fusion | flops 1348730880 | bytes 9240576 | tf_op jit(solution)/shard_map/dot_general | solution.py:302
  84.6 3.7 %fusion.8 = f32[512,1536]{1,0:T(8,128)S(1)} fusion(bf16[2048,512]{1,0:T(8,128)(2,1)S(1)} %bitcast.216, bf16[2048,512]{1,0:T(8,128)(2,1)S(1)} %bitcast.214, bf16[2048,512]{1,0:T(8,128)(2,1)S(1)} %fusion.5, bf16[2048,256]{1,0:T(8,128)(2,1)S(1)} %bitcast.210, bf16[2048,256]{1,0:T(8,128)(2,1)S(1)} %bitcast.207), kind=kOutput, calls=%fused_computation.37 | convolution fusion | flops 3244294144 | bytes 11534336 | tf_op jit(solution)/shard_map/dot_general | solution.py:17
  88.4 3.5 %convolution_convert_fusion = bf16[2048,512]{1,0:T(8,128)(2,1)S(1)} fusion(bf16[2048,512]{1,0:T(8,128)(2,1)S(1)} %bitcast.217, bf16[2048,512]{1,0:T(8,128)(2,1)S(1)} %bitcast.215, bf16[2048,512]{1,0:T(8,128)(2,1)S(1)} %fusion.5, bf16[256,256]{1,0:T(8,128)(2,1)S(1)} %get-tuple-element.100, bf16[256,256]{1,0:T(8,128)(2,1)S(1)} %copy-done.19, ...), kind=kOutput, calls=%fused_computation.32 | convolution fusion | flops 3260022784 | bytes 9961472 | tf_op jit(solution)/shard_map/dot_general | solution.py:322
  91.9 1.4 fusion.142
  96.3 3.5 %fusion.153 = f32[512,1536]{1,0:T(8,128)S(1)} fusion(bf16[2048,512]{1,0:T(8,128)(2,1)S(1)} %bitcast.227, bf16[2048,1536]{1,0:T(8,128)(2,1)S(1)} %pad_maximum_fusion.2), kind=kOutput, calls=%fused_computation.305 | convolution fusion | flops 3221225472 | bytes 11534336 | tf_op jit(solution)/shard_map/dot_general | solution.py:17
  99.8 5.1 %fusion.154 = f32[1536,512]{0,1:T(8,128)} fusion(bf16[2048,1536]{1,0:T(8,128)(2,1)S(1)} %pad_maximum_fusion.2, bf16[2048,512]{1,0:T(8,128)(2,1)S(1)} %bitcast.221), kind=kOutput, calls=%fused_computation.306 | convolution fusion | flops 3221225472 | bytes 11534336 | tf_op jit(solution)/shard_map/dot_general | solution.py:17
  107.8 2.0 fusion.57
  110.9 5.1 %all-to-all-start.1 = ((bf16[32,10,640]{2,1,0:T(8,128)(2,1)}), bf16[32,10,640]{2,1,0:T(8,128)(2,1)S(1)}, u32[]{:S(2)}, u32[]{:S(2)}) async-start(bf16[32,10,640]{2,1,0:T(8,128)(2,1)} %reshape.197), calls=%async_computation.1 | async-start | bytes 1310720 | tf_op jit(solution)/shard_map/all_to_all | solution.py:341
  116.1 2.8 %dynamic-slice_bitcast_fusion.2 = f32[1,256,1536]{2,1,0:T(8,128)} fusion(f32[512,1536]{1,0:T(8,128)} %copy-done.16, s32[]{:T(128)S(6)} %select_n.265), kind=kLoop, calls=%fused_computation.110 | loop fusion | bytes 3145732 | tf_op jit(solution)/shard_map/stack | solution.py:107
  122.6 6.3 %all-to-all-done.1 = bf16[32,10,640]{2,1,0:T(8,128)(2,1)S(1)} async-done(((bf16[32,10,640]{2,1,0:T(8,128)(2,1)}), bf16[32,10,640]{2,1,0:T(8,128)(2,1)S(1)}, u32[]{:S(2)}, u32[]{:S(2)}) %all-to-all-start.1) | async-done | bytes 409632 | tf_op jit(solution)/shard_map/all_to_all | solution.py:341
  131.2 3.0 %maximum_add_fusion = f32[2,256,1536]{2,1,0:T(8,128)S(1)} fusion(f32[1,256,1536]{2,1,0:T(8,128)} %dynamic-slice_bitcast_fusion.2, f32[1,256,1536]{2,1,0:T(8,128)} %dynamic-slice_bitcast_fusion.3, bf16[2,256,1536]{2,1,0:T(8,128)(2,1)} %collective-permute-done.7), kind=kLoop, calls=%fused_computation.30 | loop fusion | flops 2359296 | bytes 7864320 | tf_op jit(solution)/shard_map/add | solution.py:115
  134.3 1.7 collective-permute-start.8
  136.0 3.6 %fusion.155 = f32[512,1536]{1,0:T(8,128)S(1)} fusion(bf16[2048,512]{1,0:T(8,128)(2,1)S(1)} %bitcast.224, bf16[2048,1536]{1,0:T(8,128)(2,1)S(1)} %bitcast.200), kind=kOutput, calls=%fused_computation.307 | convolution fusion | flops 3221225472 | bytes 11534336 | tf_op jit(solution)/shard_map/dot_general | solution.py:17
  139.5 7.1 %collective-permute-done.8 = bf16[2,128,1536]{2,1,0:T(8,128)(2,1)S(1)} collective-permute-done((bf16[2,128,1536]{2,1,0:T(8,128)(2,1)S(1)}, bf16[2,128,1536]{2,1,0:T(8,128)(2,1)S(1)}, u32[]{:S(2)}, u32[]{:S(2)}) %collective-permute-start.8) | collective-permute-done | bytes 786464 | tf_op jit(solution)/shard_map/ppermute | solution.py:65
  148.3 5.6 %collective-permute-done.9 = bf16[2,64,1536]{2,1,0:T(8,128)(2,1)S(1)} collective-permute-done((bf16[2,64,1536]{2,1,0:T(8,128)(2,1)S(1)}, bf16[2,64,1536]{2,1,0:T(8,128)(2,1)S(1)}, u32[]{:S(2)}, u32[]{:S(2)}) %collective-permute-start.9) | collective-permute-done | bytes 393248 | tf_op jit(solution)/shard_map/ppermute | solution.py:65
  154.2 4.4 %collective-permute-done.10 = bf16[2,32,1536]{2,1,0:T(8,128)(2,1)S(1)} collective-permute-done((bf16[2,32,1536]{2,1,0:T(8,128)(2,1)S(1)}, bf16[2,32,1536]{2,1,0:T(8,128)(2,1)S(1)}, u32[]{:S(2)}, u32[]{:S(2)}) %collective-permute-start.10) | collective-permute-done | bytes 196640 | tf_op jit(solution)/shard_map/ppermute | solution.py:65
  158.8 4.6 %collective-permute-done.11 = bf16[2,32,768]{2,1,0:T(8,128)(2,1)S(1)} collective-permute-done((bf16[2,32,768]{2,1,0:T(8,128)(2,1)S(1)}, bf16[2,32,768]{2,1,0:T(8,128)(2,1)S(1)}, u32[]{:S(2)}, u32[]{:S(2)}) %collective-permute-start.11) | collective-permute-done | bytes 98336 | tf_op jit(solution)/shard_map/ppermute | solution.py:29
  164.8 2.1 collective-permute-start.19
  167.0 2.3 collective-permute-done.12
  169.6 6.7 %collective-permute-done.13 = f32[2,32,768]{2,1,0:T(8,128)S(1)} collective-permute-done((f32[2,32,768]{2,1,0:T(8,128)S(1)}, f32[2,32,768]{2,1,0:T(8,128)S(1)}, u32[]{:S(2)}, u32[]{:S(2)}) %collective-permute-start.13) | collective-permute-done | bytes 196640 | tf_op jit(solution)/shard_map/ppermute | solution.py:65
  178.1 3.1 %collective-permute-done.14 = bf16[2,32,768]{2,1,0:T(8,128)(2,1)S(1)} collective-permute-done((bf16[2,32,768]{2,1,0:T(8,128)(2,1)S(1)}, bf16[2,32,768]{2,1,0:T(8,128)(2,1)S(1)}, u32[]{:S(2)}, u32[]{:S(2)}) %collective-permute-start.14) | collective-permute-done | bytes 98336 | tf_op jit(solution)/shard_map/ppermute | solution.py:65
  181.4 6.7 %collective-permute-done.20 = bf16[2,64,1536]{2,1,0:T(8,128)(2,1)S(1)} collective-permute-done((bf16[2,64,1536]{2,1,0:T(8,128)(2,1)S(1)}, bf16[2,64,1536]{2,1,0:T(8,128)(2,1)S(1)}, u32[]{:S(2)}, u32[]{:S(2)}) %collective-permute-start.20) | collective-permute-done | bytes 393248 | tf_op jit(solution)/shard_map/ppermute | solution.py:65
  189.1 4.1 %collective-permute-done.21 = bf16[2,32,1536]{2,1,0:T(8,128)(2,1)S(1)} collective-permute-done((bf16[2,32,1536]{2,1,0:T(8,128)(2,1)S(1)}, bf16[2,32,1536]{2,1,0:T(8,128)(2,1)S(1)}, u32[]{:S(2)}, u32[]{:S(2)}) %collective-permute-start.21) | collective-permute-done | bytes 196640 | tf_op jit(solution)/shard_map/ppermute | solution.py:65
  193.3 4.6 %collective-permute-done.22 = bf16[2,32,768]{2,1,0:T(8,128)(2,1)S(1)} collective-permute-done((bf16[2,32,768]{2,1,0:T(8,128)(2,1)S(1)}, bf16[2,32,768]{2,1,0:T(8,128)(2,1)S(1)}, u32[]{:S(2)}, u32[]{:S(2)}) %collective-permute-start.22) | collective-permute-done | bytes 98336 | tf_op jit(solution)/shard_map/ppermute | solution.py:29
  198.8 10.8 %collective-permute-start.17 = (bf16[2,256,768]{2,1,0:T(8,128)(2,1)S(1)}, bf16[2,256,768]{2,1,0:T(8,128)(2,1)S(1)}, u32[]{:S(2)}, u32[]{:S(2)}) collective-permute-start(bf16[2,256,768]{2,1,0:T(8,128)(2,1)S(1)} %pad_maximum_fusion.17), channel_id=1, source_target_pairs={{0,2},{2,0},{1,3},{3,1},{4,6},{6,4},{5,7},{7,5},{8,10},{10,8},{9,1... | collective-permute-start | bytes 2359304 | tf_op jit(solution)/shard_map/ppermute | solution.py:29
  209.6 1.8 collective-permute-start.24
  212.1 4.3 %collective-permute-done.24 = f32[2,32,768]{2,1,0:T(8,128)S(1)} collective-permute-done((f32[2,32,768]{2,1,0:T(8,128)S(1)}, f32[2,32,768]{2,1,0:T(8,128)S(1)}, u32[]{:S(2)}, u32[]{:S(2)}) %collective-permute-start.24) | collective-permute-done | bytes 196640 | tf_op jit(solution)/shard_map/ppermute | solution.py:65
  217.2 2.8 %collective-permute-done.25 = bf16[2,32,768]{2,1,0:T(8,128)(2,1)S(1)} collective-permute-done((bf16[2,32,768]{2,1,0:T(8,128)(2,1)S(1)}, bf16[2,32,768]{2,1,0:T(8,128)(2,1)S(1)}, u32[]{:S(2)}, u32[]{:S(2)}) %collective-permute-start.25) | collective-permute-done | bytes 98336 | tf_op jit(solution)/shard_map/ppermute | solution.py:65
  220.5 4.2 %collective-permute-done.26 = bf16[2,64,768]{2,1,0:T(8,128)(2,1)S(1)} collective-permute-done((bf16[2,64,768]{2,1,0:T(8,128)(2,1)S(1)}, bf16[2,64,768]{2,1,0:T(8,128)(2,1)S(1)}, u32[]{:S(2)}, u32[]{:S(2)}) %collective-permute-start.26) | collective-permute-done | bytes 196640 | tf_op jit(solution)/shard_map/ppermute | solution.py:65
  225.0 7.7 %collective-permute-done.27 = bf16[2,128,768]{2,1,0:T(8,128)(2,1)S(1)} collective-permute-done((bf16[2,128,768]{2,1,0:T(8,128)(2,1)S(1)}, bf16[2,128,768]{2,1,0:T(8,128)(2,1)S(1)}, u32[]{:S(2)}, u32[]{:S(2)}) %collective-permute-start.27) | collective-permute-done | bytes 393248 | tf_op jit(solution)/shard_map/ppermute | solution.py:65
  232.9 10.9 %collective-permute-start.28 = (bf16[2,256,768]{2,1,0:T(8,128)(2,1)S(1)}, bf16[2,256,768]{2,1,0:T(8,128)(2,1)S(1)}, u32[]{:S(2)}, u32[]{:S(2)}) collective-permute-start(bf16[2,256,768]{2,1,0:T(8,128)(2,1)S(1)} %pad_maximum_fusion.18), channel_id=1, source_target_pairs={{0,2},{2,0},{1,3},{3,1},{4,6},{6,4},{5,7},{7,5},{8,10},{10,8},{9,1... | collective-permute-start | bytes 2359304 | tf_op jit(solution)/shard_map/ppermute | solution.py:29
  246.3 2.6 %stack.156 = f32[9,512,256]{2,1,0:T(8,128)} convert(bf16[9,512,256]{2,1,0:T(8,128)(2,1)S(1)} %fusion.106) | non-fusion elementwise | flops 1179648 | bytes 7077888 | tf_op jit(solution)/shard_map/stack | solution.py:355
  (292 shorter events, 49.6 us)
Async XLA Ops:
  2.1 10.6 %copy-start.20 = (bf16[1,128,512]{2,1,0:T(8,128)(2,1)S(1)}, bf16[1,128,512]{2,1,0:T(8,128)(2,1)}, u32[]{:S(2)}) copy-start(bf16[1,128,512]{2,1,0:T(8,128)(2,1)} %param.12) | copy-start | bytes 393220
  2.9 9.8 %copy-start.51 = (s32[1,1,16,128]{3,2,1,0:T(8,128)S(1)}, s32[1,1,16,128]{3,2,1,0:T(8,128)}, u32[]{:S(2)}) copy-start(s32[1,1,16,128]{3,2,1,0:T(8,128)} %param.17) | copy-start | bytes 24580
  2.9 9.9 %copy-start.56 = (s32[1,128]{1,0:T(1,128)S(1)}, s32[1,128]{1,0:T(1,128)}, u32[]{:S(2)}) copy-start(s32[1,128]{1,0:T(1,128)} %param.16) | copy-start | bytes 1540
  2.9 9.9 %copy-start.57 = (s32[1,128]{1,0:T(1,128)S(1)}, s32[1,128]{1,0:T(1,128)}, u32[]{:S(2)}) copy-start(s32[1,128]{1,0:T(1,128)} %param.15) | copy-start | bytes 1540
  2.9 10.1 %copy-start.55 = (bf16[1,128]{1,0:T(2,128)(2,1)S(1)}, bf16[1,128]{1,0:T(2,128)(2,1)}, u32[]{:S(2)}) copy-start(bf16[1,128]{1,0:T(2,128)(2,1)} %param.13) | copy-start | bytes 772
  2.9 10.2 %copy-start.58 = (s32[1,128,1]{1,2,0:T(1,128)S(1)}, s32[1,128,1]{1,2,0:T(1,128)}, u32[]{:S(2)}) copy-start(s32[1,128,1]{1,2,0:T(1,128)} %param.14) | copy-start | bytes 1540
  2.9 26.6 %collective-permute-start.2 = (bf16[256,768]{1,0:T(8,128)(2,1)}, bf16[256,768]{1,0:T(8,128)(2,1)}, u32[]{:S(2)}, u32[]{:S(2)}) collective-permute-start(bf16[256,768]{1,0:T(8,128)(2,1)} %pad_maximum_fusion.19), channel_id=1, source_target_pairs={{1,64},{64,1},{65,0},{0,65},{3,66},{66,3},{67,2},{2,67},{5,68},{68... | collective-permute-start | bytes 1179656 | tf_op jit(solution)/shard_map/ppermute | solution.py:29
  6.7 41.7 %collective-permute-start.1 = (bf16[16,1,64,512]{3,2,1,0:T(8,128)(2,1)S(1)}, bf16[16,1,64,512]{3,2,1,0:T(8,128)(2,1)}, u32[]{:S(2)}, u32[]{:S(2)}) collective-permute-start(bf16[16,1,64,512]{3,2,1,0:T(8,128)(2,1)S(1)} %get-tuple-element.36), channel_id=1, source_target_pairs={{2,0},{4,2},{6,4},{8,6},{10,8},{12,10},{14,12},{16,14},{18,16},{20... | collective-permute-start | bytes 3145736 | tf_op jit(solution)/shard_map/ppermute | solution.py:161
  9.6 40.3 %collective-permute-start = (bf16[16,1,64,512]{3,2,1,0:T(8,128)(2,1)S(1)}, bf16[16,1,64,512]{3,2,1,0:T(8,128)(2,1)}, u32[]{:S(2)}, u32[]{:S(2)}) collective-permute-start(bf16[16,1,64,512]{3,2,1,0:T(8,128)(2,1)S(1)} %get-tuple-element.35), channel_id=1, source_target_pairs={{0,2},{2,4},{4,6},{6,8},{8,10},{10,12},{12,14},{14,16},{16,18},{18... | collective-permute-start | bytes 3145736 | tf_op jit(solution)/shard_map/ppermute | solution.py:160
  13.3 10.9 %copy-start.53 = (s32[128]{0:T(128)}, s32[128]{0:T(128)S(1)}, u32[]{:S(2)}) copy-start(s32[128]{0:T(128)S(1)} %multiply_add_fusion) | copy-start | bytes 1540
  14.7 24.9 %all-to-all-start = ((bf16[32,10,640]{2,1,0:T(8,128)(2,1)}), bf16[32,10,640]{2,1,0:T(8,128)(2,1)S(1)}, u32[]{:S(2)}, u32[]{:S(2)}) async-start(bf16[32,10,640]{2,1,0:T(8,128)(2,1)} %reshape.184), calls=%async_computation | async-start | bytes 1310720 | tf_op jit(solution)/shard_map/all_to_all | solution.py:223
  29.5 12.3 %collective-permute-start.3 = (bf16[256,768]{1,0:T(8,128)(2,1)}, bf16[256,768]{1,0:T(8,128)(2,1)S(1)}, u32[]{:S(2)}, u32[]{:S(2)}) collective-permute-start(bf16[256,768]{1,0:T(8,128)(2,1)} %collective-permute-done.2), channel_id=1, source_target_pairs={{0,4},{4,0},{8,12},{12,8},{1,5},{5,1},{9,13},{13,9},{2,6},{6,2},{1... | collective-permute-start | bytes 1179656 | tf_op jit(solution)/shard_map/ppermute | solution.py:29
  30.9 13.8 %collective-permute-start.4 = (bf16[256,768]{1,0:T(8,128)(2,1)}, bf16[256,768]{1,0:T(8,128)(2,1)}, u32[]{:S(2)}, u32[]{:S(2)}) collective-permute-start(bf16[256,768]{1,0:T(8,128)(2,1)} %collective-permute-done.2), channel_id=1, source_target_pairs={{4,8},{8,4},{12,0},{0,12},{5,9},{9,5},{13,1},{1,13},{6,10},{10,6},... | collective-permute-start | bytes 1179656 | tf_op jit(solution)/shard_map/ppermute | solution.py:29
  32.7 12.0 %collective-permute-start.5 = (bf16[256,768]{1,0:T(8,128)(2,1)}, bf16[256,768]{1,0:T(8,128)(2,1)}, u32[]{:S(2)}, u32[]{:S(2)}) collective-permute-start(bf16[256,768]{1,0:T(8,128)(2,1)} %collective-permute-done.2), channel_id=1, source_target_pairs={{0,16},{16,0},{32,48},{48,32},{1,17},{17,1},{33,49},{49,33},{2,18}... | collective-permute-start | bytes 1179656 | tf_op jit(solution)/shard_map/ppermute | solution.py:29
  39.8 35.5 %copy-start.17 = (bf16[320,640]{1,0:T(8,128)(2,1)}, bf16[320,640]{1,0:T(8,128)(2,1)S(1)}, u32[]{:S(2)}) copy-start(bf16[320,640]{1,0:T(8,128)(2,1)S(1)} %reshape.185) | copy-start | bytes 1228804
  40.0 7.3 %copy-start.48 = (f32[320,19]{0,1:T(8,128)}, f32[320,19]{0,1:T(8,128)S(1)}, u32[]{:S(2)}) copy-start(f32[320,19]{0,1:T(8,128)S(1)} %convert_element_type.154) | copy-start | bytes 72964
  40.1 7.2 %copy-start.29 = (pred[128,320]{0,1:T(8,128)(4,1)}, pred[128,320]{0,1:T(8,128)(4,1)S(1)}, u32[]{:S(2)}) copy-start(pred[128,320]{0,1:T(8,128)(4,1)S(1)} %iota_compare_fusion.4) | copy-start | bytes 122884
  47.3 13.0 %collective-permute-start.6 = (bf16[4,256,768]{2,1,0:T(8,128)(2,1)}, bf16[4,256,768]{2,1,0:T(8,128)(2,1)S(1)}, u32[]{:S(2)}, u32[]{:S(2)}) collective-permute-start(bf16[4,256,768]{2,1,0:T(8,128)(2,1)} %get-tuple-element.46), channel_id=1, source_target_pairs={{0,2},{2,0},{1,3},{3,1},{4,6},{6,4},{5,7},{7,5},{8,10},{10,8},{9,1... | collective-permute-start | bytes 4718600 | tf_op jit(solution)/shard_map/ppermute | solution.py:29
  49.8 9.3 %copy-start.7 = (bf16[16,2,64,512]{3,2,1,0:T(8,128)(2,1)}, bf16[16,2,64,512]{3,2,1,0:T(8,128)(2,1)S(1)}, u32[]{:S(2)}) copy-start(bf16[16,2,64,512]{3,2,1,0:T(8,128)(2,1)S(1)} %pad_maximum_fusion.8) | copy-start | bytes 6291460
  52.2 9.2 %copy-start.10 = (bf16[16,2,64,512]{3,2,1,0:T(8,128)(2,1)}, bf16[16,2,64,512]{3,2,1,0:T(8,128)(2,1)S(1)}, u32[]{:S(2)}) copy-start(bf16[16,2,64,512]{3,2,1,0:T(8,128)(2,1)S(1)} %pad_maximum_fusion.7) | copy-start | bytes 6291460
  88.4 16.5 %copy-start.13 = (f32[512,1536]{1,0:T(8,128)}, f32[512,1536]{1,0:T(8,128)S(1)}, u32[]{:S(2)}) copy-start(f32[512,1536]{1,0:T(8,128)S(1)} %fusion.8) | copy-start | bytes 9437188
  106.4 24.8 %collective-permute-start.7 = (bf16[2,256,1536]{2,1,0:T(8,128)(2,1)}, bf16[2,256,1536]{2,1,0:T(8,128)(2,1)}, u32[]{:S(2)}, u32[]{:S(2)}) collective-permute-start(bf16[2,256,1536]{2,1,0:T(8,128)(2,1)} %pad_maximum_fusion.11), channel_id=1, source_target_pairs={{0,2},{2,0},{1,3},{3,1},{4,6},{6,4},{5,7},{7,5},{8,10},{10,8},{9,1... | collective-permute-start | bytes 4718600 | tf_op jit(solution)/shard_map/ppermute | solution.py:29
  110.9 18.0 %all-to-all-start.1 = ((bf16[32,10,640]{2,1,0:T(8,128)(2,1)}), bf16[32,10,640]{2,1,0:T(8,128)(2,1)S(1)}, u32[]{:S(2)}, u32[]{:S(2)}) async-start(bf16[32,10,640]{2,1,0:T(8,128)(2,1)} %reshape.197), calls=%async_computation.1 | async-start | bytes 1310720 | tf_op jit(solution)/shard_map/all_to_all | solution.py:341
  121.3 8.5 %copy-start.54 = (s32[128]{0:T(128)S(1)}, s32[128]{0:T(128)}, u32[]{:S(2)}) copy-start(s32[128]{0:T(128)} %copy-done.53) | copy-start | bytes 1540
  121.4 14.6 %slice-start = ((s8[6291456]{0:T(1024)(128)(4,1)}), s8[2097152]{0:T(1024)(128)(4,1)S(1)}, s32[]{:S(2)}) async-start(s8[6291456]{0:T(1024)(128)(4,1)} %bitcast.199), calls=%async_computation.2 | async-start | bytes 4194304
  134.3 12.3 %collective-permute-start.8 = (bf16[2,128,1536]{2,1,0:T(8,128)(2,1)S(1)}, bf16[2,128,1536]{2,1,0:T(8,128)(2,1)S(1)}, u32[]{:S(2)}, u32[]{:S(2)}) collective-permute-start(bf16[2,128,1536]{2,1,0:T(8,128)(2,1)S(1)} %dynamic-slice_convert_fusion.3), channel_id=1, source_target_pairs={{0,4},{1,5},{2,14},{3,15},{4,0},{5,1},{6,10},{7,11},{8,12},{9,13},... | collective-permute-start | bytes 2359304 | tf_op jit(solution)/shard_map/ppermute | solution.py:65
  146.9 7.0 %collective-permute-start.9 = (bf16[2,64,1536]{2,1,0:T(8,128)(2,1)S(1)}, bf16[2,64,1536]{2,1,0:T(8,128)(2,1)S(1)}, u32[]{:S(2)}, u32[]{:S(2)}) collective-permute-start(bf16[2,64,1536]{2,1,0:T(8,128)(2,1)S(1)} %dynamic-slice_convert_fusion.7), channel_id=1, source_target_pairs={{0,12},{1,13},{2,6},{3,7},{4,8},{5,9},{6,2},{7,3},{8,4},{9,5},{10,... | collective-permute-start | bytes 1179656 | tf_op jit(solution)/shard_map/ppermute | solution.py:65
  147.2 17.0 %collective-permute-start.18 = (bf16[2,256,1536]{2,1,0:T(8,128)(2,1)S(1)}, bf16[2,256,1536]{2,1,0:T(8,128)(2,1)S(1)}, u32[]{:S(2)}, u32[]{:S(2)}) collective-permute-start(bf16[2,256,1536]{2,1,0:T(8,128)(2,1)S(1)} %pad_maximum_fusion.12), channel_id=1, source_target_pairs={{0,2},{2,0},{1,3},{3,1},{4,6},{6,4},{5,7},{7,5},{8,10},{10,8},{9,1... | collective-permute-start | bytes 4718600 | tf_op jit(solution)/shard_map/ppermute | solution.py:29
  154.0 10.2 %copy-start.3 = (f32[1,256,1536]{2,1,0:T(8,128)S(1)}, f32[1,256,1536]{2,1,0:T(8,128)}, u32[]{:S(2)}) copy-start(f32[1,256,1536]{2,1,0:T(8,128)} %dynamic-slice_bitcast_fusion.1) | copy-start | bytes 4718596
  154.0 4.6 %collective-permute-start.10 = (bf16[2,32,1536]{2,1,0:T(8,128)(2,1)S(1)}, bf16[2,32,1536]{2,1,0:T(8,128)(2,1)S(1)}, u32[]{:S(2)}, u32[]{:S(2)}) collective-permute-start(bf16[2,32,1536]{2,1,0:T(8,128)(2,1)S(1)} %dynamic-slice_convert_fusion.9), channel_id=1, source_target_pairs={{0,1},{1,0},{2,3},{3,2},{4,5},{5,4},{6,7},{7,6},{8,9},{9,8},{10,11... | collective-permute-start | bytes 589832 | tf_op jit(solution)/shard_map/ppermute | solution.py:65
  158.7 4.8 %collective-permute-start.11 = (bf16[2,32,768]{2,1,0:T(8,128)(2,1)S(1)}, bf16[2,32,768]{2,1,0:T(8,128)(2,1)S(1)}, u32[]{:S(2)}, u32[]{:S(2)}) collective-permute-start(bf16[2,32,768]{2,1,0:T(8,128)(2,1)S(1)} %pad_maximum_fusion.25), channel_id=1, source_target_pairs={{1,64},{64,1},{65,0},{0,65},{3,66},{66,3},{67,2},{2,67},{5,68},{68... | collective-permute-start | bytes 294920 | tf_op jit(solution)/shard_map/ppermute | solution.py:29
  163.5 5.8 %collective-permute-start.12 = (f32[2,32,768]{2,1,0:T(8,128)S(1)}, f32[2,32,768]{2,1,0:T(8,128)S(1)}, u32[]{:S(2)}, u32[]{:S(2)}) collective-permute-start(f32[2,32,768]{2,1,0:T(8,128)S(1)} %maximum_add_fusion.2), channel_id=1, source_target_pairs={{0,16},{1,17},{2,50},{3,51},{4,20},{5,21},{6,54},{7,55},{8,24},{9,... | collective-permute-start | bytes 589832 | tf_op jit(solution)/shard_map/ppermute | solution.py:65
  164.8 12.9 %collective-permute-start.19 = (bf16[2,128,1536]{2,1,0:T(8,128)(2,1)S(1)}, bf16[2,128,1536]{2,1,0:T(8,128)(2,1)S(1)}, u32[]{:S(2)}, u32[]{:S(2)}) collective-permute-start(bf16[2,128,1536]{2,1,0:T(8,128)(2,1)S(1)} %dynamic-slice_convert_fusion), channel_id=1, source_target_pairs={{0,16},{1,17},{2,50},{3,51},{4,20},{5,21},{6,54},{7,55},{8,24},{9,... | collective-permute-start | bytes 2359304 | tf_op jit(solution)/shard_map/ppermute | solution.py:65
  169.3 7.0 %collective-permute-start.13 = (f32[2,32,768]{2,1,0:T(8,128)S(1)}, f32[2,32,768]{2,1,0:T(8,128)S(1)}, u32[]{:S(2)}, u32[]{:S(2)}) collective-permute-start(f32[2,32,768]{2,1,0:T(8,128)S(1)} %add.250), channel_id=1, source_target_pairs={{0,48},{1,49},{2,18},{3,19},{4,52},{5,53},{6,22},{7,23},{8,56},{9,... | collective-permute-start | bytes 589832 | tf_op jit(solution)/shard_map/ppermute | solution.py:65
  169.5 8.6 %collective-permute-start.29 = (bf16[128,640]{1,0:T(8,128)(2,1)S(1)}, bf16[128,640]{1,0:T(8,128)(2,1)S(1)}, u32[]{:S(2)}, u32[]{:S(2)}) collective-permute-start(bf16[128,640]{1,0:T(8,128)(2,1)S(1)} %pad_maximum_fusion.24), channel_id=1, source_target_pairs={{0,64},{64,0},{1,65},{65,1},{2,66},{66,2},{3,67},{67,3},{4,68},{68... | collective-permute-start | bytes 491528 | tf_op jit(solution)/shard_map/ppermute | solution.py:346
  176.4 4.9 %collective-permute-start.14 = (bf16[2,32,768]{2,1,0:T(8,128)(2,1)S(1)}, bf16[2,32,768]{2,1,0:T(8,128)(2,1)S(1)}, u32[]{:S(2)}, u32[]{:S(2)}) collective-permute-start(bf16[2,32,768]{2,1,0:T(8,128)(2,1)S(1)} %add_convert_fusion.1), channel_id=1, source_target_pairs={{0,1},{1,0},{2,3},{3,2},{4,5},{5,4},{6,7},{7,6},{8,9},{9,8},{10,11... | collective-permute-start | bytes 294920 | tf_op jit(solution)/shard_map/ppermute | solution.py:65
  178.0 10.1 %collective-permute-start.20 = (bf16[2,64,1536]{2,1,0:T(8,128)(2,1)S(1)}, bf16[2,64,1536]{2,1,0:T(8,128)(2,1)S(1)}, u32[]{:S(2)}, u32[]{:S(2)}) collective-permute-start(bf16[2,64,1536]{2,1,0:T(8,128)(2,1)S(1)} %dynamic-slice_convert_fusion.6), channel_id=1, source_target_pairs={{0,48},{1,49},{2,18},{3,19},{4,52},{5,53},{6,22},{7,23},{8,56},{9,... | collective-permute-start | bytes 1179656 | tf_op jit(solution)/shard_map/ppermute | solution.py:65
  181.3 7.0 %collective-permute-start.15 = (bf16[2,64,768]{2,1,0:T(8,128)(2,1)S(1)}, bf16[2,64,768]{2,1,0:T(8,128)(2,1)S(1)}, u32[]{:S(2)}, u32[]{:S(2)}) collective-permute-start(bf16[2,64,768]{2,1,0:T(8,128)(2,1)S(1)} %pad_maximum_fusion.22), channel_id=1, source_target_pairs={{0,12},{1,13},{2,6},{3,7},{4,8},{5,9},{6,2},{7,3},{8,4},{9,5},{10,... | collective-permute-start | bytes 589832 | tf_op jit(solution)/shard_map/ppermute | solution.py:65
  188.2 4.9 %collective-permute-start.21 = (bf16[2,32,1536]{2,1,0:T(8,128)(2,1)S(1)}, bf16[2,32,1536]{2,1,0:T(8,128)(2,1)S(1)}, u32[]{:S(2)}, u32[]{:S(2)}) collective-permute-start(bf16[2,32,1536]{2,1,0:T(8,128)(2,1)S(1)} %dynamic-slice_convert_fusion.8), channel_id=1, source_target_pairs={{0,1},{1,0},{2,3},{3,2},{4,5},{5,4},{6,7},{7,6},{8,9},{9,8},{10,11... | collective-permute-start | bytes 589832 | tf_op jit(solution)/shard_map/ppermute | solution.py:65
  188.4 10.2 %collective-permute-start.16 = (bf16[2,128,768]{2,1,0:T(8,128)(2,1)S(1)}, bf16[2,128,768]{2,1,0:T(8,128)(2,1)S(1)}, u32[]{:S(2)}, u32[]{:S(2)}) collective-permute-start(bf16[2,128,768]{2,1,0:T(8,128)(2,1)S(1)} %pad_maximum_fusion.20), channel_id=1, source_target_pairs={{0,4},{1,5},{2,14},{3,15},{4,0},{5,1},{6,10},{7,11},{8,12},{9,13},... | collective-permute-start | bytes 1179656 | tf_op jit(solution)/shard_map/ppermute | solution.py:65
  193.2 4.8 %collective-permute-start.22 = (bf16[2,32,768]{2,1,0:T(8,128)(2,1)S(1)}, bf16[2,32,768]{2,1,0:T(8,128)(2,1)S(1)}, u32[]{:S(2)}, u32[]{:S(2)}) collective-permute-start(bf16[2,32,768]{2,1,0:T(8,128)(2,1)S(1)} %pad_maximum_fusion.26), channel_id=1, source_target_pairs={{1,64},{64,1},{65,0},{0,65},{3,66},{66,3},{67,2},{2,67},{5,68},{68... | collective-permute-start | bytes 294920 | tf_op jit(solution)/shard_map/ppermute | solution.py:29
  198.0 11.6 %collective-permute-start.23 = (f32[2,32,768]{2,1,0:T(8,128)S(1)}, f32[2,32,768]{2,1,0:T(8,128)S(1)}, u32[]{:S(2)}, u32[]{:S(2)}) collective-permute-start(f32[2,32,768]{2,1,0:T(8,128)S(1)} %maximum_add_fusion.3), channel_id=1, source_target_pairs={{0,4},{1,5},{2,14},{3,15},{4,0},{5,1},{6,10},{7,11},{8,12},{9,13},... | collective-permute-start | bytes 589832 | tf_op jit(solution)/shard_map/ppermute | solution.py:65
  198.8 21.3 %collective-permute-start.17 = (bf16[2,256,768]{2,1,0:T(8,128)(2,1)S(1)}, bf16[2,256,768]{2,1,0:T(8,128)(2,1)S(1)}, u32[]{:S(2)}, u32[]{:S(2)}) collective-permute-start(bf16[2,256,768]{2,1,0:T(8,128)(2,1)S(1)} %pad_maximum_fusion.17), channel_id=1, source_target_pairs={{0,2},{2,0},{1,3},{3,1},{4,6},{6,4},{5,7},{7,5},{8,10},{10,8},{9,1... | collective-permute-start | bytes 2359304 | tf_op jit(solution)/shard_map/ppermute | solution.py:29
  209.6 6.8 %collective-permute-start.24 = (f32[2,32,768]{2,1,0:T(8,128)S(1)}, f32[2,32,768]{2,1,0:T(8,128)S(1)}, u32[]{:S(2)}, u32[]{:S(2)}) collective-permute-start(f32[2,32,768]{2,1,0:T(8,128)S(1)} %add.261), channel_id=1, source_target_pairs={{0,12},{1,13},{2,6},{3,7},{4,8},{5,9},{6,2},{7,3},{8,4},{9,5},{10,... | collective-permute-start | bytes 589832 | tf_op jit(solution)/shard_map/ppermute | solution.py:65
  216.5 3.5 %collective-permute-start.25 = (bf16[2,32,768]{2,1,0:T(8,128)(2,1)S(1)}, bf16[2,32,768]{2,1,0:T(8,128)(2,1)S(1)}, u32[]{:S(2)}, u32[]{:S(2)}) collective-permute-start(bf16[2,32,768]{2,1,0:T(8,128)(2,1)S(1)} %add_convert_fusion), channel_id=1, source_target_pairs={{0,1},{1,0},{2,3},{3,2},{4,5},{5,4},{6,7},{7,6},{8,9},{9,8},{10,11... | collective-permute-start | bytes 294920 | tf_op jit(solution)/shard_map/ppermute | solution.py:65
  220.0 4.6 %collective-permute-start.26 = (bf16[2,64,768]{2,1,0:T(8,128)(2,1)S(1)}, bf16[2,64,768]{2,1,0:T(8,128)(2,1)S(1)}, u32[]{:S(2)}, u32[]{:S(2)}) collective-permute-start(bf16[2,64,768]{2,1,0:T(8,128)(2,1)S(1)} %pad_maximum_fusion.23), channel_id=1, source_target_pairs={{0,48},{1,49},{2,18},{3,19},{4,52},{5,53},{6,22},{7,23},{8,56},{9,... | collective-permute-start | bytes 589832 | tf_op jit(solution)/shard_map/ppermute | solution.py:65
  224.8 7.9 %collective-permute-start.27 = (bf16[2,128,768]{2,1,0:T(8,128)(2,1)S(1)}, bf16[2,128,768]{2,1,0:T(8,128)(2,1)S(1)}, u32[]{:S(2)}, u32[]{:S(2)}) collective-permute-start(bf16[2,128,768]{2,1,0:T(8,128)(2,1)S(1)} %pad_maximum_fusion.21), channel_id=1, source_target_pairs={{0,16},{1,17},{2,50},{3,51},{4,20},{5,21},{6,54},{7,55},{8,24},{9,... | collective-permute-start | bytes 1179656 | tf_op jit(solution)/shard_map/ppermute | solution.py:65
  232.9 12.8 %collective-permute-start.28 = (bf16[2,256,768]{2,1,0:T(8,128)(2,1)S(1)}, bf16[2,256,768]{2,1,0:T(8,128)(2,1)S(1)}, u32[]{:S(2)}, u32[]{:S(2)}) collective-permute-start(bf16[2,256,768]{2,1,0:T(8,128)(2,1)S(1)} %pad_maximum_fusion.18), channel_id=1, source_target_pairs={{0,2},{2,0},{1,3},{3,1},{4,6},{6,4},{5,7},{7,5},{8,10},{10,8},{9,1... | collective-permute-start | bytes 2359304 | tf_op jit(solution)/shard_map/ppermute | solution.py:29
  (46 other events, 123.7 us)

commit v2 on v1

--- a/solution.py
+++ b/solution.py
@@ -39,14 +39,7 @@
     return place >> 1 if kind else (place ^ (place >> 1)) & 1
 
 
-def partner(dim, place):
-    _, kind = dim
-    if kind == 0:
-        return place ^ 1
-    return (place + (1 if place & 1 else -1)) % 4
-
-
-def swap_by_core(value, dims):
+def permute_by_core(value, axes, flip):
     sizes = [lax.axis_size(name) for name in ALL]
     perm = []
     for index in range(math.prod(sizes)):
@@ -55,8 +48,7 @@
             spot[name] = rest % size
             rest //= size
         spot["y"] = spot["fsdp"] * 2 + spot["scan"]
-        dim = dims[spot["core"]]
-        spot[dim[0]] = partner(dim, spot[dim[0]])
+        spot[axes[spot["core"]]] ^= flip
         spot["fsdp"], spot["scan"] = spot["y"] // 2, spot["y"] % 2
         target = 0
         for name, size in zip(ALL, sizes):
@@ -65,25 +57,48 @@
     return lax.ppermute(value, ALL, perm)
 
 
-def bit_by_core(dims):
-    return jnp.where(lax.axis_index("core") == 0, bit(*dims[0]), bit(*dims[1]))
-
-
-def halve(value, dims):
-    size = value.shape[1] // 2
-    mine = bit_by_core(dims)
-    sent = lax.dynamic_slice_in_dim(value, (1 - mine) * size, size, 1)
-    kept = lax.dynamic_slice_in_dim(value, mine * size, size, 1)
-    return kept + swap_by_core(sent.astype(BF), dims).astype(F32)
-
-
-def own_columns(value):
+def place_by_core(axes):
+    first, second = (lax.axis_index(axis) for axis in axes)
+    return jnp.where(lax.axis_index("core") == 0, first, second)
+
+
+def quarter(value, axes):
+    size = value.shape[1] // 4
+    mine = place_by_core(axes)
+    total = lax.dynamic_slice_in_dim(value, mine * size, size, 1)
+    for flip in (1, 3, 2):
+        sent = lax.dynamic_slice_in_dim(value, (mine ^ flip) * size, size, 1)
+        total = total + permute_by_core(sent.astype(BF), axes, flip).astype(F32)
+    return total
+
+
+def sum_columns(value):
     cols = value.shape[2] // 6
     own, far = (
         jnp.concatenate([value[:, :, (2 * g + h) * cols :][:, :, :cols] for g in range(3)], axis=2)
         for h in range(2)
     )
-    return own + swap(far.astype(BF), "y", 1).astype(F32)
+    own, far = own.astype(BF), far.astype(BF)
+    near = permute_by_core(own, ("y", "y"), 1)
+    across = permute_by_core(far, ("y", "y"), 3)
+    opposite = permute_by_core(far, ("y", "y"), 2)
+    return (own.astype(F32) + near.astype(F32)) + (across.astype(F32) + opposite.astype(F32))
+
+
+def regather(value, axes):
+    mine = place_by_core(axes)
+    got = [value] + [permute_by_core(value, axes, flip) for flip in (1, 2, 3)]
+    pieces = []
+    for spot in range(4):
+        flip = mine ^ spot
+        pieces.append(
+            jnp.where(
+                flip < 2,
+                jnp.where(flip == 0, got[0], got[1]),
+                jnp.where(flip == 2, got[2], got[3]),
+            )
+        )
+    return jnp.concatenate(pieces, axis=1)
 
 
 def joined(value, other, mine):
@@ -91,13 +106,6 @@
     return jnp.concatenate(
         [jnp.where(first, value, other), jnp.where(first, other, value)], axis=1
     )
-
-
-XA, XB, YA, ZA, ZB = ("x", 0), ("x", 1), ("y", 0), ("z", 0), ("z", 1)
-STEPS = {
-    "s1": ((XA, XB), (XB, XA), (YA, YA), (ZA, ZB), (ZB, ZA)),
-    "s2": ((ZA, ZB), (ZB, ZA), (YA, YA), (XA, XB), (XB, XA)),
-}
 
 
 def reduce_first(grads, flips):
@@ -115,22 +123,20 @@
     return kept + swap(sent.astype(BF), "core", 0).astype(F32)
 
 
-def reduce_rest(name, value):
-    steps = STEPS[name]
-    for index in range(3):
-        value = halve(value, steps[index])
-    value = own_columns(value)
-    for index in range(3, 5):
-        value = value + swap_by_core(value, steps[index])
-    value = value.astype(BF)
-    for index in (2, 1, 0):
-        other = swap_by_core(value, steps[index])
-        value = joined(value, other, bit_by_core(steps[index]))
+def reduce_middle(value):
+    value = quarter(value, ("x", "z"))
+    value = quarter(value, ("z", "x"))
+    return sum_columns(value).astype(BF)
+
+
+def reduce_last(value):
+    value = regather(value, ("z", "x"))
+    value = regather(value, ("x", "z"))
     return joined(value, swap(value, "core", 0), lax.axis_index("core"))
 
 
 def blocks_of(spatial, temporal):
-    color = bit("x", 0) ^ (bit("x", 1) * 2) ^ (bit("z", 0) * 3)
+    color = bit("z", 0) ^ (bit("z", 1) * 2) ^ (bit("y", 0) * 3)
     rows, cols = spatial.shape[1] // 2, spatial.shape[2]
     core = lax.axis_index("core")
     start = core * rows
@@ -139,7 +145,7 @@
     part = jnp.where(color == 3, lags, taps)
     part = jnp.concatenate([part[0], part[1], part[2]], axis=1)
     part = swap(part, "y", 1)
-    parts = [part, swap(part, "x", 0), swap(part, "x", 1), swap(part, "z", 0)]
+    parts = [part, swap(part, "z", 0), swap(part, "z", 1), swap(part, "y", 0)]
     mine = jnp.stack(parts)
     other = swap(mine, "core", 0)
     both = jnp.stack([mine, other])
@@ -227,12 +233,6 @@
         concat_axis=0,
         tiled=True,
     ).reshape(slot_count, PACK)
-    slot_weight = held[:, :channels]
-    extras = held[:, channels : channels + 3 + frames].astype(F32)
-    slot_bias = extras[:, 0]
-    slot_cell = jnp.where(extras[:, 2] > 0.5, extras[:, 1].astype(jnp.int32), cells)
-    slot_spikes = extras[:, 3:].T
-
     shifted_rows = [
         jnp.concatenate([low, frames_in[:, :1]], axis=1).reshape(-1, channels),
         frames_in.reshape(-1, channels),
@@ -258,7 +258,13 @@
     )
     near_out = convolve(near_weights)
     far_out = convolve(jnp.concatenate([block(h, g) for g in range(3) for h in range(2)]))
+    far_out, held = lax.optimization_barrier((far_out, held))
     spatial_out = jnp.concatenate([near_out, far_out], axis=2)
+    slot_weight = held[:, :channels]
+    extras = held[:, channels : channels + 3 + frames].astype(F32)
+    slot_bias = extras[:, :1]
+    slot_cell = jnp.where(extras[:, 2:3] > 0.5, extras[:, 1:2].astype(jnp.int32), cells)
+    slot_spikes = extras[:, 3:]
 
     lag_blocks = [block(q ^ fsdp, 3) for q in range(2)]
     temporal = [
@@ -286,23 +292,21 @@
         )
     features = jax.nn.elu(mixed).astype(BF)
 
-    here = jnp.arange(cells)[:, None] == slot_cell[None, :]
+    here = slot_cell == jnp.arange(cells)[None, :]
     scores = lax.dot_general(
-        features, slot_weight, (((1,), (1,)), ((), ())), preferred_element_type=F32
-    ).reshape(frames, cells, slot_count)
-    logits = jnp.sum(jnp.where(here[None], scores, 0.0), axis=1) + slot_bias[None, :]
+        slot_weight, features, (((1,), (1,)), ((), ())), preferred_element_type=F32
+    ).reshape(slot_count, frames, cells)
+    logits = jnp.sum(jnp.where(here[:, None, :], scores, 0.0), axis=2) + slot_bias
     delta = (jnp.exp(logits) - slot_spikes) * scale_factor
     coarse = lax.reduce_precision(delta, 8, 7)
-    pieces = jnp.concatenate([coarse, delta - coarse], axis=1).astype(BF)
-    here_twice = jnp.concatenate([here, here], axis=1)
-    spread_twice = jnp.where(here_twice[None], pieces[:, None, :], jnp.zeros((), BF)).reshape(
-        -1, 2 * slot_count
-    )
-    spread = spread_twice[:, :slot_count]
-    feature_grad = jnp.dot(
-        spread_twice,
-        jnp.concatenate([slot_weight, slot_weight]),
-        preferred_element_type=F32,
+    spread, rest = (
+        jnp.where(here[:, None, :], piece.astype(BF)[:, :, None], jnp.zeros((), BF)).reshape(
+            slot_count, -1
+        )
+        for piece in (coarse, delta - coarse)
+    )
+    feature_grad = contract_rows(
+        jnp.concatenate([spread, rest]), jnp.concatenate([slot_weight, slot_weight])
     )
     slope = jnp.where(mixed > 0, 1.0, jnp.exp(jnp.minimum(mixed, 0.0)))
     mixed_grad = (feature_grad * slope).astype(BF)
@@ -311,10 +315,10 @@
         [back_pad[lag : lag + frames].reshape(-1, channels) for lag in range(3)], axis=1
     )
     grad_t = contract_rows(spatial_out.reshape(-1, channels), later)
-    slot_grad = contract_rows(spread, features)
-    slot_bias_grad = jnp.sum(delta, axis=0)
+    slot_grad = jnp.dot(spread, features, preferred_element_type=F32)
+    slot_bias_grad = jnp.sum(delta, axis=1, keepdims=True)
     back = jnp.concatenate(
-        [slot_grad, slot_bias_grad[:, None], jnp.zeros((slot_count, PACK - channels - 1), F32)],
+        [slot_grad, slot_bias_grad, jnp.zeros((slot_count, PACK - channels - 1), F32)],
         axis=1,
     ).astype(BF)
     back = lax.optimization_barrier(back)
@@ -335,15 +339,18 @@
     first_part, wider = lax.optimization_barrier((first_part, wider))
     grad_2 = contract_rows(shifted_rows[2], wider)
     second_part = reduce_first((grad_1, grad_2), (0, 0))
-    total_1 = reduce_rest("s1", first_part)
-    total_2 = reduce_rest("s2", second_part)
+    middle_1 = reduce_middle(first_part)
+    middle_2 = reduce_middle(second_part)
 
     returned = lax.all_to_all(
         back.reshape(tile_count, capacity, PACK), TILE, split_axis=0, concat_axis=0, tiled=True
     ).reshape(slot_count, PACK)
+    returned, middle_2 = lax.optimization_barrier((returned, middle_2))
     mine = contract_rows(selector, returned)
     mine = jnp.concatenate([local(mine[:, :channels]), mine[:, channels:]], axis=1).astype(BF)
     other = lax.ppermute(mine, "fsdp", [(0, 1), (1, 0)])
+    total_1 = reduce_last(middle_1)
+    total_2 = reduce_last(middle_2)
     summed = mine.astype(F32) + other.astype(F32)
     weight_grad = summed[:, :channels]
     bias_grad = summed[:, channels]

time: 254 us -> 253 us (level)
  waiting for transfers between devices: 85.4 us -> 51.4 us
  starting transfers between devices: 60.9 us -> 90.7 us
  other arithmetic: 25 us -> 31 us
    ppermute x16 -> x30, starting transfers between devices: 8.42 us -> 33.7 us  [permute_by_core(): return lax.ppermute(value, ALL, perm)]
    ppermute x16 -> x30, waiting for transfers between devices: 60.3 us -> 41 us  [permute_by_core(): return lax.ppermute(value, ALL, perm)]
    all_to_all x1, starting transfers between devices: 5.12 us -> 15.1 us  [compute(): lax.all_to_all(back.reshape(tile_count, capacity, PACK), TILE, split_axis...]
    ppermute x11 -> x9, waiting for transfers between devices: 13 us -> 4.95 us  [swap(): return lax.ppermute(value, name, perm)]
    all_to_all x1, waiting for transfers between devices: 6.29 us -> 0.01 us  [compute(): lax.all_to_all(back.reshape(tile_count, capacity, PACK), TILE, split_axis...]
    ppermute x11 -> x9, starting transfers between devices: 32 us -> 26.3 us  [swap(): return lax.ppermute(value, name, perm)]
    select_n x8, other arithmetic: 0.78 us -> 4.61 us  [the longest x1 3.06 us: compute(): jnp.where(here[:, None, :], piece.astype(BF)[:, :, None], jnp.zeros((), BF))]
    another operation x8, local copies, waits for them, and re-layouts: 5.8 us -> 2.19 us  [reduce_first(): jnp.stack([lax.dynamic_slice_in_dim(grad, (core ^ flip ^ far) * size, siz...]
  transfers between devices with their start and end apart: 32 -> 44, of which waited for: 20 -> 21; matrix products, arithmetic and copies ran while one was open for 17% -> 20% of each run, Pallas kernels for 0% -> 0%
where the time goes in v2:
time: 253 us; the launch traced here: 249 us
  starting transfers between devices  90.7 us (36%)
  waiting for transfers between devices  51.4 us (20%)
  matrix products  42.3 us (17%)
  other arithmetic  31 us (12%)
  local copies, waits for them, and re-layouts  30.5 us (12%)
  between operations  2.63 us (1%)
    ppermute x30, waiting for transfers between devices, permute_by_core(): return lax.ppermute(value, ALL, perm)  41 us
    ppermute x30, starting transfers between devices, permute_by_core(): return lax.ppermute(value, ALL, perm)  33.7 us
    ppermute x9, starting transfers between devices, swap(): return lax.ppermute(value, name, perm)  26.3 us
    dot_general x6, matrix products, contract_rows(): lax.dot_general(left, right, (((0,), (0,)), ((), ())), preferred_element_...  18.2 us
    all_to_all x1, starting transfers between devices, compute(): lax.all_to_all(back.reshape(tile_count, capacity, PACK), TILE, split_axis...  15.1 us
    dot_general x2, matrix products, convolve(): sums = jnp.dot(taller, weights, preferred_element_type=F32)  10.2 us
    unnamed x138, local copies, waits for them, and re-layouts  9.04 us
    all_to_all x1, starting transfers between devices, compute(): lax.all_to_all(packed.reshape(tile_count, capacity, PACK), TILE, split_ax...  7.88 us
  transfers between devices with their start and end apart: 44, of which 21 were waited for; matrix products, arithmetic and copies ran while one was open for 20% of the time, Pallas kernels for 0%

profile of v2, /device:TPU:1, one launch (start us, length us, event | category | flops | bytes accessed | tf_op | source)
XLA Modules:
  0.0 248.6 jit_solution(9216722638911006413)
XLA Ops:
  2.2 3.6 %collective-permute-start.2 = (bf16[256,768]{1,0:T(8,128)(2,1)S(1)}, bf16[256,768]{1,0:T(8,128)(2,1)}, u32[]{:S(2)}, u32[]{:S(2)}) collective-permute-start(bf16[256,768]{1,0:T(8,128)(2,1)S(1)} %pad_maximum_fusion.19), channel_id=1, source_target_pairs={{1,64},{64,1},{65,0},{0,65},{3,66},{66,3},{67,2},{2,67},{5,68},{68... | collective-permute-start | bytes 1179656 | tf_op jit(solution)/shard_map/ppermute | solution.py:29
  7.3 3.9 %collective-permute-start = (bf16[16,1,64,512]{3,2,1,0:T(8,128)(2,1)}, bf16[16,1,64,512]{3,2,1,0:T(8,128)(2,1)}, u32[]{:S(2)}, u32[]{:S(2)}) collective-permute-start(bf16[16,1,64,512]{3,2,1,0:T(8,128)(2,1)} %get-tuple-element.45), channel_id=1, source_target_pairs={{0,2},{2,4},{4,6},{6,8},{8,10},{10,12},{12,14},{14,16},{16,18},{18... | collective-permute-start | bytes 3145736 | tf_op jit(solution)/shard_map/ppermute | solution.py:166
  13.4 7.9 %all-to-all-start = ((bf16[32,10,640]{2,1,0:T(8,128)(2,1)}), bf16[32,10,640]{2,1,0:T(8,128)(2,1)S(1)}, u32[]{:S(2)}, u32[]{:S(2)}) async-start(bf16[32,10,640]{2,1,0:T(8,128)(2,1)} %reshape.155), calls=%async_computation | async-start | bytes 1310720 | tf_op jit(solution)/shard_map/all_to_all | solution.py:229
  21.3 2.1 collective-permute-start.1
  26.3 2.8 %collective-permute-start.4 = (bf16[256,768]{1,0:T(8,128)(2,1)}, bf16[256,768]{1,0:T(8,128)(2,1)}, u32[]{:S(2)}, u32[]{:S(2)}) collective-permute-start(bf16[256,768]{1,0:T(8,128)(2,1)} %collective-permute-done.2), channel_id=1, source_target_pairs={{16,32},{32,16},{48,0},{0,48},{17,33},{33,17},{49,1},{1,49},{18,34... | collective-permute-start | bytes 1179656 | tf_op jit(solution)/shard_map/ppermute | solution.py:29
  31.3 5.5 %all-to-all-done = bf16[32,10,640]{2,1,0:T(8,128)(2,1)S(1)} async-done(((bf16[32,10,640]{2,1,0:T(8,128)(2,1)}), bf16[32,10,640]{2,1,0:T(8,128)(2,1)S(1)}, u32[]{:S(2)}, u32[]{:S(2)}) %all-to-all-start) | async-done | bytes 409632 | tf_op jit(solution)/shard_map/all_to_all | solution.py:229
  37.6 4.3 %collective-permute-done.4 = bf16[256,768]{1,0:T(8,128)(2,1)} collective-permute-done((bf16[256,768]{1,0:T(8,128)(2,1)}, bf16[256,768]{1,0:T(8,128)(2,1)}, u32[]{:S(2)}, u32[]{:S(2)}) %collective-permute-start.4) | collective-permute-done | bytes 393248 | tf_op jit(solution)/shard_map/ppermute | solution.py:29
  41.8 2.7 %fusion.131 = (bf16[1,4,256,768]{3,2,1,0:T(8,128)(2,1)S(1)}, bf16[4,256,768]{2,1,0:T(8,128)(2,1)}) fusion(bf16[1,256,768]{2,1,0:T(8,128)(2,1)} %bitcast.21, bf16[1,256,768]{2,1,0:T(8,128)(2,1)} %bitcast.20, bf16[1,256,768]{2,1,0:T(8,128)(2,1)} %bitcast.19, bf16[1,256,768]{2,1,0:T(8,128)(2,1)} %bitcast.18), kind=kLoop, calls=%fused_computation.295 | loop fusion | flops 2359296 | bytes 4718592 | tf_op jit(solution)/shard_map/stack | solution.py:151
  46.4 1.8 pad_maximum_fusion.7
  48.3 2.6 %pad_maximum_fusion.8 = bf16[16,2,64,512]{3,2,1,0:T(8,128)(2,1)S(1)} fusion(bf16[16,1,64,512]{3,2,1,0:T(8,128)(2,1)} %collective-permute-done.1, bf16[16,1,64,512]{3,2,1,0:T(8,128)(2,1)} %get-tuple-element.45), kind=kLoop, calls=%fused_computation.67 | loop fusion | flops 1048576 | bytes 4194304 | tf_op jit(solution)/shard_map/concatenate | solution.py:239
  51.7 5.1 %fusion.10 = f32[2048,768]{1,0:T(8,128)S(1)} fusion(bf16[2048,512]{1,0:T(8,128)(2,1)S(1)} %bitcast.219, bf16[2048,512]{1,0:T(8,128)(2,1)S(1)} %bitcast.216, bf16[2048,512]{1,0:T(8,128)(2,1)S(1)} %bitcast.222, bf16[512,256]{1,0:T(8,128)(2,1)S(1)} %copy-done.43, bf16[512,256]{1,0:T(8,128)(2,1)S(1)} %copy-done.36, bf16[512,256]{1,0:T(8,128)(2,1)S(1)} %copy-done.37, ...), kind=kOutput, calls=%fused_computation.38 | convolution fusion | flops 4871946240 | bytes 14942208 | tf_op jit(solution)/shard_map/dot_general | solution.py:244
  61.4 5.1 %fusion.9 = f32[2048,768]{1,0:T(8,128)S(1)} fusion(bf16[1536,768]{1,0:T(8,128)(2,1)S(1)} %bitcast_dynamic-update-slice_fusion, bf16[2048,512]{1,0:T(8,128)(2,1)S(1)} %bitcast.220, bf16[2048,512]{1,0:T(8,128)(2,1)S(1)} %bitcast.217, bf16[2048,512]{1,0:T(8,128)(2,1)S(1)} %bitcast.223), kind=kOutput, calls=%fused_computation.37 | convolution fusion | flops 4850712576 | bytes 14942208 | tf_op jit(solution)/shard_map/dot_general | solution.py:244
  67.1 2.0 fusion.31
  71.5 1.8 fusion.12
  79.3 2.0 convolution_bitcast_fusion
  83.1 3.1 %broadcast_select_fusion.1 = (bf16[320,16,128]{2,1,0:T(8,128)(2,1)S(1)}, bf16[320,16,128]{2,1,0:T(8,128)(2,1)S(1)}) fusion(pred[320,128]{1,0:T(8,128)(4,1)} %copy-done.34, bf16[320,16]{1,0:T(8,128)(2,1)S(1)} %copy.36, bf16[320,16]{1,0:T(8,128)(2,1)S(1)} %copy.37), kind=kLoop, calls=%fused_computation.112 | loop fusion | flops 1310720 | bytes 2682880 | tf_op jit(solution)/shard_map/jit(_where)/select_n | solution.py:303
  86.2 4.2 %convolution_convert_fusion.2 = bf16[320,512]{1,0:T(8,128)(2,1)S(1)} fusion(bf16[40,8,16,128]{3,2,1,0:T(8,128)(2,1)S(1)} %bitcast.202, f32[2048,512]{1,0:T(8,128)} %copy-done), kind=kOutput, calls=%fused_computation.114 | convolution fusion | flops 675446784 | bytes 5832704 | tf_op jit(solution)/shard_map/dot_general | solution.py:318
  92.6 2.3 fusion.5
  96.3 3.5 %convolution_convert_fusion = bf16[2048,512]{1,0:T(8,128)(2,1)S(1)} fusion(bf16[2048,512]{1,0:T(8,128)(2,1)S(1)} %bitcast.213, bf16[2048,512]{1,0:T(8,128)(2,1)S(1)} %bitcast.211, bf16[2048,512]{1,0:T(8,128)(2,1)S(1)} %fusion.5, bf16[256,256]{1,0:T(8,128)(2,1)S(1)} %copy-done.24, bf16[256,256]{1,0:T(8,128)(2,1)S(1)} %copy-done.20, ...), kind=kOutput, calls=%fused_computation.32 | convolution fusion | flops 3260022784 | bytes 9961472 | tf_op jit(solution)/shard_map/dot_general | solution.py:326
  99.8 5.1 %fusion.11 = f32[512,1536]{1,0:T(8,128)} fusion(bf16[2048,512]{1,0:T(8,128)(2,1)S(1)} %bitcast.214, bf16[2048,512]{1,0:T(8,128)(2,1)S(1)} %bitcast.212, bf16[2048,512]{1,0:T(8,128)(2,1)S(1)} %fusion.5, bf16[2048,256]{1,0:T(8,128)(2,1)S(1)} %bitcast.209, bf16[2048,256]{1,0:T(8,128)(2,1)S(1)} %bitcast.206), kind=kOutput, calls=%fused_computation.39 | convolution fusion | flops 3244294144 | bytes 11534336 | tf_op jit(solution)/shard_map/dot_general | solution.py:17
  106.2 15.1 %all-to-all-start.1 = ((bf16[32,10,640]{2,1,0:T(8,128)(2,1)}), bf16[32,10,640]{2,1,0:T(8,128)(2,1)}, u32[]{:S(2)}, u32[]{:S(2)}) async-start(bf16[32,10,640]{2,1,0:T(8,128)(2,1)} %reshape.167), calls=%async_computation.1 | async-start | bytes 1310720 | tf_op jit(solution)/shard_map/all_to_all | solution.py:345
  125.8 3.5 %fusion.146 = f32[512,1536]{1,0:T(8,128)S(1)} fusion(bf16[2048,512]{1,0:T(8,128)(2,1)S(1)} %bitcast.224, bf16[2048,1536]{1,0:T(8,128)(2,1)S(1)} %pad_maximum_fusion.2), kind=kOutput, calls=%fused_computation.309 | convolution fusion | flops 3221225472 | bytes 11534336 | tf_op jit(solution)/shard_map/dot_general | solution.py:17
  131.0 3.4 %fusion.147 = f32[1536,512]{0,1:T(8,128)S(1)} fusion(bf16[2048,1536]{1,0:T(8,128)(2,1)S(1)} %pad_maximum_fusion.2, bf16[2048,512]{1,0:T(8,128)(2,1)S(1)} %bitcast.218), kind=kOutput, calls=%fused_computation.310 | convolution fusion | flops 3221225472 | bytes 11534336 | tf_op jit(solution)/shard_map/dot_general | solution.py:17
  136.9 2.4 collective-permute-start.10
  139.6 3.5 %fusion.148 = f32[512,1536]{1,0:T(8,128)S(1)} fusion(bf16[2048,512]{1,0:T(8,128)(2,1)S(1)} %bitcast.221, bf16[2048,1536]{1,0:T(8,128)(2,1)S(1)} %pad_maximum_fusion.2), kind=kOutput, calls=%fused_computation.311 | convolution fusion | flops 3221225472 | bytes 11534336 | tf_op jit(solution)/shard_map/dot_general | solution.py:17
  143.1 5.9 %collective-permute-done.10 = bf16[2,64,1536]{2,1,0:T(8,128)(2,1)S(1)} collective-permute-done((bf16[2,64,1536]{2,1,0:T(8,128)(2,1)S(1)}, bf16[2,64,1536]{2,1,0:T(8,128)(2,1)S(1)}, u32[]{:S(2)}, u32[]{:S(2)}) %collective-permute-start.10) | collective-permute-done | bytes 393248 | tf_op jit(solution)/shard_map/ppermute | solution.py:57
  149.0 2.8 %collective-permute-done.9 = bf16[2,64,1536]{2,1,0:T(8,128)(2,1)S(1)} collective-permute-done((bf16[2,64,1536]{2,1,0:T(8,128)(2,1)S(1)}, bf16[2,64,1536]{2,1,0:T(8,128)(2,1)S(1)}, u32[]{:S(2)}, u32[]{:S(2)}) %collective-permute-start.9) | collective-permute-done | bytes 393248 | tf_op jit(solution)/shard_map/ppermute | solution.py:57
  153.1 2.4 collective-permute-start.13
  156.1 2.4 collective-permute-done.13
  158.5 1.9 collective-permute-done.12
  161.0 1.9 collective-permute-start.15
  163.4 4.4 %collective-permute-start.24 = (bf16[2,256,1536]{2,1,0:T(8,128)(2,1)S(1)}, bf16[2,256,1536]{2,1,0:T(8,128)(2,1)}, u32[]{:S(2)}, u32[]{:S(2)}) collective-permute-start(bf16[2,256,1536]{2,1,0:T(8,128)(2,1)S(1)} %pad_maximum_fusion.12), channel_id=1, source_target_pairs={{0,2},{2,0},{1,3},{3,1},{4,6},{6,4},{5,7},{7,5},{8,10},{10,8},{9,1... | collective-permute-start | bytes 4718600 | tf_op jit(solution)/shard_map/ppermute | solution.py:29
  169.1 2.7 %collective-permute-start.17 = (bf16[2,16,768]{2,1,0:T(8,128)(2,1)}, bf16[2,16,768]{2,1,0:T(8,128)(2,1)}, u32[]{:S(2)}, u32[]{:S(2)}) collective-permute-start(bf16[2,16,768]{2,1,0:T(8,128)(2,1)} %add_convert_fusion.3), channel_id=1, source_target_pairs={{0,16},{1,17},{2,6},{3,7},{4,20},{5,21},{6,2},{7,3},{8,24},{9,25},... | collective-permute-start | bytes 147464 | tf_op jit(solution)/shard_map/ppermute | solution.py:57
  179.3 2.0 collective-permute-done.21
  181.2 2.0 collective-permute-done.22
  183.6 6.5 %collective-permute-start.23 = (bf16[2,256,768]{2,1,0:T(8,128)(2,1)S(1)}, bf16[2,256,768]{2,1,0:T(8,128)(2,1)S(1)}, u32[]{:S(2)}, u32[]{:S(2)}) collective-permute-start(bf16[2,256,768]{2,1,0:T(8,128)(2,1)S(1)} %pad_maximum_fusion.17), channel_id=1, source_target_pairs={{0,2},{2,0},{1,3},{3,1},{4,6},{6,4},{5,7},{7,5},{8,10},{10,8},{9,1... | collective-permute-start | bytes 2359304 | tf_op jit(solution)/shard_map/ppermute | solution.py:29
  190.1 1.9 maximum_add_fusion.1
  196.6 2.6 %collective-permute-done.25 = bf16[2,64,1536]{2,1,0:T(8,128)(2,1)S(1)} collective-permute-done((bf16[2,64,1536]{2,1,0:T(8,128)(2,1)S(1)}, bf16[2,64,1536]{2,1,0:T(8,128)(2,1)S(1)}, u32[]{:S(2)}, u32[]{:S(2)}) %collective-permute-start.25) | collective-permute-done | bytes 393248 | tf_op jit(solution)/shard_map/ppermute | solution.py:57
  199.2 5.1 %collective-permute-done.27 = bf16[2,64,1536]{2,1,0:T(8,128)(2,1)S(1)} collective-permute-done((bf16[2,64,1536]{2,1,0:T(8,128)(2,1)S(1)}, bf16[2,64,1536]{2,1,0:T(8,128)(2,1)S(1)}, u32[]{:S(2)}, u32[]{:S(2)}) %collective-permute-start.27) | collective-permute-done | bytes 393248 | tf_op jit(solution)/shard_map/ppermute | solution.py:57
  204.3 2.9 %collective-permute-done.26 = bf16[2,64,1536]{2,1,0:T(8,128)(2,1)S(1)} collective-permute-done((bf16[2,64,1536]{2,1,0:T(8,128)(2,1)S(1)}, bf16[2,64,1536]{2,1,0:T(8,128)(2,1)S(1)}, u32[]{:S(2)}, u32[]{:S(2)}) %collective-permute-start.26) | collective-permute-done | bytes 393248 | tf_op jit(solution)/shard_map/ppermute | solution.py:57
  209.1 2.2 collective-permute-start.29
  214.4 2.0 collective-permute-start.32
  217.0 2.4 collective-permute-done.31
  219.4 2.4 collective-permute-start.36
  223.9 2.3 collective-permute-done.35
  230.7 2.7 %collective-permute-done.38 = bf16[2,64,768]{2,1,0:T(8,128)(2,1)S(1)} collective-permute-done((bf16[2,64,768]{2,1,0:T(8,128)(2,1)S(1)}, bf16[2,64,768]{2,1,0:T(8,128)(2,1)S(1)}, u32[]{:S(2)}, u32[]{:S(2)}) %collective-permute-start.38) | collective-permute-done | bytes 196640 | tf_op jit(solution)/shard_map/ppermute | solution.py:57
  235.4 7.0 %collective-permute-start.40 = (bf16[2,256,768]{2,1,0:T(8,128)(2,1)S(1)}, bf16[2,256,768]{2,1,0:T(8,128)(2,1)S(1)}, u32[]{:S(2)}, u32[]{:S(2)}) collective-permute-start(bf16[2,256,768]{2,1,0:T(8,128)(2,1)S(1)} %pad_maximum_fusion.18), channel_id=1, source_target_pairs={{0,2},{2,0},{1,3},{3,1},{4,6},{6,4},{5,7},{7,5},{8,10},{10,8},{9,1... | collective-permute-start | bytes 2359304 | tf_op jit(solution)/shard_map/ppermute | solution.py:29
  245.7 2.6 %stack.156 = f32[9,512,256]{2,1,0:T(8,128)} convert(bf16[9,512,256]{2,1,0:T(8,128)(2,1)S(1)} %fusion.104) | non-fusion elementwise | flops 1179648 | bytes 7077888 | tf_op jit(solution)/shard_map/stack | solution.py:362
  (309 shorter events, 75.5 us)
Async XLA Ops:
  2.2 24.1 %collective-permute-start.2 = (bf16[256,768]{1,0:T(8,128)(2,1)S(1)}, bf16[256,768]{1,0:T(8,128)(2,1)}, u32[]{:S(2)}, u32[]{:S(2)}) collective-permute-start(bf16[256,768]{1,0:T(8,128)(2,1)S(1)} %pad_maximum_fusion.19), channel_id=1, source_target_pairs={{1,64},{64,1},{65,0},{0,65},{3,66},{66,3},{67,2},{2,67},{5,68},{68... | collective-permute-start | bytes 1179656 | tf_op jit(solution)/shard_map/ppermute | solution.py:29
  7.3 39.0 %collective-permute-start = (bf16[16,1,64,512]{3,2,1,0:T(8,128)(2,1)}, bf16[16,1,64,512]{3,2,1,0:T(8,128)(2,1)}, u32[]{:S(2)}, u32[]{:S(2)}) collective-permute-start(bf16[16,1,64,512]{3,2,1,0:T(8,128)(2,1)} %get-tuple-element.45), channel_id=1, source_target_pairs={{0,2},{2,4},{4,6},{6,8},{8,10},{10,12},{12,14},{14,16},{16,18},{18... | collective-permute-start | bytes 3145736 | tf_op jit(solution)/shard_map/ppermute | solution.py:166
  13.4 16.5 %copy-start.6 = (bf16[9,512,256]{2,1,0:T(8,128)(2,1)S(1)}, bf16[9,512,256]{2,1,0:T(8,128)(2,1)}, u32[]{:S(2)}) copy-start(bf16[9,512,256]{2,1,0:T(8,128)(2,1)} %param.10) | copy-start | bytes 7077892
  13.4 23.4 %all-to-all-start = ((bf16[32,10,640]{2,1,0:T(8,128)(2,1)}), bf16[32,10,640]{2,1,0:T(8,128)(2,1)S(1)}, u32[]{:S(2)}, u32[]{:S(2)}) async-start(bf16[32,10,640]{2,1,0:T(8,128)(2,1)} %reshape.155), calls=%async_computation | async-start | bytes 1310720 | tf_op jit(solution)/shard_map/all_to_all | solution.py:229
  21.3 27.0 %collective-permute-start.1 = (bf16[16,1,64,512]{3,2,1,0:T(8,128)(2,1)}, bf16[16,1,64,512]{3,2,1,0:T(8,128)(2,1)}, u32[]{:S(2)}, u32[]{:S(2)}) collective-permute-start(bf16[16,1,64,512]{3,2,1,0:T(8,128)(2,1)} %get-tuple-element.46), channel_id=1, source_target_pairs={{2,0},{4,2},{6,4},{8,6},{10,8},{12,10},{14,12},{16,14},{18,16},{20... | collective-permute-start | bytes 3145736 | tf_op jit(solution)/shard_map/ppermute | solution.py:167
  26.3 11.3 %collective-permute-start.5 = (bf16[256,768]{1,0:T(8,128)(2,1)}, bf16[256,768]{1,0:T(8,128)(2,1)}, u32[]{:S(2)}, u32[]{:S(2)}) collective-permute-start(bf16[256,768]{1,0:T(8,128)(2,1)} %collective-permute-done.2), channel_id=1, source_target_pairs={{0,1},{1,0},{64,65},{65,64},{2,3},{3,2},{66,67},{67,66},{4,5},{5,4... | collective-permute-start | bytes 1179656 | tf_op jit(solution)/shard_map/ppermute | solution.py:29
  26.3 15.6 %collective-permute-start.4 = (bf16[256,768]{1,0:T(8,128)(2,1)}, bf16[256,768]{1,0:T(8,128)(2,1)}, u32[]{:S(2)}, u32[]{:S(2)}) collective-permute-start(bf16[256,768]{1,0:T(8,128)(2,1)} %collective-permute-done.2), channel_id=1, source_target_pairs={{16,32},{32,16},{48,0},{0,48},{17,33},{33,17},{49,1},{1,49},{18,34... | collective-permute-start | bytes 1179656 | tf_op jit(solution)/shard_map/ppermute | solution.py:29
  29.1 12.7 %collective-permute-start.3 = (bf16[256,768]{1,0:T(8,128)(2,1)}, bf16[256,768]{1,0:T(8,128)(2,1)}, u32[]{:S(2)}, u32[]{:S(2)}) collective-permute-start(bf16[256,768]{1,0:T(8,128)(2,1)} %collective-permute-done.2), channel_id=1, source_target_pairs={{0,16},{16,0},{32,48},{48,32},{1,17},{17,1},{33,49},{49,33},{2,18}... | collective-permute-start | bytes 1179656 | tf_op jit(solution)/shard_map/ppermute | solution.py:29
  36.9 42.4 %copy-start.5 = (bf16[320,640]{1,0:T(8,128)(2,1)}, bf16[320,640]{1,0:T(8,128)(2,1)S(1)}, u32[]{:S(2)}) copy-start(bf16[320,640]{1,0:T(8,128)(2,1)S(1)} %reshape.156) | copy-start | bytes 1228804
  44.6 14.3 %collective-permute-start.6 = (bf16[4,256,768]{2,1,0:T(8,128)(2,1)}, bf16[4,256,768]{2,1,0:T(8,128)(2,1)S(1)}, u32[]{:S(2)}, u32[]{:S(2)}) collective-permute-start(bf16[4,256,768]{2,1,0:T(8,128)(2,1)} %get-tuple-element.56), channel_id=1, source_target_pairs={{0,2},{2,0},{1,3},{3,1},{4,6},{6,4},{5,7},{7,5},{8,10},{10,8},{9,1... | collective-permute-start | bytes 4718600 | tf_op jit(solution)/shard_map/ppermute | solution.py:29
  106.2 65.7 %all-to-all-start.1 = ((bf16[32,10,640]{2,1,0:T(8,128)(2,1)}), bf16[32,10,640]{2,1,0:T(8,128)(2,1)}, u32[]{:S(2)}, u32[]{:S(2)}) async-start(bf16[32,10,640]{2,1,0:T(8,128)(2,1)} %reshape.167), calls=%async_computation.1 | async-start | bytes 1310720 | tf_op jit(solution)/shard_map/all_to_all | solution.py:345
  129.6 5.1 %collective-permute-start.7 = (bf16[2,256,1536]{2,1,0:T(8,128)(2,1)S(1)}, bf16[2,256,1536]{2,1,0:T(8,128)(2,1)S(1)}, u32[]{:S(2)}, u32[]{:S(2)}) collective-permute-start(bf16[2,256,1536]{2,1,0:T(8,128)(2,1)S(1)} %pad_maximum_fusion.11), channel_id=1, source_target_pairs={{0,2},{2,0},{1,3},{3,1},{4,6},{6,4},{5,7},{7,5},{8,10},{10,8},{9,1... | collective-permute-start | bytes 4718600 | tf_op jit(solution)/shard_map/ppermute | solution.py:29
  135.4 7.7 %collective-permute-start.8 = (bf16[2,64,1536]{2,1,0:T(8,128)(2,1)S(1)}, bf16[2,64,1536]{2,1,0:T(8,128)(2,1)S(1)}, u32[]{:S(2)}, u32[]{:S(2)}) collective-permute-start(bf16[2,64,1536]{2,1,0:T(8,128)(2,1)S(1)} %get-tuple-element.25), channel_id=1, source_target_pairs={{0,4},{1,5},{2,18},{3,19},{4,0},{5,1},{6,22},{7,23},{8,12},{9,13},... | collective-permute-start | bytes 1179656 | tf_op jit(solution)/shard_map/ppermute | solution.py:57
  136.9 12.2 %collective-permute-start.10 = (bf16[2,64,1536]{2,1,0:T(8,128)(2,1)S(1)}, bf16[2,64,1536]{2,1,0:T(8,128)(2,1)S(1)}, u32[]{:S(2)}, u32[]{:S(2)}) collective-permute-start(bf16[2,64,1536]{2,1,0:T(8,128)(2,1)S(1)} %get-tuple-element.26), channel_id=1, source_target_pairs={{0,8},{1,9},{2,34},{3,35},{4,12},{5,13},{6,38},{7,39},{8,0},{9,1},... | collective-permute-start | bytes 1179656 | tf_op jit(solution)/shard_map/ppermute | solution.py:57
  139.3 12.5 %collective-permute-start.9 = (bf16[2,64,1536]{2,1,0:T(8,128)(2,1)S(1)}, bf16[2,64,1536]{2,1,0:T(8,128)(2,1)S(1)}, u32[]{:S(2)}, u32[]{:S(2)}) collective-permute-start(bf16[2,64,1536]{2,1,0:T(8,128)(2,1)S(1)} %get-tuple-element.27), channel_id=1, source_target_pairs={{0,12},{1,13},{2,50},{3,51},{4,8},{5,9},{6,54},{7,55},{8,4},{9,5},... | collective-permute-start | bytes 1179656 | tf_op jit(solution)/shard_map/ppermute | solution.py:57
  143.1 13.0 %copy-start.15 = (f32[512,1536]{1,0:T(8,128)}, f32[512,1536]{1,0:T(8,128)S(1)}, u32[]{:S(2)}) copy-start(f32[512,1536]{1,0:T(8,128)S(1)} %fusion.148) | copy-start | bytes 9437188
  152.1 4.0 %collective-permute-start.11 = (bf16[2,16,1536]{2,1,0:T(8,128)(2,1)S(1)}, bf16[2,16,1536]{2,1,0:T(8,128)(2,1)S(1)}, u32[]{:S(2)}, u32[]{:S(2)}) collective-permute-start(bf16[2,16,1536]{2,1,0:T(8,128)(2,1)S(1)} %get-tuple-element.71), channel_id=1, source_target_pairs={{0,16},{1,17},{2,6},{3,7},{4,20},{5,21},{6,2},{7,3},{8,24},{9,25},... | collective-permute-start | bytes 294920 | tf_op jit(solution)/shard_map/ppermute | solution.py:57
  153.1 5.5 %collective-permute-start.13 = (bf16[2,16,1536]{2,1,0:T(8,128)(2,1)S(1)}, bf16[2,16,1536]{2,1,0:T(8,128)(2,1)S(1)}, u32[]{:S(2)}, u32[]{:S(2)}) collective-permute-start(bf16[2,16,1536]{2,1,0:T(8,128)(2,1)S(1)} %get-tuple-element.72), channel_id=1, source_target_pairs={{0,32},{1,33},{2,10},{3,11},{4,36},{5,37},{6,14},{7,15},{8,40},{9,... | collective-permute-start | bytes 294920 | tf_op jit(solution)/shard_map/ppermute | solution.py:57
  155.5 5.0 %collective-permute-start.12 = (bf16[2,16,1536]{2,1,0:T(8,128)(2,1)S(1)}, bf16[2,16,1536]{2,1,0:T(8,128)(2,1)S(1)}, u32[]{:S(2)}, u32[]{:S(2)}) collective-permute-start(bf16[2,16,1536]{2,1,0:T(8,128)(2,1)S(1)} %get-tuple-element.73), channel_id=1, source_target_pairs={{0,48},{1,49},{2,14},{3,15},{4,52},{5,53},{6,10},{7,11},{8,56},{9,... | collective-permute-start | bytes 294920 | tf_op jit(solution)/shard_map/ppermute | solution.py:57
  160.5 7.3 %collective-permute-start.16 = (bf16[2,16,768]{2,1,0:T(8,128)(2,1)S(1)}, bf16[2,16,768]{2,1,0:T(8,128)(2,1)S(1)}, u32[]{:S(2)}, u32[]{:S(2)}) collective-permute-start(bf16[2,16,768]{2,1,0:T(8,128)(2,1)S(1)} %pad_maximum_fusion.24), channel_id=1, source_target_pairs={{0,64},{1,65},{2,66},{3,67},{4,68},{5,69},{6,70},{7,71},{8,72},{9,... | collective-permute-start | bytes 147464 | tf_op jit(solution)/shard_map/ppermute | solution.py:57
  161.0 6.9 %collective-permute-start.15 = (bf16[2,16,768]{2,1,0:T(8,128)(2,1)S(1)}, bf16[2,16,768]{2,1,0:T(8,128)(2,1)S(1)}, u32[]{:S(2)}, u32[]{:S(2)}) collective-permute-start(bf16[2,16,768]{2,1,0:T(8,128)(2,1)S(1)} %pad_maximum_fusion.24), channel_id=1, source_target_pairs={{0,65},{1,64},{2,67},{3,66},{4,69},{5,68},{6,71},{7,70},{8,73},{9,... | collective-permute-start | bytes 147464 | tf_op jit(solution)/shard_map/ppermute | solution.py:57
  162.9 5.0 %collective-permute-start.14 = (bf16[2,16,768]{2,1,0:T(8,128)(2,1)S(1)}, bf16[2,16,768]{2,1,0:T(8,128)(2,1)S(1)}, u32[]{:S(2)}, u32[]{:S(2)}) collective-permute-start(bf16[2,16,768]{2,1,0:T(8,128)(2,1)S(1)} %pad_maximum_fusion.23), channel_id=1, source_target_pairs={{0,1},{1,0},{2,3},{3,2},{4,5},{5,4},{6,7},{7,6},{8,9},{9,8},{10,11... | collective-permute-start | bytes 147464 | tf_op jit(solution)/shard_map/ppermute | solution.py:57
  163.4 26.7 %collective-permute-start.24 = (bf16[2,256,1536]{2,1,0:T(8,128)(2,1)S(1)}, bf16[2,256,1536]{2,1,0:T(8,128)(2,1)}, u32[]{:S(2)}, u32[]{:S(2)}) collective-permute-start(bf16[2,256,1536]{2,1,0:T(8,128)(2,1)S(1)} %pad_maximum_fusion.12), channel_id=1, source_target_pairs={{0,2},{2,0},{1,3},{3,1},{4,6},{6,4},{5,7},{7,5},{8,10},{10,8},{9,1... | collective-permute-start | bytes 4718600 | tf_op jit(solution)/shard_map/ppermute | solution.py:29
  168.5 4.6 %collective-permute-start.19 = (bf16[2,16,768]{2,1,0:T(8,128)(2,1)}, bf16[2,16,768]{2,1,0:T(8,128)(2,1)}, u32[]{:S(2)}, u32[]{:S(2)}) collective-permute-start(bf16[2,16,768]{2,1,0:T(8,128)(2,1)} %add_convert_fusion.3), channel_id=1, source_target_pairs={{0,48},{1,49},{2,14},{3,15},{4,52},{5,53},{6,10},{7,11},{8,56},{9,... | collective-permute-start | bytes 147464 | tf_op jit(solution)/shard_map/ppermute | solution.py:57
  168.8 4.8 %collective-permute-start.18 = (bf16[2,16,768]{2,1,0:T(8,128)(2,1)}, bf16[2,16,768]{2,1,0:T(8,128)(2,1)}, u32[]{:S(2)}, u32[]{:S(2)}) collective-permute-start(bf16[2,16,768]{2,1,0:T(8,128)(2,1)} %add_convert_fusion.3), channel_id=1, source_target_pairs={{0,32},{1,33},{2,10},{3,11},{4,36},{5,37},{6,14},{7,15},{8,40},{9,... | collective-permute-start | bytes 147464 | tf_op jit(solution)/shard_map/ppermute | solution.py:57
  169.1 5.0 %collective-permute-start.17 = (bf16[2,16,768]{2,1,0:T(8,128)(2,1)}, bf16[2,16,768]{2,1,0:T(8,128)(2,1)}, u32[]{:S(2)}, u32[]{:S(2)}) collective-permute-start(bf16[2,16,768]{2,1,0:T(8,128)(2,1)} %add_convert_fusion.3), channel_id=1, source_target_pairs={{0,16},{1,17},{2,6},{3,7},{4,20},{5,21},{6,2},{7,3},{8,24},{9,25},... | collective-permute-start | bytes 147464 | tf_op jit(solution)/shard_map/ppermute | solution.py:57
  175.0 6.2 %collective-permute-start.21 = (bf16[2,64,768]{2,1,0:T(8,128)(2,1)S(1)}, bf16[2,64,768]{2,1,0:T(8,128)(2,1)S(1)}, u32[]{:S(2)}, u32[]{:S(2)}) collective-permute-start(bf16[2,64,768]{2,1,0:T(8,128)(2,1)S(1)} %pad_maximum_fusion.20), channel_id=1, source_target_pairs={{0,8},{1,9},{2,34},{3,35},{4,12},{5,13},{6,38},{7,39},{8,0},{9,1},... | collective-permute-start | bytes 589832 | tf_op jit(solution)/shard_map/ppermute | solution.py:57
  175.4 7.8 %collective-permute-start.22 = (bf16[2,64,768]{2,1,0:T(8,128)(2,1)S(1)}, bf16[2,64,768]{2,1,0:T(8,128)(2,1)S(1)}, u32[]{:S(2)}, u32[]{:S(2)}) collective-permute-start(bf16[2,64,768]{2,1,0:T(8,128)(2,1)S(1)} %pad_maximum_fusion.20), channel_id=1, source_target_pairs={{0,12},{1,13},{2,50},{3,51},{4,8},{5,9},{6,54},{7,55},{8,4},{9,5},... | collective-permute-start | bytes 589832 | tf_op jit(solution)/shard_map/ppermute | solution.py:57
  176.4 6.9 %collective-permute-start.20 = (bf16[2,64,768]{2,1,0:T(8,128)(2,1)S(1)}, bf16[2,64,768]{2,1,0:T(8,128)(2,1)S(1)}, u32[]{:S(2)}, u32[]{:S(2)}) collective-permute-start(bf16[2,64,768]{2,1,0:T(8,128)(2,1)S(1)} %pad_maximum_fusion.20), channel_id=1, source_target_pairs={{0,4},{1,5},{2,18},{3,19},{4,0},{5,1},{6,22},{7,23},{8,12},{9,13},... | collective-permute-start | bytes 589832 | tf_op jit(solution)/shard_map/ppermute | solution.py:57
  183.6 12.5 %collective-permute-start.23 = (bf16[2,256,768]{2,1,0:T(8,128)(2,1)S(1)}, bf16[2,256,768]{2,1,0:T(8,128)(2,1)S(1)}, u32[]{:S(2)}, u32[]{:S(2)}) collective-permute-start(bf16[2,256,768]{2,1,0:T(8,128)(2,1)S(1)} %pad_maximum_fusion.17), channel_id=1, source_target_pairs={{0,2},{2,0},{1,3},{3,1},{4,6},{6,4},{5,7},{7,5},{8,10},{10,8},{9,1... | collective-permute-start | bytes 2359304 | tf_op jit(solution)/shard_map/ppermute | solution.py:29
  192.2 7.0 %collective-permute-start.25 = (bf16[2,64,1536]{2,1,0:T(8,128)(2,1)S(1)}, bf16[2,64,1536]{2,1,0:T(8,128)(2,1)S(1)}, u32[]{:S(2)}, u32[]{:S(2)}) collective-permute-start(bf16[2,64,1536]{2,1,0:T(8,128)(2,1)S(1)} %get-tuple-element.22), channel_id=1, source_target_pairs={{0,4},{1,5},{2,18},{3,19},{4,0},{5,1},{6,22},{7,23},{8,12},{9,13},... | collective-permute-start | bytes 1179656 | tf_op jit(solution)/shard_map/ppermute | solution.py:57
  193.1 11.1 %collective-permute-start.27 = (bf16[2,64,1536]{2,1,0:T(8,128)(2,1)S(1)}, bf16[2,64,1536]{2,1,0:T(8,128)(2,1)S(1)}, u32[]{:S(2)}, u32[]{:S(2)}) collective-permute-start(bf16[2,64,1536]{2,1,0:T(8,128)(2,1)S(1)} %get-tuple-element.23), channel_id=1, source_target_pairs={{0,8},{1,9},{2,34},{3,35},{4,12},{5,13},{6,38},{7,39},{8,0},{9,1},... | collective-permute-start | bytes 1179656 | tf_op jit(solution)/shard_map/ppermute | solution.py:57
  194.8 12.3 %collective-permute-start.26 = (bf16[2,64,1536]{2,1,0:T(8,128)(2,1)S(1)}, bf16[2,64,1536]{2,1,0:T(8,128)(2,1)S(1)}, u32[]{:S(2)}, u32[]{:S(2)}) collective-permute-start(bf16[2,64,1536]{2,1,0:T(8,128)(2,1)S(1)} %get-tuple-element.24), channel_id=1, source_target_pairs={{0,12},{1,13},{2,50},{3,51},{4,8},{5,9},{6,54},{7,55},{8,4},{9,5},... | collective-permute-start | bytes 1179656 | tf_op jit(solution)/shard_map/ppermute | solution.py:57
  196.6 26.4 %copy-start.58 = (s32[128]{0:T(128)S(1)}, s32[128]{0:T(128)}, u32[]{:S(2)}) copy-start(s32[128]{0:T(128)} %copy-done.57) | copy-start | bytes 1540
  207.4 4.0 %collective-permute-start.28 = (bf16[2,16,1536]{2,1,0:T(8,128)(2,1)S(1)}, bf16[2,16,1536]{2,1,0:T(8,128)(2,1)S(1)}, u32[]{:S(2)}, u32[]{:S(2)}) collective-permute-start(bf16[2,16,1536]{2,1,0:T(8,128)(2,1)S(1)} %get-tuple-element.64), channel_id=1, source_target_pairs={{0,16},{1,17},{2,6},{3,7},{4,20},{5,21},{6,2},{7,3},{8,24},{9,25},... | collective-permute-start | bytes 294920 | tf_op jit(solution)/shard_map/ppermute | solution.py:57
  207.5 5.1 %collective-permute-start.30 = (bf16[2,16,1536]{2,1,0:T(8,128)(2,1)S(1)}, bf16[2,16,1536]{2,1,0:T(8,128)(2,1)S(1)}, u32[]{:S(2)}, u32[]{:S(2)}) collective-permute-start(bf16[2,16,1536]{2,1,0:T(8,128)(2,1)S(1)} %get-tuple-element.65), channel_id=1, source_target_pairs={{0,32},{1,33},{2,10},{3,11},{4,36},{5,37},{6,14},{7,15},{8,40},{9,... | collective-permute-start | bytes 294920 | tf_op jit(solution)/shard_map/ppermute | solution.py:57
  209.1 5.0 %collective-permute-start.29 = (bf16[2,16,1536]{2,1,0:T(8,128)(2,1)S(1)}, bf16[2,16,1536]{2,1,0:T(8,128)(2,1)S(1)}, u32[]{:S(2)}, u32[]{:S(2)}) collective-permute-start(bf16[2,16,1536]{2,1,0:T(8,128)(2,1)S(1)} %get-tuple-element.66), channel_id=1, source_target_pairs={{0,48},{1,49},{2,14},{3,15},{4,52},{5,53},{6,10},{7,11},{8,56},{9,... | collective-permute-start | bytes 294920 | tf_op jit(solution)/shard_map/ppermute | solution.py:57
  214.2 5.2 %collective-permute-start.33 = (bf16[2,16,768]{2,1,0:T(8,128)(2,1)S(1)}, bf16[2,16,768]{2,1,0:T(8,128)(2,1)S(1)}, u32[]{:S(2)}, u32[]{:S(2)}) collective-permute-start(bf16[2,16,768]{2,1,0:T(8,128)(2,1)S(1)} %pad_maximum_fusion.26), channel_id=1, source_target_pairs={{0,64},{1,65},{2,66},{3,67},{4,68},{5,69},{6,70},{7,71},{8,72},{9,... | collective-permute-start | bytes 147464 | tf_op jit(solution)/shard_map/ppermute | solution.py:57
  214.4 4.9 %collective-permute-start.32 = (bf16[2,16,768]{2,1,0:T(8,128)(2,1)S(1)}, bf16[2,16,768]{2,1,0:T(8,128)(2,1)S(1)}, u32[]{:S(2)}, u32[]{:S(2)}) collective-permute-start(bf16[2,16,768]{2,1,0:T(8,128)(2,1)S(1)} %pad_maximum_fusion.26), channel_id=1, source_target_pairs={{0,65},{1,64},{2,67},{3,66},{4,69},{5,68},{6,71},{7,70},{8,73},{9,... | collective-permute-start | bytes 147464 | tf_op jit(solution)/shard_map/ppermute | solution.py:57
  216.4 2.9 %collective-permute-start.31 = (bf16[2,16,768]{2,1,0:T(8,128)(2,1)S(1)}, bf16[2,16,768]{2,1,0:T(8,128)(2,1)S(1)}, u32[]{:S(2)}, u32[]{:S(2)}) collective-permute-start(bf16[2,16,768]{2,1,0:T(8,128)(2,1)S(1)} %pad_maximum_fusion.25), channel_id=1, source_target_pairs={{0,1},{1,0},{2,3},{3,2},{4,5},{5,4},{6,7},{7,6},{8,9},{9,8},{10,11... | collective-permute-start | bytes 147464 | tf_op jit(solution)/shard_map/ppermute | solution.py:57
  219.4 4.5 %collective-permute-start.36 = (bf16[2,16,768]{2,1,0:T(8,128)(2,1)S(1)}, bf16[2,16,768]{2,1,0:T(8,128)(2,1)S(1)}, u32[]{:S(2)}, u32[]{:S(2)}) collective-permute-start(bf16[2,16,768]{2,1,0:T(8,128)(2,1)S(1)} %add_convert_fusion.2), channel_id=1, source_target_pairs={{0,48},{1,49},{2,14},{3,15},{4,52},{5,53},{6,10},{7,11},{8,56},{9,... | collective-permute-start | bytes 147464 | tf_op jit(solution)/shard_map/ppermute | solution.py:57
  221.8 4.4 %collective-permute-start.35 = (bf16[2,16,768]{2,1,0:T(8,128)(2,1)S(1)}, bf16[2,16,768]{2,1,0:T(8,128)(2,1)S(1)}, u32[]{:S(2)}, u32[]{:S(2)}) collective-permute-start(bf16[2,16,768]{2,1,0:T(8,128)(2,1)S(1)} %add_convert_fusion.2), channel_id=1, source_target_pairs={{0,32},{1,33},{2,10},{3,11},{4,36},{5,37},{6,14},{7,15},{8,40},{9,... | collective-permute-start | bytes 147464 | tf_op jit(solution)/shard_map/ppermute | solution.py:57
  222.1 4.2 %collective-permute-start.34 = (bf16[2,16,768]{2,1,0:T(8,128)(2,1)S(1)}, bf16[2,16,768]{2,1,0:T(8,128)(2,1)S(1)}, u32[]{:S(2)}, u32[]{:S(2)}) collective-permute-start(bf16[2,16,768]{2,1,0:T(8,128)(2,1)S(1)} %add_convert_fusion.2), channel_id=1, source_target_pairs={{0,16},{1,17},{2,6},{3,7},{4,20},{5,21},{6,2},{7,3},{8,24},{9,25},... | collective-permute-start | bytes 147464 | tf_op jit(solution)/shard_map/ppermute | solution.py:57
  226.3 7.1 %collective-permute-start.38 = (bf16[2,64,768]{2,1,0:T(8,128)(2,1)S(1)}, bf16[2,64,768]{2,1,0:T(8,128)(2,1)S(1)}, u32[]{:S(2)}, u32[]{:S(2)}) collective-permute-start(bf16[2,64,768]{2,1,0:T(8,128)(2,1)S(1)} %pad_maximum_fusion.21), channel_id=1, source_target_pairs={{0,8},{1,9},{2,34},{3,35},{4,12},{5,13},{6,38},{7,39},{8,0},{9,1},... | collective-permute-start | bytes 589832 | tf_op jit(solution)/shard_map/ppermute | solution.py:57
  226.9 8.1 %collective-permute-start.39 = (bf16[2,64,768]{2,1,0:T(8,128)(2,1)S(1)}, bf16[2,64,768]{2,1,0:T(8,128)(2,1)S(1)}, u32[]{:S(2)}, u32[]{:S(2)}) collective-permute-start(bf16[2,64,768]{2,1,0:T(8,128)(2,1)S(1)} %pad_maximum_fusion.21), channel_id=1, source_target_pairs={{0,12},{1,13},{2,50},{3,51},{4,8},{5,9},{6,54},{7,55},{8,4},{9,5},... | collective-permute-start | bytes 589832 | tf_op jit(solution)/shard_map/ppermute | solution.py:57
  228.0 7.0 %collective-permute-start.37 = (bf16[2,64,768]{2,1,0:T(8,128)(2,1)S(1)}, bf16[2,64,768]{2,1,0:T(8,128)(2,1)S(1)}, u32[]{:S(2)}, u32[]{:S(2)}) collective-permute-start(bf16[2,64,768]{2,1,0:T(8,128)(2,1)S(1)} %pad_maximum_fusion.21), channel_id=1, source_target_pairs={{0,4},{1,5},{2,18},{3,19},{4,0},{5,1},{6,22},{7,23},{8,12},{9,13},... | collective-permute-start | bytes 589832 | tf_op jit(solution)/shard_map/ppermute | solution.py:57
  229.1 14.6 %collective-permute-start.41 = (bf16[128,640]{1,0:T(8,128)(2,1)S(1)}, bf16[128,640]{1,0:T(8,128)(2,1)S(1)}, u32[]{:S(2)}, u32[]{:S(2)}) collective-permute-start(bf16[128,640]{1,0:T(8,128)(2,1)S(1)} %pad_maximum_fusion.22), channel_id=1, source_target_pairs={{0,64},{64,0},{1,65},{65,1},{2,66},{66,2},{3,67},{67,3},{4,68},{68... | collective-permute-start | bytes 491528 | tf_op jit(solution)/shard_map/ppermute | solution.py:351
  235.4 9.7 %collective-permute-start.40 = (bf16[2,256,768]{2,1,0:T(8,128)(2,1)S(1)}, bf16[2,256,768]{2,1,0:T(8,128)(2,1)S(1)}, u32[]{:S(2)}, u32[]{:S(2)}) collective-permute-start(bf16[2,256,768]{2,1,0:T(8,128)(2,1)S(1)} %pad_maximum_fusion.18), channel_id=1, source_target_pairs={{0,2},{2,0},{1,3},{3,1},{4,6},{6,4},{5,7},{7,5},{8,10},{10,8},{9,1... | collective-permute-start | bytes 2359304 | tf_op jit(solution)/shard_map/ppermute | solution.py:29
  (60 other events, 194.4 us)

commit v3 on v2

--- a/solution.py
+++ b/solution.py
@@ -123,8 +123,11 @@
     return kept + swap(sent.astype(BF), "core", 0).astype(F32)
 
 
+def reduce_rows(value):
+    return quarter(value, ("x", "z"))
+
+
 def reduce_middle(value):
-    value = quarter(value, ("x", "z"))
     value = quarter(value, ("z", "x"))
     return sum_columns(value).astype(BF)
 
@@ -339,18 +342,16 @@
     first_part, wider = lax.optimization_barrier((first_part, wider))
     grad_2 = contract_rows(shifted_rows[2], wider)
     second_part = reduce_first((grad_1, grad_2), (0, 0))
-    middle_1 = reduce_middle(first_part)
-    middle_2 = reduce_middle(second_part)
+    middle = reduce_middle(jnp.concatenate([reduce_rows(first_part), reduce_rows(second_part)]))
 
     returned = lax.all_to_all(
         back.reshape(tile_count, capacity, PACK), TILE, split_axis=0, concat_axis=0, tiled=True
     ).reshape(slot_count, PACK)
-    returned, middle_2 = lax.optimization_barrier((returned, middle_2))
+    returned, middle = lax.optimization_barrier((returned, middle))
     mine = contract_rows(selector, returned)
     mine = jnp.concatenate([local(mine[:, :channels]), mine[:, channels:]], axis=1).astype(BF)
     other = lax.ppermute(mine, "fsdp", [(0, 1), (1, 0)])
-    total_1 = reduce_last(middle_1)
-    total_2 = reduce_last(middle_2)
+    total = reduce_last(middle)
     summed = mine.astype(F32) + other.astype(F32)
     weight_grad = summed[:, :channels]
     bias_grad = summed[:, channels]
@@ -358,8 +359,8 @@
     def taps(value):
         return [value[:, b * half : (b + 1) * half].astype(F32) for b in range(3)]
 
-    total_temporal = jnp.stack(taps(total_1[0]))
-    total_spatial = jnp.stack(taps(total_1[1]) + taps(total_2[0]) + taps(total_2[1]))
+    total_temporal = jnp.stack(taps(total[0]))
+    total_spatial = jnp.stack(taps(total[1]) + taps(total[2]) + taps(total[3]))
     return (total_spatial, total_temporal, weight_grad[None], bias_grad[None])
 
 

time: 253 us -> 227 us (0.90)
  starting transfers between devices: 90.7 us -> 61.6 us
  waiting for transfers between devices: 51.4 us -> 54.8 us
    ppermute x9 -> x8, starting transfers between devices: 26.3 us -> 10.7 us  [swap(): return lax.ppermute(value, name, perm)]
    ppermute x30 -> x18, waiting for transfers between devices: 41 us -> 27.8 us  [permute_by_core(): return lax.ppermute(value, ALL, perm)]
    all_to_all x1, waiting for transfers between devices: 0.01 us -> 8.63 us  [compute(): lax.all_to_all(back.reshape(tile_count, capacity, PACK), TILE, split_axis...]
    ppermute x1, waiting for transfers between devices: 0.01 us -> 7.09 us  [compute(): other = lax.ppermute(mine, 'fsdp', [(0, 1), (1, 0)])]
    all_to_all x1, starting transfers between devices: 15.1 us -> 8.2 us  [compute(): lax.all_to_all(back.reshape(tile_count, capacity, PACK), TILE, split_axis...]
    ppermute x30 -> x18, starting transfers between devices: 33.7 us -> 28.6 us  [permute_by_core(): return lax.ppermute(value, ALL, perm)]
    unnamed x138 -> x124, local copies, waits for them, and re-layouts: 9.04 us -> 12.5 us
  transfers between devices with their start and end apart: 44 -> 31, of which waited for: 21 -> 12; matrix products, arithmetic and copies ran while one was open for 20% -> 17% of each run, Pallas kernels for 0% -> 0%
where the time goes in v3:
time: 227 us; the launch traced here: 223 us
  starting transfers between devices  61.6 us (27%)
  waiting for transfers between devices  54.8 us (24%)
  matrix products  40.9 us (18%)
  local copies, waits for them, and re-layouts  32.3 us (14%)
  other arithmetic  31.1 us (14%)
  between operations  2.45 us (1%)
    ppermute x18, starting transfers between devices, permute_by_core(): return lax.ppermute(value, ALL, perm)  28.6 us
    ppermute x18, waiting for transfers between devices, permute_by_core(): return lax.ppermute(value, ALL, perm)  27.8 us
    dot_general x6, matrix products, contract_rows(): lax.dot_general(left, right, (((0,), (0,)), ((), ())), preferred_element_...  16.6 us
    unnamed x124, local copies, waits for them, and re-layouts  12.5 us
    ppermute x8, starting transfers between devices, swap(): return lax.ppermute(value, name, perm)  10.7 us
    dot_general x2, matrix products, convolve(): sums = jnp.dot(taller, weights, preferred_element_type=F32)  10.2 us
    all_to_all x1, waiting for transfers between devices, compute(): lax.all_to_all(back.reshape(tile_count, capacity, PACK), TILE, split_axis...  8.63 us
    all_to_all x1, starting transfers between devices, compute(): lax.all_to_all(back.reshape(tile_count, capacity, PACK), TILE, split_axis...  8.2 us
  transfers between devices with their start and end apart: 31, of which 12 were waited for; matrix products, arithmetic and copies ran while one was open for 17% of the time, Pallas kernels for 0%

profile of v3, /device:TPU:1, one launch (start us, length us, event | category | flops | bytes accessed | tf_op | source)
XLA Modules:
  0.0 223.1 jit_solution(2878449955330358879)
XLA Ops:
  2.2 3.6 %collective-permute-start.2 = (bf16[256,768]{1,0:T(8,128)(2,1)S(1)}, bf16[256,768]{1,0:T(8,128)(2,1)}, u32[]{:S(2)}, u32[]{:S(2)}) collective-permute-start(bf16[256,768]{1,0:T(8,128)(2,1)S(1)} %pad_maximum_fusion.17), channel_id=1, source_target_pairs={{1,64},{64,1},{65,0},{0,65},{3,66},{66,3},{67,2},{2,67},{5,68},{68... | collective-permute-start | bytes 1179656 | tf_op jit(solution)/shard_map/ppermute | solution.py:29
  5.8 1.5 fusion.149
  7.3 3.9 %collective-permute-start = (bf16[16,1,64,512]{3,2,1,0:T(8,128)(2,1)}, bf16[16,1,64,512]{3,2,1,0:T(8,128)(2,1)}, u32[]{:S(2)}, u32[]{:S(2)}) collective-permute-start(bf16[16,1,64,512]{3,2,1,0:T(8,128)(2,1)} %get-tuple-element.51), channel_id=1, source_target_pairs={{0,2},{2,4},{4,6},{6,8},{8,10},{10,12},{12,14},{14,16},{16,18},{18... | collective-permute-start | bytes 3145736 | tf_op jit(solution)/shard_map/ppermute | solution.py:169
  13.4 7.9 %all-to-all-start = ((bf16[32,10,640]{2,1,0:T(8,128)(2,1)}), bf16[32,10,640]{2,1,0:T(8,128)(2,1)S(1)}, u32[]{:S(2)}, u32[]{:S(2)}) async-start(bf16[32,10,640]{2,1,0:T(8,128)(2,1)} %reshape.154), calls=%async_computation | async-start | bytes 1310720 | tf_op jit(solution)/shard_map/all_to_all | solution.py:232
  21.3 2.1 collective-permute-start.1
  25.5 2.8 %collective-permute-start.4 = (bf16[256,768]{1,0:T(8,128)(2,1)}, bf16[256,768]{1,0:T(8,128)(2,1)}, u32[]{:S(2)}, u32[]{:S(2)}) collective-permute-start(bf16[256,768]{1,0:T(8,128)(2,1)} %collective-permute-done.2), channel_id=1, source_target_pairs={{16,32},{32,16},{48,0},{0,48},{17,33},{33,17},{49,1},{1,49},{18,34... | collective-permute-start | bytes 1179656 | tf_op jit(solution)/shard_map/ppermute | solution.py:29
  30.5 6.3 %all-to-all-done = bf16[32,10,640]{2,1,0:T(8,128)(2,1)S(1)} async-done(((bf16[32,10,640]{2,1,0:T(8,128)(2,1)}), bf16[32,10,640]{2,1,0:T(8,128)(2,1)S(1)}, u32[]{:S(2)}, u32[]{:S(2)}) %all-to-all-start) | async-done | bytes 409632 | tf_op jit(solution)/shard_map/all_to_all | solution.py:232
  36.9 5.0 %collective-permute-done.4 = bf16[256,768]{1,0:T(8,128)(2,1)} collective-permute-done((bf16[256,768]{1,0:T(8,128)(2,1)}, bf16[256,768]{1,0:T(8,128)(2,1)}, u32[]{:S(2)}, u32[]{:S(2)}) %collective-permute-start.4) | collective-permute-done | bytes 393248 | tf_op jit(solution)/shard_map/ppermute | solution.py:29
  41.9 2.7 %fusion.143 = (bf16[1,4,256,768]{3,2,1,0:T(8,128)(2,1)S(1)}, bf16[4,256,768]{2,1,0:T(8,128)(2,1)}) fusion(bf16[1,256,768]{2,1,0:T(8,128)(2,1)} %bitcast.10, bf16[1,256,768]{2,1,0:T(8,128)(2,1)} %bitcast.9, bf16[1,256,768]{2,1,0:T(8,128)(2,1)} %bitcast.8, bf16[1,256,768]{2,1,0:T(8,128)(2,1)} %bitcast.7), kind=kLoop, calls=%fused_computation.293 | loop fusion | flops 2359296 | bytes 4718592 | tf_op jit(solution)/shard_map/stack | solution.py:154
  46.1 1.8 pad_maximum_fusion.7
  48.0 2.6 %pad_maximum_fusion.8 = bf16[16,2,64,512]{3,2,1,0:T(8,128)(2,1)S(1)} fusion(bf16[16,1,64,512]{3,2,1,0:T(8,128)(2,1)} %collective-permute-done.1, bf16[16,1,64,512]{3,2,1,0:T(8,128)(2,1)} %get-tuple-element.51), kind=kLoop, calls=%fused_computation.81 | loop fusion | flops 1048576 | bytes 4194304 | tf_op jit(solution)/shard_map/concatenate | solution.py:242
  51.4 5.1 %fusion.9 = f32[2048,768]{1,0:T(8,128)S(1)} fusion(bf16[2048,512]{1,0:T(8,128)(2,1)S(1)} %bitcast.219, bf16[2048,512]{1,0:T(8,128)(2,1)S(1)} %bitcast.216, bf16[2048,512]{1,0:T(8,128)(2,1)S(1)} %bitcast.222, bf16[512,256]{1,0:T(8,128)(2,1)S(1)} %copy-done.36, bf16[512,256]{1,0:T(8,128)(2,1)S(1)} %copy-done.37, bf16[512,256]{1,0:T(8,128)(2,1)S(1)} %copy-done.30, ...), kind=kOutput, calls=%fused_computation.43 | convolution fusion | flops 4871946240 | bytes 14942208 | tf_op jit(solution)/shard_map/dot_general | solution.py:247
  57.1 1.5 fusion.31
  61.1 5.1 %fusion.10 = f32[2048,768]{1,0:T(8,128)S(1)} fusion(bf16[1536,768]{1,0:T(8,128)(2,1)S(1)} %bitcast_dynamic-update-slice_fusion, bf16[2048,512]{1,0:T(8,128)(2,1)S(1)} %bitcast.220, bf16[2048,512]{1,0:T(8,128)(2,1)S(1)} %bitcast.217, bf16[2048,512]{1,0:T(8,128)(2,1)S(1)} %bitcast.223), kind=kOutput, calls=%fused_computation.44 | convolution fusion | flops 4850712576 | bytes 14942208 | tf_op jit(solution)/shard_map/dot_general | solution.py:247
  66.8 2.0 fusion.33
  71.2 1.8 fusion.12
  79.0 2.0 convolution_bitcast_fusion
  82.8 3.1 %broadcast_select_fusion.2 = (bf16[320,16,128]{2,1,0:T(8,128)(2,1)S(1)}, bf16[320,16,128]{2,1,0:T(8,128)(2,1)S(1)}) fusion(pred[320,128]{1,0:T(8,128)(4,1)} %copy-done.28, bf16[320,16]{1,0:T(8,128)(2,1)S(1)} %copy.38, bf16[320,16]{1,0:T(8,128)(2,1)S(1)} %copy.36), kind=kLoop, calls=%fused_computation.124 | loop fusion | flops 1310720 | bytes 2682880 | tf_op jit(solution)/shard_map/jit(_where)/select_n | solution.py:306
  86.9 1.6 copy-done.1
  88.6 2.3 %fusion.5 = bf16[2048,512]{1,0:T(8,128)(2,1)S(1)} fusion(f32[2048,512]{1,0:T(8,128)S(1)} %copy-done.1, bf16[320,2048]{1,0:T(8,128)(2,1)S(1)} %bitcast.225, bf16[320,2048]{1,0:T(8,128)(2,1)S(1)} %bitcast.226, bf16[320,512]{1,0:T(8,128)(2,1)S(1)} %slice-done), kind=kOutput, calls=%fused_computation.28 | convolution fusion | flops 1353973760 | bytes 9240576 | tf_op jit(solution)/shard_map/dot_general | solution.py:17
  92.1 3.5 %convolution_convert_fusion = bf16[2048,512]{1,0:T(8,128)(2,1)S(1)} fusion(bf16[2048,512]{1,0:T(8,128)(2,1)S(1)} %bitcast.213, bf16[2048,512]{1,0:T(8,128)(2,1)S(1)} %bitcast.211, bf16[2048,512]{1,0:T(8,128)(2,1)S(1)} %fusion.5, bf16[256,256]{1,0:T(8,128)(2,1)S(1)} %get-tuple-element.103, bf16[256,256]{1,0:T(8,128)(2,1)S(1)} %copy-done.22, ...), kind=kOutput, calls=%fused_computation.38 | convolution fusion | flops 3260022784 | bytes 9961472 | tf_op jit(solution)/shard_map/dot_general | solution.py:329
  95.6 3.5 %fusion.11 = f32[512,1536]{1,0:T(8,128)S(1)} fusion(bf16[2048,512]{1,0:T(8,128)(2,1)S(1)} %bitcast.214, bf16[2048,512]{1,0:T(8,128)(2,1)S(1)} %bitcast.212, bf16[2048,512]{1,0:T(8,128)(2,1)S(1)} %fusion.5, bf16[2048,256]{1,0:T(8,128)(2,1)S(1)} %bitcast.209, bf16[2048,256]{1,0:T(8,128)(2,1)S(1)} %bitcast.206), kind=kOutput, calls=%fused_computation.45 | convolution fusion | flops 3244294144 | bytes 11534336 | tf_op jit(solution)/shard_map/dot_general | solution.py:17
  103.6 3.5 %fusion.156 = f32[512,1536]{1,0:T(8,128)S(1)} fusion(bf16[2048,512]{1,0:T(8,128)(2,1)S(1)} %bitcast.224, bf16[2048,1536]{1,0:T(8,128)(2,1)S(1)} %pad_maximum_fusion.2), kind=kOutput, calls=%fused_computation.305 | convolution fusion | flops 3221225472 | bytes 11534336 | tf_op jit(solution)/shard_map/dot_general | solution.py:17
  108.7 3.5 %fusion.157 = f32[1536,512]{0,1:T(8,128)S(1)} fusion(bf16[2048,1536]{1,0:T(8,128)(2,1)S(1)} %pad_maximum_fusion.2, bf16[2048,512]{1,0:T(8,128)(2,1)S(1)} %bitcast.218), kind=kOutput, calls=%fused_computation.306 | convolution fusion | flops 3221225472 | bytes 11534336 | tf_op jit(solution)/shard_map/dot_general | solution.py:17
  112.4 1.5 copy-done.20
  115.7 3.6 %fusion.158 = f32[512,1536]{1,0:T(8,128)S(1)} fusion(bf16[2048,512]{1,0:T(8,128)(2,1)S(1)} %bitcast.221, bf16[2048,1536]{1,0:T(8,128)(2,1)S(1)} %pad_maximum_fusion.2), kind=kOutput, calls=%fused_computation.307 | convolution fusion | flops 3221225472 | bytes 11534336 | tf_op jit(solution)/shard_map/dot_general | solution.py:17
  119.4 1.5 pad_maximum_fusion.12
  121.9 1.6 dynamic-slice_bitcast_fusion.1
  123.6 4.3 %convolution_convert_fusion.2 = bf16[320,512]{1,0:T(8,128)(2,1)S(1)} fusion(bf16[40,8,16,128]{3,2,1,0:T(8,128)(2,1)S(1)} %bitcast.202, f32[2048,512]{1,0:T(8,128)} %copy-done), kind=kOutput, calls=%fused_computation.127 | convolution fusion | flops 675446784 | bytes 5832704 | tf_op jit(solution)/shard_map/dot_general | solution.py:321
  128.9 3.3 %collective-permute-start.10 = (bf16[2,64,1536]{2,1,0:T(8,128)(2,1)S(1)}, bf16[2,64,1536]{2,1,0:T(8,128)(2,1)S(1)}, u32[]{:S(2)}, u32[]{:S(2)}) collective-permute-start(bf16[2,64,1536]{2,1,0:T(8,128)(2,1)S(1)} %get-tuple-element.32), channel_id=1, source_target_pairs={{0,8},{1,9},{2,34},{3,35},{4,12},{5,13},{6,38},{7,39},{8,0},{9,1},... | collective-permute-start | bytes 1179656 | tf_op jit(solution)/shard_map/ppermute | solution.py:57
  132.3 1.9 maximum_add_fusion.1
  134.5 3.8 %collective-permute-start.14 = (bf16[2,64,1536]{2,1,0:T(8,128)(2,1)S(1)}, bf16[2,64,1536]{2,1,0:T(8,128)(2,1)S(1)}, u32[]{:S(2)}, u32[]{:S(2)}) collective-permute-start(bf16[2,64,1536]{2,1,0:T(8,128)(2,1)S(1)} %get-tuple-element.29), channel_id=1, source_target_pairs={{0,8},{1,9},{2,34},{3,35},{4,12},{5,13},{6,38},{7,39},{8,0},{9,1},... | collective-permute-start | bytes 1179656 | tf_op jit(solution)/shard_map/ppermute | solution.py:57
  138.3 3.3 %collective-permute-done.10 = bf16[2,64,1536]{2,1,0:T(8,128)(2,1)S(1)} collective-permute-done((bf16[2,64,1536]{2,1,0:T(8,128)(2,1)S(1)}, bf16[2,64,1536]{2,1,0:T(8,128)(2,1)S(1)}, u32[]{:S(2)}, u32[]{:S(2)}) %collective-permute-start.10) | collective-permute-done | bytes 393248 | tf_op jit(solution)/shard_map/ppermute | solution.py:57
  141.6 2.6 %collective-permute-done.9 = bf16[2,64,1536]{2,1,0:T(8,128)(2,1)S(1)} collective-permute-done((bf16[2,64,1536]{2,1,0:T(8,128)(2,1)S(1)}, bf16[2,64,1536]{2,1,0:T(8,128)(2,1)S(1)}, u32[]{:S(2)}, u32[]{:S(2)}) %collective-permute-start.9) | collective-permute-done | bytes 393248 | tf_op jit(solution)/shard_map/ppermute | solution.py:57
  144.4 5.9 %collective-permute-done.14 = bf16[2,64,1536]{2,1,0:T(8,128)(2,1)S(1)} collective-permute-done((bf16[2,64,1536]{2,1,0:T(8,128)(2,1)S(1)}, bf16[2,64,1536]{2,1,0:T(8,128)(2,1)S(1)}, u32[]{:S(2)}, u32[]{:S(2)}) %collective-permute-start.14) | collective-permute-done | bytes 393248 | tf_op jit(solution)/shard_map/ppermute | solution.py:57
  150.4 2.6 %collective-permute-done.13 = bf16[2,64,1536]{2,1,0:T(8,128)(2,1)S(1)} collective-permute-done((bf16[2,64,1536]{2,1,0:T(8,128)(2,1)S(1)}, bf16[2,64,1536]{2,1,0:T(8,128)(2,1)S(1)}, u32[]{:S(2)}, u32[]{:S(2)}) %collective-permute-start.13) | collective-permute-done | bytes 393248 | tf_op jit(solution)/shard_map/ppermute | solution.py:57
  153.3 9.3 %collective-permute-start.16 = (bf16[4,16,1536]{2,1,0:T(8,128)(2,1)S(1)}, bf16[4,16,1536]{2,1,0:T(8,128)(2,1)S(1)}, u32[]{:S(2)}, u32[]{:S(2)}) collective-permute-start(bf16[4,16,1536]{2,1,0:T(8,128)(2,1)S(1)} %get-tuple-element.58), channel_id=1, source_target_pairs={{0,48},{1,49},{2,14},{3,15},{4,52},{5,53},{6,10},{7,11},{8,56},{9,... | collective-permute-start | bytes 589832 | tf_op jit(solution)/shard_map/ppermute | solution.py:57
  164.8 8.2 %all-to-all-start.1 = ((bf16[32,10,640]{2,1,0:T(8,128)(2,1)}), bf16[32,10,640]{2,1,0:T(8,128)(2,1)S(1)}, u32[]{:S(2)}, u32[]{:S(2)}) async-start(bf16[32,10,640]{2,1,0:T(8,128)(2,1)} %reshape.161), calls=%async_computation.1 | async-start | bytes 1310720 | tf_op jit(solution)/shard_map/all_to_all | solution.py:347
  174.1 3.1 %collective-permute-start.19 = (bf16[4,16,768]{2,1,0:T(8,128)(2,1)S(1)}, bf16[4,16,768]{2,1,0:T(8,128)(2,1)S(1)}, u32[]{:S(2)}, u32[]{:S(2)}) collective-permute-start(bf16[4,16,768]{2,1,0:T(8,128)(2,1)S(1)} %pad_maximum_fusion.21), channel_id=1, source_target_pairs={{0,65},{1,64},{2,67},{3,66},{4,69},{5,68},{6,71},{7,70},{8,73},{9,... | collective-permute-start | bytes 294920 | tf_op jit(solution)/shard_map/ppermute | solution.py:57
  177.2 8.6 %all-to-all-done.1 = bf16[32,10,640]{2,1,0:T(8,128)(2,1)S(1)} async-done(((bf16[32,10,640]{2,1,0:T(8,128)(2,1)}), bf16[32,10,640]{2,1,0:T(8,128)(2,1)S(1)}, u32[]{:S(2)}, u32[]{:S(2)}) %all-to-all-start.1) | async-done | bytes 409632 | tf_op jit(solution)/shard_map/all_to_all | solution.py:347
  186.1 1.5 collective-permute-start.23
  189.4 1.7 collective-permute-done.23
  191.1 1.7 collective-permute-done.22
  195.6 5.8 %collective-permute-done.25 = bf16[4,64,768]{2,1,0:T(8,128)(2,1)S(1)} collective-permute-done((bf16[4,64,768]{2,1,0:T(8,128)(2,1)S(1)}, bf16[4,64,768]{2,1,0:T(8,128)(2,1)S(1)}, u32[]{:S(2)}, u32[]{:S(2)}) %collective-permute-start.25) | collective-permute-done | bytes 393248 | tf_op jit(solution)/shard_map/ppermute | solution.py:57
  201.5 4.2 %collective-permute-done.26 = bf16[4,64,768]{2,1,0:T(8,128)(2,1)S(1)} collective-permute-done((bf16[4,64,768]{2,1,0:T(8,128)(2,1)S(1)}, bf16[4,64,768]{2,1,0:T(8,128)(2,1)S(1)}, u32[]{:S(2)}, u32[]{:S(2)}) %collective-permute-start.26) | collective-permute-done | bytes 393248 | tf_op jit(solution)/shard_map/ppermute | solution.py:57
  206.3 2.5 %collective-permute-start.27 = (bf16[4,256,768]{2,1,0:T(8,128)(2,1)S(1)}, bf16[4,256,768]{2,1,0:T(8,128)(2,1)S(1)}, u32[]{:S(2)}, u32[]{:S(2)}) collective-permute-start(bf16[4,256,768]{2,1,0:T(8,128)(2,1)S(1)} %pad_maximum_fusion.13), channel_id=1, source_target_pairs={{0,2},{2,0},{1,3},{3,1},{4,6},{6,4},{5,7},{7,5},{8,10},{10,8},{9,1... | collective-permute-start | bytes 4718600 | tf_op jit(solution)/shard_map/ppermute | solution.py:29
  209.3 7.1 %collective-permute-done.28 = bf16[128,640]{1,0:T(8,128)(2,1)S(1)} collective-permute-done((bf16[128,640]{1,0:T(8,128)(2,1)S(1)}, bf16[128,640]{1,0:T(8,128)(2,1)S(1)}, u32[]{:S(2)}, u32[]{:S(2)}) %collective-permute-start.28) | collective-permute-done | bytes 163872 | tf_op jit(solution)/shard_map/ppermute | solution.py:353
  219.0 2.6 %stack.156 = f32[9,512,256]{2,1,0:T(8,128)} convert(bf16[9,512,256]{2,1,0:T(8,128)(2,1)S(1)} %fusion.116) | non-fusion elementwise | flops 1179648 | bytes 7077888 | tf_op jit(solution)/shard_map/stack | solution.py:363
  (256 shorter events, 49.7 us)
Async XLA Ops:
  0.6 5.2 %copy-start.10 = (bf16[1,1,16,2,64,512]{5,4,3,2,1,0:T(8,128)(2,1)S(1)}, bf16[1,1,16,2,64,512]{5,4,3,2,1,0:T(8,128)(2,1)}, u32[]{:S(2)}) copy-start(bf16[1,1,16,2,64,512]{5,4,3,2,1,0:T(8,128)(2,1)} %param.9) | copy-start | bytes 6291460
  2.1 9.2 %copy-start.53 = (s32[1,128,1]{1,2,0:T(1,128)S(1)}, s32[1,128,1]{1,2,0:T(1,128)}, u32[]{:S(2)}) copy-start(s32[1,128,1]{1,2,0:T(1,128)} %param.14) | copy-start | bytes 1540
  2.1 9.4 %copy-start.54 = (s32[1,128]{1,0:T(1,128)S(1)}, s32[1,128]{1,0:T(1,128)}, u32[]{:S(2)}) copy-start(s32[1,128]{1,0:T(1,128)} %param.16) | copy-start | bytes 1540
  2.1 9.4 %copy-start.55 = (s32[1,128]{1,0:T(1,128)S(1)}, s32[1,128]{1,0:T(1,128)}, u32[]{:S(2)}) copy-start(s32[1,128]{1,0:T(1,128)} %param.15) | copy-start | bytes 1540
  2.1 9.6 %copy-start.52 = (bf16[1,128]{1,0:T(2,128)(2,1)S(1)}, bf16[1,128]{1,0:T(2,128)(2,1)}, u32[]{:S(2)}) copy-start(bf16[1,128]{1,0:T(2,128)(2,1)} %param.13) | copy-start | bytes 772
  2.1 9.7 %copy-start.48 = (s32[1,1,16,128]{3,2,1,0:T(8,128)S(1)}, s32[1,1,16,128]{3,2,1,0:T(8,128)}, u32[]{:S(2)}) copy-start(s32[1,1,16,128]{3,2,1,0:T(8,128)} %param.17) | copy-start | bytes 24580
  2.2 9.8 %copy-start.23 = (bf16[1,128,512]{2,1,0:T(8,128)(2,1)S(1)}, bf16[1,128,512]{2,1,0:T(8,128)(2,1)}, u32[]{:S(2)}) copy-start(bf16[1,128,512]{2,1,0:T(8,128)(2,1)} %param.12) | copy-start | bytes 393220
  2.2 23.3 %collective-permute-start.2 = (bf16[256,768]{1,0:T(8,128)(2,1)S(1)}, bf16[256,768]{1,0:T(8,128)(2,1)}, u32[]{:S(2)}, u32[]{:S(2)}) collective-permute-start(bf16[256,768]{1,0:T(8,128)(2,1)S(1)} %pad_maximum_fusion.17), channel_id=1, source_target_pairs={{1,64},{64,1},{65,0},{0,65},{3,66},{66,3},{67,2},{2,67},{5,68},{68... | collective-permute-start | bytes 1179656 | tf_op jit(solution)/shard_map/ppermute | solution.py:29
  7.3 38.8 %collective-permute-start = (bf16[16,1,64,512]{3,2,1,0:T(8,128)(2,1)}, bf16[16,1,64,512]{3,2,1,0:T(8,128)(2,1)}, u32[]{:S(2)}, u32[]{:S(2)}) collective-permute-start(bf16[16,1,64,512]{3,2,1,0:T(8,128)(2,1)} %get-tuple-element.51), channel_id=1, source_target_pairs={{0,2},{2,4},{4,6},{6,8},{8,10},{10,12},{12,14},{14,16},{16,18},{18... | collective-permute-start | bytes 3145736 | tf_op jit(solution)/shard_map/ppermute | solution.py:169
  13.4 15.7 %copy-start.9 = (bf16[9,512,256]{2,1,0:T(8,128)(2,1)S(1)}, bf16[9,512,256]{2,1,0:T(8,128)(2,1)}, u32[]{:S(2)}) copy-start(bf16[9,512,256]{2,1,0:T(8,128)(2,1)} %param.10) | copy-start | bytes 7077892
  13.4 23.4 %all-to-all-start = ((bf16[32,10,640]{2,1,0:T(8,128)(2,1)}), bf16[32,10,640]{2,1,0:T(8,128)(2,1)S(1)}, u32[]{:S(2)}, u32[]{:S(2)}) async-start(bf16[32,10,640]{2,1,0:T(8,128)(2,1)} %reshape.154), calls=%async_computation | async-start | bytes 1310720 | tf_op jit(solution)/shard_map/all_to_all | solution.py:232
  21.3 26.7 %collective-permute-start.1 = (bf16[16,1,64,512]{3,2,1,0:T(8,128)(2,1)}, bf16[16,1,64,512]{3,2,1,0:T(8,128)(2,1)}, u32[]{:S(2)}, u32[]{:S(2)}) collective-permute-start(bf16[16,1,64,512]{3,2,1,0:T(8,128)(2,1)} %get-tuple-element.52), channel_id=1, source_target_pairs={{2,0},{4,2},{6,4},{8,6},{10,8},{12,10},{14,12},{16,14},{18,16},{20... | collective-permute-start | bytes 3145736 | tf_op jit(solution)/shard_map/ppermute | solution.py:170
  25.5 11.4 %collective-permute-start.5 = (bf16[256,768]{1,0:T(8,128)(2,1)}, bf16[256,768]{1,0:T(8,128)(2,1)}, u32[]{:S(2)}, u32[]{:S(2)}) collective-permute-start(bf16[256,768]{1,0:T(8,128)(2,1)} %collective-permute-done.2), channel_id=1, source_target_pairs={{0,1},{1,0},{64,65},{65,64},{2,3},{3,2},{66,67},{67,66},{4,5},{5,4... | collective-permute-start | bytes 1179656 | tf_op jit(solution)/shard_map/ppermute | solution.py:29
  25.5 16.4 %collective-permute-start.4 = (bf16[256,768]{1,0:T(8,128)(2,1)}, bf16[256,768]{1,0:T(8,128)(2,1)}, u32[]{:S(2)}, u32[]{:S(2)}) collective-permute-start(bf16[256,768]{1,0:T(8,128)(2,1)} %collective-permute-done.2), channel_id=1, source_target_pairs={{16,32},{32,16},{48,0},{0,48},{17,33},{33,17},{49,1},{1,49},{18,34... | collective-permute-start | bytes 1179656 | tf_op jit(solution)/shard_map/ppermute | solution.py:29
  28.3 13.6 %collective-permute-start.3 = (bf16[256,768]{1,0:T(8,128)(2,1)}, bf16[256,768]{1,0:T(8,128)(2,1)}, u32[]{:S(2)}, u32[]{:S(2)}) collective-permute-start(bf16[256,768]{1,0:T(8,128)(2,1)} %collective-permute-done.2), channel_id=1, source_target_pairs={{0,16},{16,0},{32,48},{48,32},{1,17},{17,1},{33,49},{49,33},{2,18}... | collective-permute-start | bytes 1179656 | tf_op jit(solution)/shard_map/ppermute | solution.py:29
  36.9 42.1 %copy-start.8 = (bf16[320,640]{1,0:T(8,128)(2,1)}, bf16[320,640]{1,0:T(8,128)(2,1)S(1)}, u32[]{:S(2)}) copy-start(bf16[320,640]{1,0:T(8,128)(2,1)S(1)} %reshape.155) | copy-start | bytes 1228804
  44.7 14.0 %collective-permute-start.6 = (bf16[4,256,768]{2,1,0:T(8,128)(2,1)}, bf16[4,256,768]{2,1,0:T(8,128)(2,1)S(1)}, u32[]{:S(2)}, u32[]{:S(2)}) collective-permute-start(bf16[4,256,768]{2,1,0:T(8,128)(2,1)} %get-tuple-element.61), channel_id=1, source_target_pairs={{0,2},{2,0},{1,3},{3,1},{4,6},{6,4},{5,7},{7,5},{8,10},{10,8},{9,1... | collective-permute-start | bytes 4718600 | tf_op jit(solution)/shard_map/ppermute | solution.py:29
  46.1 4.5 %copy-start.37 = (bf16[512,256]{1,0:T(8,128)(2,1)S(1)}, bf16[512,256]{1,0:T(8,128)(2,1)}, u32[]{:S(2)}) copy-start(bf16[512,256]{1,0:T(8,128)(2,1)} %get-tuple-element.46) | copy-start | bytes 786436
  47.9 8.7 %copy-start.15 = (bf16[16,2,64,512]{3,2,1,0:T(8,128)(2,1)}, bf16[16,2,64,512]{3,2,1,0:T(8,128)(2,1)S(1)}, u32[]{:S(2)}) copy-start(bf16[16,2,64,512]{3,2,1,0:T(8,128)(2,1)S(1)} %pad_maximum_fusion.7) | copy-start | bytes 6291460
  47.9 3.4 %copy-start.36 = (bf16[512,256]{1,0:T(8,128)(2,1)S(1)}, bf16[512,256]{1,0:T(8,128)(2,1)}, u32[]{:S(2)}) copy-start(bf16[512,256]{1,0:T(8,128)(2,1)} %get-tuple-element.45) | copy-start | bytes 786436
  50.5 9.1 %copy-start.13 = (bf16[16,2,64,512]{3,2,1,0:T(8,128)(2,1)}, bf16[16,2,64,512]{3,2,1,0:T(8,128)(2,1)S(1)}, u32[]{:S(2)}) copy-start(bf16[16,2,64,512]{3,2,1,0:T(8,128)(2,1)S(1)} %pad_maximum_fusion.8) | copy-start | bytes 6291460
  71.2 10.3 %copy-start.28 = (pred[320,128]{1,0:T(8,128)(4,1)}, pred[320,128]{1,0:T(8,128)(4,1)S(1)}, u32[]{:S(2)}) copy-start(pred[320,128]{1,0:T(8,128)(4,1)S(1)} %iota_compare_fusion.1) | copy-start | bytes 122884
  107.4 6.7 %collective-permute-start.7 = (bf16[2,256,1536]{2,1,0:T(8,128)(2,1)S(1)}, bf16[2,256,1536]{2,1,0:T(8,128)(2,1)S(1)}, u32[]{:S(2)}, u32[]{:S(2)}) collective-permute-start(bf16[2,256,1536]{2,1,0:T(8,128)(2,1)S(1)} %pad_maximum_fusion.11), channel_id=1, source_target_pairs={{0,2},{2,0},{1,3},{3,1},{4,6},{6,4},{5,7},{7,5},{8,10},{10,8},{9,1... | collective-permute-start | bytes 4718600 | tf_op jit(solution)/shard_map/ppermute | solution.py:29
  121.5 10.8 %collective-permute-start.11 = (bf16[2,256,1536]{2,1,0:T(8,128)(2,1)}, bf16[2,256,1536]{2,1,0:T(8,128)(2,1)}, u32[]{:S(2)}, u32[]{:S(2)}) collective-permute-start(bf16[2,256,1536]{2,1,0:T(8,128)(2,1)} %pad_maximum_fusion.12), channel_id=1, source_target_pairs={{0,2},{2,0},{1,3},{3,1},{4,6},{6,4},{5,7},{7,5},{8,10},{10,8},{9,1... | collective-permute-start | bytes 4718600 | tf_op jit(solution)/shard_map/ppermute | solution.py:29
  123.6 8.6 %copy-start.19 = (f32[512,1536]{1,0:T(8,128)S(1)}, f32[512,1536]{1,0:T(8,128)}, u32[]{:S(2)}) copy-start(f32[512,1536]{1,0:T(8,128)} %copy-done.18) | copy-start | bytes 9437188
  128.1 10.3 %collective-permute-start.8 = (bf16[2,64,1536]{2,1,0:T(8,128)(2,1)S(1)}, bf16[2,64,1536]{2,1,0:T(8,128)(2,1)S(1)}, u32[]{:S(2)}, u32[]{:S(2)}) collective-permute-start(bf16[2,64,1536]{2,1,0:T(8,128)(2,1)S(1)} %get-tuple-element.31), channel_id=1, source_target_pairs={{0,4},{1,5},{2,18},{3,19},{4,0},{5,1},{6,22},{7,23},{8,12},{9,13},... | collective-permute-start | bytes 1179656 | tf_op jit(solution)/shard_map/ppermute | solution.py:57
  128.9 12.8 %collective-permute-start.10 = (bf16[2,64,1536]{2,1,0:T(8,128)(2,1)S(1)}, bf16[2,64,1536]{2,1,0:T(8,128)(2,1)S(1)}, u32[]{:S(2)}, u32[]{:S(2)}) collective-permute-start(bf16[2,64,1536]{2,1,0:T(8,128)(2,1)S(1)} %get-tuple-element.32), channel_id=1, source_target_pairs={{0,8},{1,9},{2,34},{3,35},{4,12},{5,13},{6,38},{7,39},{8,0},{9,1},... | collective-permute-start | bytes 1179656 | tf_op jit(solution)/shard_map/ppermute | solution.py:57
  132.2 12.1 %collective-permute-start.9 = (bf16[2,64,1536]{2,1,0:T(8,128)(2,1)S(1)}, bf16[2,64,1536]{2,1,0:T(8,128)(2,1)S(1)}, u32[]{:S(2)}, u32[]{:S(2)}) collective-permute-start(bf16[2,64,1536]{2,1,0:T(8,128)(2,1)S(1)} %get-tuple-element.33), channel_id=1, source_target_pairs={{0,12},{1,13},{2,50},{3,51},{4,8},{5,9},{6,54},{7,55},{8,4},{9,5},... | collective-permute-start | bytes 1179656 | tf_op jit(solution)/shard_map/ppermute | solution.py:57
  134.4 10.0 %collective-permute-start.12 = (bf16[2,64,1536]{2,1,0:T(8,128)(2,1)S(1)}, bf16[2,64,1536]{2,1,0:T(8,128)(2,1)S(1)}, u32[]{:S(2)}, u32[]{:S(2)}) collective-permute-start(bf16[2,64,1536]{2,1,0:T(8,128)(2,1)S(1)} %get-tuple-element.28), channel_id=1, source_target_pairs={{0,4},{1,5},{2,18},{3,19},{4,0},{5,1},{6,22},{7,23},{8,12},{9,13},... | collective-permute-start | bytes 1179656 | tf_op jit(solution)/shard_map/ppermute | solution.py:57
  134.5 15.9 %collective-permute-start.14 = (bf16[2,64,1536]{2,1,0:T(8,128)(2,1)S(1)}, bf16[2,64,1536]{2,1,0:T(8,128)(2,1)S(1)}, u32[]{:S(2)}, u32[]{:S(2)}) collective-permute-start(bf16[2,64,1536]{2,1,0:T(8,128)(2,1)S(1)} %get-tuple-element.29), channel_id=1, source_target_pairs={{0,8},{1,9},{2,34},{3,35},{4,12},{5,13},{6,38},{7,39},{8,0},{9,1},... | collective-permute-start | bytes 1179656 | tf_op jit(solution)/shard_map/ppermute | solution.py:57
  138.3 14.6 %collective-permute-start.13 = (bf16[2,64,1536]{2,1,0:T(8,128)(2,1)S(1)}, bf16[2,64,1536]{2,1,0:T(8,128)(2,1)S(1)}, u32[]{:S(2)}, u32[]{:S(2)}) collective-permute-start(bf16[2,64,1536]{2,1,0:T(8,128)(2,1)S(1)} %get-tuple-element.30), channel_id=1, source_target_pairs={{0,12},{1,13},{2,50},{3,51},{4,8},{5,9},{6,54},{7,55},{8,4},{9,5},... | collective-permute-start | bytes 1179656 | tf_op jit(solution)/shard_map/ppermute | solution.py:57
  144.4 8.8 %copy-start.2 = (f32[2,64,1536]{2,1,0:T(8,128)}, f32[2,64,1536]{2,1,0:T(8,128)S(1)}, u32[]{:S(2)}) copy-start(f32[2,64,1536]{2,1,0:T(8,128)S(1)} %convert_add_fusion.1) | copy-start | bytes 2359300
  153.2 19.8 %copy-start.3 = (f32[2,64,1536]{2,1,0:T(8,128)S(1)}, f32[2,64,1536]{2,1,0:T(8,128)}, u32[]{:S(2)}) copy-start(f32[2,64,1536]{2,1,0:T(8,128)} %copy-done.2) | copy-start | bytes 2359300
  153.2 19.8 %collective-permute-start.15 = (bf16[4,16,1536]{2,1,0:T(8,128)(2,1)S(1)}, bf16[4,16,1536]{2,1,0:T(8,128)(2,1)S(1)}, u32[]{:S(2)}, u32[]{:S(2)}) collective-permute-start(bf16[4,16,1536]{2,1,0:T(8,128)(2,1)S(1)} %get-tuple-element.57), channel_id=1, source_target_pairs={{0,16},{1,17},{2,6},{3,7},{4,20},{5,21},{6,2},{7,3},{8,24},{9,25},... | collective-permute-start | bytes 589832 | tf_op jit(solution)/shard_map/ppermute | solution.py:57
  153.3 19.7 %collective-permute-start.16 = (bf16[4,16,1536]{2,1,0:T(8,128)(2,1)S(1)}, bf16[4,16,1536]{2,1,0:T(8,128)(2,1)S(1)}, u32[]{:S(2)}, u32[]{:S(2)}) collective-permute-start(bf16[4,16,1536]{2,1,0:T(8,128)(2,1)S(1)} %get-tuple-element.58), channel_id=1, source_target_pairs={{0,48},{1,49},{2,14},{3,15},{4,52},{5,53},{6,10},{7,11},{8,56},{9,... | collective-permute-start | bytes 589832 | tf_op jit(solution)/shard_map/ppermute | solution.py:57
  162.6 10.4 %collective-permute-start.17 = (bf16[4,16,1536]{2,1,0:T(8,128)(2,1)S(1)}, bf16[4,16,1536]{2,1,0:T(8,128)(2,1)S(1)}, u32[]{:S(2)}, u32[]{:S(2)}) collective-permute-start(bf16[4,16,1536]{2,1,0:T(8,128)(2,1)S(1)} %get-tuple-element.59), channel_id=1, source_target_pairs={{0,32},{1,33},{2,10},{3,11},{4,36},{5,37},{6,14},{7,15},{8,40},{9,... | collective-permute-start | bytes 589832 | tf_op jit(solution)/shard_map/ppermute | solution.py:57
  164.8 21.0 %all-to-all-start.1 = ((bf16[32,10,640]{2,1,0:T(8,128)(2,1)}), bf16[32,10,640]{2,1,0:T(8,128)(2,1)S(1)}, u32[]{:S(2)}, u32[]{:S(2)}) async-start(bf16[32,10,640]{2,1,0:T(8,128)(2,1)} %reshape.161), calls=%async_computation.1 | async-start | bytes 1310720 | tf_op jit(solution)/shard_map/all_to_all | solution.py:347
  173.2 12.8 %collective-permute-start.18 = (bf16[4,16,768]{2,1,0:T(8,128)(2,1)S(1)}, bf16[4,16,768]{2,1,0:T(8,128)(2,1)S(1)}, u32[]{:S(2)}, u32[]{:S(2)}) collective-permute-start(bf16[4,16,768]{2,1,0:T(8,128)(2,1)S(1)} %pad_maximum_fusion.20), channel_id=1, source_target_pairs={{0,1},{1,0},{2,3},{3,2},{4,5},{5,4},{6,7},{7,6},{8,9},{9,8},{10,11... | collective-permute-start | bytes 294920 | tf_op jit(solution)/shard_map/ppermute | solution.py:57
  173.3 12.7 %collective-permute-start.20 = (bf16[4,16,768]{2,1,0:T(8,128)(2,1)S(1)}, bf16[4,16,768]{2,1,0:T(8,128)(2,1)S(1)}, u32[]{:S(2)}, u32[]{:S(2)}) collective-permute-start(bf16[4,16,768]{2,1,0:T(8,128)(2,1)S(1)} %pad_maximum_fusion.21), channel_id=1, source_target_pairs={{0,64},{1,65},{2,66},{3,67},{4,68},{5,69},{6,70},{7,71},{8,72},{9,... | collective-permute-start | bytes 294920 | tf_op jit(solution)/shard_map/ppermute | solution.py:57
  174.1 11.9 %collective-permute-start.19 = (bf16[4,16,768]{2,1,0:T(8,128)(2,1)S(1)}, bf16[4,16,768]{2,1,0:T(8,128)(2,1)S(1)}, u32[]{:S(2)}, u32[]{:S(2)}) collective-permute-start(bf16[4,16,768]{2,1,0:T(8,128)(2,1)S(1)} %pad_maximum_fusion.21), channel_id=1, source_target_pairs={{0,65},{1,64},{2,67},{3,66},{4,69},{5,68},{6,71},{7,70},{8,73},{9,... | collective-permute-start | bytes 294920 | tf_op jit(solution)/shard_map/ppermute | solution.py:57
  186.1 5.1 %collective-permute-start.23 = (bf16[4,16,768]{2,1,0:T(8,128)(2,1)S(1)}, bf16[4,16,768]{2,1,0:T(8,128)(2,1)S(1)}, u32[]{:S(2)}, u32[]{:S(2)}) collective-permute-start(bf16[4,16,768]{2,1,0:T(8,128)(2,1)S(1)} %add_convert_fusion), channel_id=1, source_target_pairs={{0,48},{1,49},{2,14},{3,15},{4,52},{5,53},{6,10},{7,11},{8,56},{9,... | collective-permute-start | bytes 294920 | tf_op jit(solution)/shard_map/ppermute | solution.py:57
  187.5 5.3 %collective-permute-start.22 = (bf16[4,16,768]{2,1,0:T(8,128)(2,1)S(1)}, bf16[4,16,768]{2,1,0:T(8,128)(2,1)S(1)}, u32[]{:S(2)}, u32[]{:S(2)}) collective-permute-start(bf16[4,16,768]{2,1,0:T(8,128)(2,1)S(1)} %add_convert_fusion), channel_id=1, source_target_pairs={{0,32},{1,33},{2,10},{3,11},{4,36},{5,37},{6,14},{7,15},{8,40},{9,... | collective-permute-start | bytes 294920 | tf_op jit(solution)/shard_map/ppermute | solution.py:57
  188.5 4.3 %collective-permute-start.21 = (bf16[4,16,768]{2,1,0:T(8,128)(2,1)S(1)}, bf16[4,16,768]{2,1,0:T(8,128)(2,1)S(1)}, u32[]{:S(2)}, u32[]{:S(2)}) collective-permute-start(bf16[4,16,768]{2,1,0:T(8,128)(2,1)S(1)} %add_convert_fusion), channel_id=1, source_target_pairs={{0,16},{1,17},{2,6},{3,7},{4,20},{5,21},{6,2},{7,3},{8,24},{9,25},... | collective-permute-start | bytes 294920 | tf_op jit(solution)/shard_map/ppermute | solution.py:57
  192.9 8.5 %collective-permute-start.25 = (bf16[4,64,768]{2,1,0:T(8,128)(2,1)S(1)}, bf16[4,64,768]{2,1,0:T(8,128)(2,1)S(1)}, u32[]{:S(2)}, u32[]{:S(2)}) collective-permute-start(bf16[4,64,768]{2,1,0:T(8,128)(2,1)S(1)} %pad_maximum_fusion.18), channel_id=1, source_target_pairs={{0,8},{1,9},{2,34},{3,35},{4,12},{5,13},{6,38},{7,39},{8,0},{9,1},... | collective-permute-start | bytes 1179656 | tf_op jit(solution)/shard_map/ppermute | solution.py:57
  194.2 11.5 %collective-permute-start.26 = (bf16[4,64,768]{2,1,0:T(8,128)(2,1)S(1)}, bf16[4,64,768]{2,1,0:T(8,128)(2,1)S(1)}, u32[]{:S(2)}, u32[]{:S(2)}) collective-permute-start(bf16[4,64,768]{2,1,0:T(8,128)(2,1)S(1)} %pad_maximum_fusion.18), channel_id=1, source_target_pairs={{0,12},{1,13},{2,50},{3,51},{4,8},{5,9},{6,54},{7,55},{8,4},{9,5},... | collective-permute-start | bytes 1179656 | tf_op jit(solution)/shard_map/ppermute | solution.py:57
  195.4 10.2 %collective-permute-start.24 = (bf16[4,64,768]{2,1,0:T(8,128)(2,1)S(1)}, bf16[4,64,768]{2,1,0:T(8,128)(2,1)S(1)}, u32[]{:S(2)}, u32[]{:S(2)}) collective-permute-start(bf16[4,64,768]{2,1,0:T(8,128)(2,1)S(1)} %pad_maximum_fusion.18), channel_id=1, source_target_pairs={{0,4},{1,5},{2,18},{3,19},{4,0},{5,1},{6,22},{7,23},{8,12},{9,13},... | collective-permute-start | bytes 1179656 | tf_op jit(solution)/shard_map/ppermute | solution.py:57
  206.3 11.5 %collective-permute-start.27 = (bf16[4,256,768]{2,1,0:T(8,128)(2,1)S(1)}, bf16[4,256,768]{2,1,0:T(8,128)(2,1)S(1)}, u32[]{:S(2)}, u32[]{:S(2)}) collective-permute-start(bf16[4,256,768]{2,1,0:T(8,128)(2,1)S(1)} %pad_maximum_fusion.13), channel_id=1, source_target_pairs={{0,2},{2,0},{1,3},{3,1},{4,6},{6,4},{5,7},{7,5},{8,10},{10,8},{9,1... | collective-permute-start | bytes 4718600 | tf_op jit(solution)/shard_map/ppermute | solution.py:29
  209.2 7.2 %collective-permute-start.28 = (bf16[128,640]{1,0:T(8,128)(2,1)S(1)}, bf16[128,640]{1,0:T(8,128)(2,1)S(1)}, u32[]{:S(2)}, u32[]{:S(2)}) collective-permute-start(bf16[128,640]{1,0:T(8,128)(2,1)S(1)} %pad_maximum_fusion.19), channel_id=1, source_target_pairs={{0,64},{64,0},{1,65},{65,1},{2,66},{66,2},{3,67},{67,3},{4,68},{68... | collective-permute-start | bytes 491528 | tf_op jit(solution)/shard_map/ppermute | solution.py:353
  (40 other events, 73.7 us)

commit v4 on v3

--- a/solution.py
+++ b/solution.py
@@ -3,6 +3,8 @@
 import jax
 import jax.numpy as jnp
 from jax import lax
+from jax.experimental import pallas as pl
+from jax.experimental.pallas import tpu as pltpu
 from jax.sharding import Mesh, PartitionSpec as P
 
 
@@ -11,6 +13,8 @@
 TILE = ("z", "x", "core")
 ALL = ("fsdp", "z", "x", "core", "scan")
 PACK = 640
+CAPACITY = 10
+WIDTH = 64
 
 
 def contract_rows(left, right):
@@ -157,7 +161,7 @@
         index = (half ^ core, group ^ color, 0, 0)
         return lax.dynamic_slice(both, index, (1, 1, rows, 3 * cols))[0, 0]
 
-    return block
+    return block, mine, other, jnp.stack([core, color]).astype(jnp.int32)
 
 
 def edges(block):
@@ -178,6 +182,136 @@
     if step > 0:
         return jnp.concatenate([value[:, :, 1:], zeros], axis=2)
     return jnp.concatenate([zeros, value[:, :, :-1]], axis=2)
+
+
+def stacked_rows(low, block, high):
+    count, rows, width, channels = block.shape
+    parts = (
+        jnp.concatenate([low[...], block[:, :1]], axis=1),
+        block[...],
+        jnp.concatenate([block[:, 1:], high[...]], axis=1),
+    )
+    return [part.reshape(count * rows * width, channels) for part in parts]
+
+
+def finish_conv(sums, width, out):
+    left, middle, right = sums
+    size = left.shape[0]
+    column = lax.broadcasted_iota(jnp.int32, left.shape, 0) % width
+    left = jnp.where(column == 0, 0.0, pltpu.roll(left, 1, 0))
+    right = jnp.where(column == width - 1, 0.0, pltpu.roll(right, size - 1, 0))
+    out[...] = (left + middle + right).astype(BF).reshape(out.shape)
+
+
+def near_body(low, block, high, weights, out):
+    stacked = stacked_rows(low, block, high)
+    sums = []
+    for b in range(3):
+        total = None
+        for a in range(3):
+            part = jnp.dot(stacked[a], weights[3 * a + b], preferred_element_type=F32)
+            total = part if total is None else total + part
+        sums.append(total)
+    finish_conv(sums, block.shape[2], out)
+
+
+def far_body(place, low, block, high, mine, other, out):
+    stacked = stacked_rows(low, block, high)
+    core, color = place[0], place[1]
+    half = out.shape[2]
+    total = None
+    for a in range(3):
+        index = color ^ a
+        first, second = mine[index], other[index]
+        for h in range(2):
+            weights = jnp.where(core == h, first, second)
+            part = jnp.dot(
+                stacked[a][:, h * half : (h + 1) * half], weights, preferred_element_type=F32
+            )
+            total = part if total is None else total + part
+    sums = [total[:, b * half : (b + 1) * half] for b in range(3)]
+    finish_conv(sums, block.shape[2], out)
+
+
+def convolve(body, low, block, high, weights, place=()):
+    frames, rows, width, channels = block.shape
+    step = 4
+    half = channels // 2
+
+    def edge(count):
+        return pl.BlockSpec((step, count, width, channels), lambda i, *_: (i, 0, 0, 0))
+
+    def whole(value):
+        return pl.BlockSpec(value.shape, lambda i, *_: (0,) * value.ndim)
+
+    return pl.pallas_call(
+        body,
+        grid_spec=pltpu.PrefetchScalarGridSpec(
+            num_scalar_prefetch=len(place),
+            grid=(frames // step,),
+            in_specs=[edge(1), edge(rows), edge(1)] + [whole(value) for value in weights],
+            out_specs=pl.BlockSpec((step, rows * width, half), lambda i, *_: (i, 0, 0)),
+        ),
+        out_shape=jax.ShapeDtypeStruct((frames, rows * width, half), BF),
+        compiler_params=pltpu.CompilerParams(vmem_limit_bytes=32 * 1024 * 1024),
+        cost_estimate=pl.CostEstimate(
+            flops=2 * frames * rows * width * 9 * channels * half,
+            bytes_accessed=2 * (block.size * 2 + 9 * channels * half + block.size // 2),
+            transcendentals=0,
+        ),
+        name="conv",
+    )(*place, low, block, high, *weights)
+
+
+def pack_body(half_of, weights, bias, tiles, rows, columns, counts, packed, selector):
+    neurons, channels = weights.shape
+    slots = packed.shape[0]
+    half = channels // 2
+    ids = jnp.broadcast_to(tiles[...], (neurons, neurons))
+    before = lax.broadcasted_iota(jnp.int32, ids.shape, 0) < lax.broadcasted_iota(
+        jnp.int32, ids.shape, 1
+    )
+    same = ids == jnp.transpose(ids)
+    rank = jnp.sum(jnp.where(same & before, 1, 0), axis=0, keepdims=True)
+    spot = tiles[...] * CAPACITY + rank
+    chosen = jnp.where(
+        lax.broadcasted_iota(jnp.int32, (slots, neurons), 0) == spot, 1.0, 0.0
+    ).astype(BF)
+    selector[...] = chosen
+    lower, upper = weights[:, :half], weights[:, half:]
+    own = jnp.where(half_of[0] == 0, lower, upper)
+    far = jnp.where(half_of[0] == 0, upper, lower)
+    packed[:, :half] = jnp.dot(chosen, own, preferred_element_type=F32).astype(BF)
+    packed[:, half:channels] = jnp.dot(chosen, far, preferred_element_type=F32).astype(BF)
+    lines = jnp.concatenate(
+        [
+            bias[...].astype(F32),
+            (rows[...] * WIDTH + columns[...]).astype(F32),
+            jnp.ones((1, neurons), F32),
+            jnp.zeros((5, neurons), F32),
+            counts[...].astype(F32),
+            jnp.zeros((packed.shape[1] - channels - 8 - counts.shape[0], neurons), F32),
+        ]
+    ).astype(BF)
+    packed[:, channels:] = lax.dot_general(
+        chosen, lines, (((1,), (1,)), ((), ())), preferred_element_type=F32
+    ).astype(BF)
+
+
+def pack(half_of, weights, bias, tiles, rows, columns, counts, slots):
+    neurons = weights.shape[0]
+    smem = pl.BlockSpec(memory_space=pltpu.SMEM)
+    vmem = pl.BlockSpec(memory_space=pltpu.VMEM)
+    return pl.pallas_call(
+        pack_body,
+        in_specs=[smem] + [vmem] * 6,
+        out_specs=[vmem, vmem],
+        out_shape=[
+            jax.ShapeDtypeStruct((slots, PACK), BF),
+            jax.ShapeDtypeStruct((slots, neurons), BF),
+        ],
+        name="pack",
+    )(half_of, weights, bias, tiles, rows, columns, counts)
 
 
 def compute(
@@ -192,7 +326,7 @@
     spikes,
 ):
     fsdp = lax.axis_index("fsdp")
-    block = blocks_of(spatial_weight, temporal_weight)
+    block, mine_blocks, other_blocks, place = blocks_of(spatial_weight, temporal_weight)
     frames_in = acts[0, 0]
     frames, rows, width, channels = frames_in.shape
     half = channels // 2
@@ -200,7 +334,7 @@
     tile_count = lax.axis_size("z") * lax.axis_size("x") * lax.axis_size("core")
     rep_count = lax.axis_size("fsdp")
     neurons = readout_weight.shape[1]
-    capacity = max(2, 5 * neurons // (2 * tile_count))
+    capacity = CAPACITY
     slot_count = tile_count * capacity
     scale_factor = 1.0 / (rep_count * frames)
     low, high = edges(frames_in)
@@ -210,25 +344,16 @@
             fsdp == 0, value, jnp.concatenate([value[:, half:], value[:, :half]], axis=1)
         )
 
-    tile_ids = tile_of[0, :, 0]
-    cell_ids = row_of[0] * width + column_of[0]
-    same_tile = tile_ids[:, None] == tile_ids[None, :]
-    order = jnp.arange(neurons)
-    rank_ids = jnp.sum((same_tile & (order[None, :] < order[:, None])).astype(jnp.int32), axis=1)
-    slot_ids = tile_ids * capacity + rank_ids
-    selector = (slot_ids[None, :] == jnp.arange(slot_count)[:, None]).astype(BF)
-    table = jnp.concatenate(
-        [
-            local(readout_weight[0]),
-            readout_bias[0][:, None],
-            cell_ids.astype(BF)[:, None],
-            jnp.ones((neurons, 1), BF),
-            spikes[0, 0].T.astype(BF),
-            jnp.zeros((neurons, PACK - channels - 3 - frames), BF),
-        ],
-        axis=1,
-    )
-    packed = jnp.dot(selector, table, preferred_element_type=F32).astype(BF)
+    packed, selector = pack(
+        fsdp.astype(jnp.int32).reshape(1),
+        readout_weight[0],
+        readout_bias,
+        tile_of.reshape(1, neurons),
+        row_of,
+        column_of,
+        spikes[0, 0],
+        slot_count,
+    )
     held = lax.all_to_all(
         packed.reshape(tile_count, capacity, PACK),
         TILE,
@@ -241,33 +366,17 @@
         frames_in.reshape(-1, channels),
         jnp.concatenate([frames_in[:, 1:], high], axis=1).reshape(-1, channels),
     ]
-    taller = jnp.concatenate(shifted_rows, axis=1)
-
-    def convolve(weights):
-        sums = jnp.dot(taller, weights, preferred_element_type=F32)
-        sums = sums.reshape(frames, rows, width, 3 * half)
-        total = (
-            shift(sums[..., :half], -1)
-            + sums[..., half : 2 * half]
-            + shift(sums[..., 2 * half :], 1)
-        )
-        return total.astype(BF).reshape(frames, cells, half)
-
-    near_weights = jnp.concatenate(
-        [
-            jnp.concatenate([spatial_weight[3 * a + b] for b in range(3)], axis=1)
-            for a in range(3)
-        ]
-    )
-    near_out = convolve(near_weights)
-    far_out = convolve(jnp.concatenate([block(h, g) for g in range(3) for h in range(2)]))
+    near_out = convolve(near_body, low, frames_in, high, (spatial_weight,))
+    far_out = convolve(
+        far_body, low, frames_in, high, (mine_blocks, other_blocks), (place,)
+    )
     far_out, held = lax.optimization_barrier((far_out, held))
     spatial_out = jnp.concatenate([near_out, far_out], axis=2)
     slot_weight = held[:, :channels]
-    extras = held[:, channels : channels + 3 + frames].astype(F32)
+    extras = held[:, channels : channels + 8 + frames].astype(F32)
     slot_bias = extras[:, :1]
     slot_cell = jnp.where(extras[:, 2:3] > 0.5, extras[:, 1:2].astype(jnp.int32), cells)
-    slot_spikes = extras[:, 3:]
+    slot_spikes = extras[:, 8:]
 
     lag_blocks = [block(q ^ fsdp, 3) for q in range(2)]
     temporal = [

time: 227 us -> 240 us (1.057)
  Pallas kernels: 0 us -> 16.9 us
  matrix products: 40.9 us -> 30.5 us
  starting transfers between devices: 61.6 us -> 66.9 us
  local copies, waits for them, and re-layouts: 32.3 us -> 34.9 us
    pallas_call x0 -> x3, Pallas kernels: none -> 16.9 us  [the longest x2 14.8 us: convolve(): pl.pallas_call(body, grid_spec=pltpu.PrefetchScalarGridSpec(num_scalar_pr...]
    dot_general x3 -> x0, matrix products: 10.5 us -> none  [the longest x2 10.2 us: convolve(): sums = jnp.dot(taller, weights, preferred_element_type=F32)]
    ppermute x18, starting transfers between devices: 28.6 us -> 21.8 us  [permute_by_core(): return lax.ppermute(value, ALL, perm)]
    all_to_all x1, starting transfers between devices: 7.88 us -> 13.8 us  [compute(): lax.all_to_all(packed.reshape(tile_count, capacity, PACK), TILE, split_ax...]
    ppermute x1, starting transfers between devices: 0.09 us -> 3.91 us  [compute(): other = lax.ppermute(mine, 'fsdp', [(0, 1), (1, 0)])]
    ppermute x8, waiting for transfers between devices: 5.02 us -> 8.83 us  [swap(): return lax.ppermute(value, name, perm)]
    convert_element_type x5 -> x1, other arithmetic: 4.24 us -> 0.73 us  [compute(): extras = held[:, channels:channels + 8 + frames].astype(F32)]
    ppermute x8, starting transfers between devices: 10.7 us -> 13.4 us  [swap(): return lax.ppermute(value, name, perm)]
  transfers between devices with their start and end apart: 31 -> 31, of which waited for: 12 -> 14; matrix products, arithmetic and copies ran while one was open for 17% -> 15% of each run, Pallas kernels for 0% -> 4%
where the time goes in v4:
time: 240 us; the launch traced here: 236 us
  starting transfers between devices  66.9 us (28%)
  waiting for transfers between devices  54.5 us (23%)
  local copies, waits for them, and re-layouts  34.9 us (15%)
  matrix products  30.5 us (13%)
  other arithmetic  30.1 us (13%)
  Pallas kernels  16.9 us (7%)
    ppermute x18, waiting for transfers between devices, permute_by_core(): return lax.ppermute(value, ALL, perm)  25.5 us
    ppermute x18, starting transfers between devices, permute_by_core(): return lax.ppermute(value, ALL, perm)  21.8 us
    dot_general x6, matrix products, contract_rows(): lax.dot_general(left, right, (((0,), (0,)), ((), ())), preferred_element_...  16.7 us
    pallas_call x2, Pallas kernels, convolve(): pl.pallas_call(body, grid_spec=pltpu.PrefetchScalarGridSpec(num_scalar_pr...  14.8 us
    all_to_all x1, starting transfers between devices, compute(): lax.all_to_all(packed.reshape(tile_count, capacity, PACK), TILE, split_ax...  13.8 us
    ppermute x8, starting transfers between devices, swap(): return lax.ppermute(value, name, perm)  13.4 us
    unnamed x83, local copies, waits for them, and re-layouts  12.2 us
    ppermute x8, waiting for transfers between devices, swap(): return lax.ppermute(value, name, perm)  8.83 us
  transfers between devices with their start and end apart: 31, of which 14 were waited for; matrix products, arithmetic and copies ran while one was open for 15% of the time, Pallas kernels for 4%

profile of v4, /device:TPU:1, one launch (start us, length us, event | category | flops | bytes accessed | tf_op | source)
XLA Modules:
  0.0 235.9 jit_solution(5737851125461515355)
XLA Ops:
  2.1 3.6 %collective-permute-start.2 = (bf16[256,768]{1,0:T(8,128)(2,1)S(1)}, bf16[256,768]{1,0:T(8,128)(2,1)S(1)}, u32[]{:S(2)}, u32[]{:S(2)}) collective-permute-start(bf16[256,768]{1,0:T(8,128)(2,1)S(1)} %pad_maximum_fusion.12), channel_id=1, source_target_pairs={{1,64},{64,1},{65,0},{0,65},{3,66},{66,3},{67,2},{2,67},{5,68},{68... | collective-permute-start | bytes 1179656 | tf_op jit(solution)/shard_map/ppermute | solution.py:33
  5.7 8.7 %collective-permute-done.2 = bf16[256,768]{1,0:T(8,128)(2,1)S(1)} collective-permute-done((bf16[256,768]{1,0:T(8,128)(2,1)S(1)}, bf16[256,768]{1,0:T(8,128)(2,1)S(1)}, u32[]{:S(2)}, u32[]{:S(2)}) %collective-permute-start.2) | collective-permute-done | bytes 393248 | tf_op jit(solution)/shard_map/ppermute | solution.py:33
  14.5 3.6 %collective-permute-start.4 = (bf16[256,768]{1,0:T(8,128)(2,1)S(1)}, bf16[256,768]{1,0:T(8,128)(2,1)S(1)}, u32[]{:S(2)}, u32[]{:S(2)}) collective-permute-start(bf16[256,768]{1,0:T(8,128)(2,1)S(1)} %collective-permute-done.2), channel_id=1, source_target_pairs={{16,32},{32,16},{48,0},{0,48},{17,33},{33,17},{49,1},{1,49},{18,34... | collective-permute-start | bytes 1179656 | tf_op jit(solution)/shard_map/ppermute | solution.py:33
  19.6 5.0 %collective-permute-start = (bf16[16,1,64,512]{3,2,1,0:T(8,128)(2,1)}, bf16[16,1,64,512]{3,2,1,0:T(8,128)(2,1)S(1)}, u32[]{:S(2)}, u32[]{:S(2)}) collective-permute-start(bf16[16,1,64,512]{3,2,1,0:T(8,128)(2,1)} %get-tuple-element.43), channel_id=1, source_target_pairs={{0,2},{2,4},{4,6},{6,8},{8,10},{10,12},{12,14},{14,16},{16,18},{18... | collective-permute-start | bytes 3145736 | tf_op jit(solution)/shard_map/ppermute | solution.py:173
  24.7 1.9 collective-permute-start.1
  26.7 1.9 fusion.105
  28.6 2.9 %collective-permute-start.6 = (bf16[4,256,768]{2,1,0:T(8,128)(2,1)}, bf16[4,256,768]{2,1,0:T(8,128)(2,1)}, u32[]{:S(2)}, u32[]{:S(2)}) collective-permute-start(bf16[4,256,768]{2,1,0:T(8,128)(2,1)} %get-tuple-element.52.mine), channel_id=1, source_target_pairs={{0,2},{2,0},{1,3},{3,1},{4,6},{6,4},{5,7},{7,5},{8,10},{10,8},{9,1... | collective-permute-start | bytes 4718600 | tf_op jit(solution)/shard_map/ppermute | solution.py:33
  31.5 2.1 pack.1
  33.6 2.0 reshape.104
  35.6 13.8 %all-to-all-start = ((bf16[32,10,640]{2,1,0:T(8,128)(2,1)}), bf16[32,10,640]{2,1,0:T(8,128)(2,1)}, u32[]{:S(2)}, u32[]{:S(2)}) async-start(bf16[32,10,640]{2,1,0:T(8,128)(2,1)} %reshape.104), calls=%async_computation | async-start | bytes 1310720 | tf_op jit(solution)/shard_map/all_to_all | solution.py:357
  49.4 2.0 fusion.109
  53.0 1.8 dynamic-slice_bitcast_fusion.5
  54.8 7.3 %all-to-all-done = bf16[32,10,640]{2,1,0:T(8,128)(2,1)} async-done(((bf16[32,10,640]{2,1,0:T(8,128)(2,1)}), bf16[32,10,640]{2,1,0:T(8,128)(2,1)}, u32[]{:S(2)}, u32[]{:S(2)}) %all-to-all-start) | async-done | bytes 409632 | tf_op jit(solution)/shard_map/all_to_all | solution.py:357
  62.1 2.0 reshape.105
  64.1 2.7 %pad_maximum_fusion.5 = bf16[16,2,64,512]{3,2,1,0:T(8,128)(2,1)} fusion(bf16[16,1,64,512]{3,2,1,0:T(8,128)(2,1)} %get-tuple-element.42, bf16[16,1,64,512]{3,2,1,0:T(8,128)(2,1)S(1)} %collective-permute-done.low), kind=kLoop, calls=%fused_computation.41 | loop fusion | flops 1048576 | bytes 4194304 | tf_op jit(solution)/shard_map/concatenate | solution.py:365
  66.8 3.3 %pad_maximum_fusion.6 = bf16[16,2,64,512]{3,2,1,0:T(8,128)(2,1)} fusion(bf16[16,1,64,512]{3,2,1,0:T(8,128)(2,1)} %collective-permute-done.1.high, bf16[16,1,64,512]{3,2,1,0:T(8,128)(2,1)} %get-tuple-element.43), kind=kLoop, calls=%fused_computation.42 | loop fusion | flops 1048576 | bytes 4194304 | tf_op jit(solution)/shard_map/concatenate | solution.py:367
  70.1 6.6 %conv.3 = bf16[16,128,256]{2,1,0:T(8,128)(2,1)S(1)} custom-call(bf16[16,1,64,512]{3,2,1,0:T(8,128)(2,1)S(1)} %collective-permute-done.low, bf16[16,2,64,512]{3,2,1,0:T(8,128)(2,1)S(1)} %bitcast.146, bf16[16,1,64,512]{3,2,1,0:T(8,128)(2,1)} %collective-permute-done.1.high, bf16[9,512,256]{2,1,0:T(8,128)(2,1)S(1)} %copy-done.4), custom_call_target="tpu_custom_call" | custom-call | flops 4831838208 | bytes 7602176 | tf_op jit(solution)/shard_map/conv/pallas_call | solution.py:247
  77.6 8.2 %conv.2 = bf16[16,128,256]{2,1,0:T(8,128)(2,1)S(1)} custom-call(s32[2]{0:T(128)S(1)} %pad_add_fusion.place, bf16[16,1,64,512]{3,2,1,0:T(8,128)(2,1)S(1)} %collective-permute-done.low, bf16[16,2,64,512]{3,2,1,0:T(8,128)(2,1)S(1)} %bitcast.147, bf16[16,1,64,512]{3,2,1,0:T(8,128)(2,1)} %collective-permute-done.1.high, ...), custom_call_target="tpu_custom_call" | custom-call | flops 4831838208 | bytes 7602176 | tf_op jit(solution)/shard_map/conv/pallas_call | solution.py:247
  86.8 2.1 copy.18
  99.1 2.0 convolution_bitcast_fusion
  107.2 2.5 %fusion.3 = bf16[2048,512]{1,0:T(8,128)(2,1)S(1)} fusion(f32[2048,512]{1,0:T(8,128)S(1)} %copy-done.8, bf16[320,2048]{1,0:T(8,128)(2,1)S(1)} %bitcast.167, bf16[320,2048]{1,0:T(8,128)(2,1)S(1)} %bitcast.168, bf16[320,512]{1,0:T(8,128)(2,1)S(1)} %slice-done), kind=kOutput, calls=%fused_computation.8 | convolution fusion | flops 1353973760 | bytes 9240576 | tf_op jit(solution)/shard_map/dot_general | solution.py:21
  110.9 3.5 %convolution_convert_fusion = bf16[2048,512]{1,0:T(8,128)(2,1)S(1)} fusion(bf16[2048,512]{1,0:T(8,128)(2,1)S(1)} %bitcast.163, bf16[2048,512]{1,0:T(8,128)(2,1)S(1)} %bitcast.161, bf16[2048,512]{1,0:T(8,128)(2,1)S(1)} %fusion.3, bf16[256,256]{1,0:T(8,128)(2,1)S(1)} %copy-done.34, bf16[256,256]{1,0:T(8,128)(2,1)S(1)} %copy-done.23, ...), kind=kOutput, calls=%fused_computation.22 | convolution fusion | flops 3260022784 | bytes 9961472 | tf_op jit(solution)/shard_map/dot_general | solution.py:438
  114.3 3.5 %fusion.7 = f32[512,1536]{1,0:T(8,128)S(1)} fusion(bf16[2048,512]{1,0:T(8,128)(2,1)S(1)} %bitcast.150, bf16[2048,512]{1,0:T(8,128)(2,1)S(1)} %bitcast.164, bf16[2048,512]{1,0:T(8,128)(2,1)S(1)} %bitcast.162, bf16[2048,512]{1,0:T(8,128)(2,1)S(1)} %fusion.3), kind=kOutput, calls=%fused_computation.27 | convolution fusion | flops 3240099840 | bytes 11534336 | tf_op jit(solution)/shard_map/dot_general | solution.py:21
  122.4 3.5 %fusion.114 = f32[512,1536]{1,0:T(8,128)S(1)} fusion(bf16[2048,512]{1,0:T(8,128)(2,1)S(1)} %bitcast.166, bf16[2048,1536]{1,0:T(8,128)(2,1)S(1)} %pad_maximum_fusion.1), kind=kOutput, calls=%fused_computation.227 | convolution fusion | flops 3221225472 | bytes 11534336 | tf_op jit(solution)/shard_map/dot_general | solution.py:21
  126.7 3.4 %fusion.115 = f32[1536,512]{0,1:T(8,128)S(1)} fusion(bf16[2048,1536]{1,0:T(8,128)(2,1)S(1)} %pad_maximum_fusion.1, bf16[2048,512]{1,0:T(8,128)(2,1)S(1)} %bitcast.148), kind=kOutput, calls=%fused_computation.228 | convolution fusion | flops 3221225472 | bytes 11534336 | tf_op jit(solution)/shard_map/dot_general | solution.py:21
  133.6 3.6 %fusion.116 = f32[512,1536]{1,0:T(8,128)S(1)} fusion(bf16[2048,512]{1,0:T(8,128)(2,1)S(1)} %bitcast.165, bf16[2048,1536]{1,0:T(8,128)(2,1)S(1)} %pad_maximum_fusion.1), kind=kOutput, calls=%fused_computation.229 | convolution fusion | flops 3221225472 | bytes 11534336 | tf_op jit(solution)/shard_map/dot_general | solution.py:21
  141.5 4.3 %convolution_convert_fusion.1 = bf16[320,512]{1,0:T(8,128)(2,1)S(1)} fusion(bf16[40,8,16,128]{3,2,1,0:T(8,128)(2,1)S(1)} %bitcast.158, f32[2048,512]{1,0:T(8,128)} %copy-done.7), kind=kOutput, calls=%fused_computation.85 | convolution fusion | flops 675446784 | bytes 5832704 | tf_op jit(solution)/shard_map/dot_general | solution.py:430
  146.1 1.7 collective-permute-start.10
  147.8 2.2 collective-permute-start.9
  150.1 1.9 maximum_add_fusion.1
  152.3 1.7 collective-permute-start.14
  153.9 2.2 collective-permute-start.13
  157.5 2.6 %collective-permute-done.9 = bf16[2,64,1536]{2,1,0:T(8,128)(2,1)S(1)} collective-permute-done((bf16[2,64,1536]{2,1,0:T(8,128)(2,1)S(1)}, bf16[2,64,1536]{2,1,0:T(8,128)(2,1)S(1)}, u32[]{:S(2)}, u32[]{:S(2)}) %collective-permute-start.9) | collective-permute-done | bytes 393248 | tf_op jit(solution)/shard_map/ppermute | solution.py:61
  161.5 4.5 %collective-permute-done.14 = bf16[2,64,1536]{2,1,0:T(8,128)(2,1)S(1)} collective-permute-done((bf16[2,64,1536]{2,1,0:T(8,128)(2,1)S(1)}, bf16[2,64,1536]{2,1,0:T(8,128)(2,1)S(1)}, u32[]{:S(2)}, u32[]{:S(2)}) %collective-permute-start.14) | collective-permute-done | bytes 393248 | tf_op jit(solution)/shard_map/ppermute | solution.py:61
  166.0 2.6 %collective-permute-done.13 = bf16[2,64,1536]{2,1,0:T(8,128)(2,1)S(1)} collective-permute-done((bf16[2,64,1536]{2,1,0:T(8,128)(2,1)S(1)}, bf16[2,64,1536]{2,1,0:T(8,128)(2,1)S(1)}, u32[]{:S(2)}, u32[]{:S(2)}) %collective-permute-start.13) | collective-permute-done | bytes 393248 | tf_op jit(solution)/shard_map/ppermute | solution.py:61
  173.2 7.1 %all-to-all-start.1 = ((bf16[32,10,640]{2,1,0:T(8,128)(2,1)}), bf16[32,10,640]{2,1,0:T(8,128)(2,1)S(1)}, u32[]{:S(2)}, u32[]{:S(2)}) async-start(bf16[32,10,640]{2,1,0:T(8,128)(2,1)} %reshape.110), calls=%async_computation.1 | async-start | bytes 1310720 | tf_op jit(solution)/shard_map/all_to_all | solution.py:456
  182.0 2.5 %collective-permute-start.20 = (bf16[4,16,768]{2,1,0:T(8,128)(2,1)S(1)}, bf16[4,16,768]{2,1,0:T(8,128)(2,1)S(1)}, u32[]{:S(2)}, u32[]{:S(2)}) collective-permute-start(bf16[4,16,768]{2,1,0:T(8,128)(2,1)S(1)} %pad_maximum_fusion.16), channel_id=1, source_target_pairs={{0,64},{1,65},{2,66},{3,67},{4,68},{5,69},{6,70},{7,71},{8,72},{9,... | collective-permute-start | bytes 294920 | tf_op jit(solution)/shard_map/ppermute | solution.py:61
  184.8 8.3 %all-to-all-done.1 = bf16[32,10,640]{2,1,0:T(8,128)(2,1)S(1)} async-done(((bf16[32,10,640]{2,1,0:T(8,128)(2,1)}), bf16[32,10,640]{2,1,0:T(8,128)(2,1)S(1)}, u32[]{:S(2)}, u32[]{:S(2)}) %all-to-all-start.1) | async-done | bytes 409632 | tf_op jit(solution)/shard_map/all_to_all | solution.py:456
  196.7 1.7 collective-permute-done.23
  198.4 1.7 collective-permute-done.22
  200.2 2.1 collective-permute-start.25
  203.1 5.6 %collective-permute-done.25 = bf16[4,64,768]{2,1,0:T(8,128)(2,1)S(1)} collective-permute-done((bf16[4,64,768]{2,1,0:T(8,128)(2,1)S(1)}, bf16[4,64,768]{2,1,0:T(8,128)(2,1)S(1)}, u32[]{:S(2)}, u32[]{:S(2)}) %collective-permute-start.25) | collective-permute-done | bytes 393248 | tf_op jit(solution)/shard_map/ppermute | solution.py:61
  208.8 4.2 %collective-permute-done.26 = bf16[4,64,768]{2,1,0:T(8,128)(2,1)S(1)} collective-permute-done((bf16[4,64,768]{2,1,0:T(8,128)(2,1)S(1)}, bf16[4,64,768]{2,1,0:T(8,128)(2,1)S(1)}, u32[]{:S(2)}, u32[]{:S(2)}) %collective-permute-start.26) | collective-permute-done | bytes 393248 | tf_op jit(solution)/shard_map/ppermute | solution.py:61
  216.5 2.4 %collective-permute-start.27 = (bf16[4,256,768]{2,1,0:T(8,128)(2,1)}, bf16[4,256,768]{2,1,0:T(8,128)(2,1)}, u32[]{:S(2)}, u32[]{:S(2)}) collective-permute-start(bf16[4,256,768]{2,1,0:T(8,128)(2,1)} %pad_maximum_fusion.10), channel_id=1, source_target_pairs={{0,2},{2,0},{1,3},{3,1},{4,6},{6,4},{5,7},{7,5},{8,10},{10,8},{9,1... | collective-permute-start | bytes 4718600 | tf_op jit(solution)/shard_map/ppermute | solution.py:33
  219.3 3.9 %collective-permute-start.28 = (bf16[128,640]{1,0:T(8,128)(2,1)S(1)}, bf16[128,640]{1,0:T(8,128)(2,1)S(1)}, u32[]{:S(2)}, u32[]{:S(2)}) collective-permute-start(bf16[128,640]{1,0:T(8,128)(2,1)S(1)} %pad_maximum_fusion.14), channel_id=1, source_target_pairs={{0,64},{64,0},{1,65},{65,1},{2,66},{66,2},{3,67},{67,3},{4,68},{68... | collective-permute-start | bytes 491528 | tf_op jit(solution)/shard_map/ppermute | solution.py:462
  223.2 4.6 %collective-permute-done.28 = bf16[128,640]{1,0:T(8,128)(2,1)S(1)} collective-permute-done((bf16[128,640]{1,0:T(8,128)(2,1)S(1)}, bf16[128,640]{1,0:T(8,128)(2,1)S(1)}, u32[]{:S(2)}, u32[]{:S(2)}) %collective-permute-start.28) | collective-permute-done | bytes 163872 | tf_op jit(solution)/shard_map/ppermute | solution.py:462
  229.2 2.0 broadcast_select_fusion
  231.7 2.6 %stack.168 = f32[9,512,256]{2,1,0:T(8,128)} convert(bf16[9,512,256]{2,1,0:T(8,128)(2,1)S(1)} %fusion.84) | non-fusion elementwise | flops 1179648 | bytes 7077888 | tf_op jit(solution)/shard_map/stack | solution.py:472
  (194 shorter events, 58.3 us)
Async XLA Ops:
  0.6 17.5 %copy-start = (bf16[1,1,16,2,64,512]{5,4,3,2,1,0:T(8,128)(2,1)S(1)}, bf16[1,1,16,2,64,512]{5,4,3,2,1,0:T(8,128)(2,1)}, u32[]{:S(2)}) copy-start(bf16[1,1,16,2,64,512]{5,4,3,2,1,0:T(8,128)(2,1)} %param.9) | copy-start | bytes 6291460
  2.1 12.3 %collective-permute-start.2 = (bf16[256,768]{1,0:T(8,128)(2,1)S(1)}, bf16[256,768]{1,0:T(8,128)(2,1)S(1)}, u32[]{:S(2)}, u32[]{:S(2)}) collective-permute-start(bf16[256,768]{1,0:T(8,128)(2,1)S(1)} %pad_maximum_fusion.12), channel_id=1, source_target_pairs={{1,64},{64,1},{65,0},{0,65},{3,66},{66,3},{67,2},{2,67},{5,68},{68... | collective-permute-start | bytes 1179656 | tf_op jit(solution)/shard_map/ppermute | solution.py:33
  14.4 12.1 %collective-permute-start.5 = (bf16[256,768]{1,0:T(8,128)(2,1)S(1)}, bf16[256,768]{1,0:T(8,128)(2,1)S(1)}, u32[]{:S(2)}, u32[]{:S(2)}) collective-permute-start(bf16[256,768]{1,0:T(8,128)(2,1)S(1)} %collective-permute-done.2), channel_id=1, source_target_pairs={{0,1},{1,0},{64,65},{65,64},{2,3},{3,2},{66,67},{67,66},{4,5},{5,4... | collective-permute-start | bytes 1179656 | tf_op jit(solution)/shard_map/ppermute | solution.py:33
  14.5 12.2 %collective-permute-start.4 = (bf16[256,768]{1,0:T(8,128)(2,1)S(1)}, bf16[256,768]{1,0:T(8,128)(2,1)S(1)}, u32[]{:S(2)}, u32[]{:S(2)}) collective-permute-start(bf16[256,768]{1,0:T(8,128)(2,1)S(1)} %collective-permute-done.2), channel_id=1, source_target_pairs={{16,32},{32,16},{48,0},{0,48},{17,33},{33,17},{49,1},{1,49},{18,34... | collective-permute-start | bytes 1179656 | tf_op jit(solution)/shard_map/ppermute | solution.py:33
  18.1 8.6 %collective-permute-start.3 = (bf16[256,768]{1,0:T(8,128)(2,1)S(1)}, bf16[256,768]{1,0:T(8,128)(2,1)S(1)}, u32[]{:S(2)}, u32[]{:S(2)}) collective-permute-start(bf16[256,768]{1,0:T(8,128)(2,1)S(1)} %collective-permute-done.2), channel_id=1, source_target_pairs={{0,16},{16,0},{32,48},{48,32},{1,17},{17,1},{33,49},{49,33},{2,18}... | collective-permute-start | bytes 1179656 | tf_op jit(solution)/shard_map/ppermute | solution.py:33
  19.6 44.5 %collective-permute-start = (bf16[16,1,64,512]{3,2,1,0:T(8,128)(2,1)}, bf16[16,1,64,512]{3,2,1,0:T(8,128)(2,1)S(1)}, u32[]{:S(2)}, u32[]{:S(2)}) collective-permute-start(bf16[16,1,64,512]{3,2,1,0:T(8,128)(2,1)} %get-tuple-element.43), channel_id=1, source_target_pairs={{0,2},{2,4},{4,6},{6,8},{8,10},{10,12},{12,14},{14,16},{16,18},{18... | collective-permute-start | bytes 3145736 | tf_op jit(solution)/shard_map/ppermute | solution.py:173
  24.7 42.1 %collective-permute-start.1 = (bf16[16,1,64,512]{3,2,1,0:T(8,128)(2,1)}, bf16[16,1,64,512]{3,2,1,0:T(8,128)(2,1)}, u32[]{:S(2)}, u32[]{:S(2)}) collective-permute-start(bf16[16,1,64,512]{3,2,1,0:T(8,128)(2,1)} %get-tuple-element.42), channel_id=1, source_target_pairs={{2,0},{4,2},{6,4},{8,6},{10,8},{12,10},{14,12},{16,14},{18,16},{20... | collective-permute-start | bytes 3145736 | tf_op jit(solution)/shard_map/ppermute | solution.py:174
  28.6 49.0 %collective-permute-start.6 = (bf16[4,256,768]{2,1,0:T(8,128)(2,1)}, bf16[4,256,768]{2,1,0:T(8,128)(2,1)}, u32[]{:S(2)}, u32[]{:S(2)}) collective-permute-start(bf16[4,256,768]{2,1,0:T(8,128)(2,1)} %get-tuple-element.52.mine), channel_id=1, source_target_pairs={{0,2},{2,0},{1,3},{3,1},{4,6},{6,4},{5,7},{7,5},{8,10},{10,8},{9,1... | collective-permute-start | bytes 4718600 | tf_op jit(solution)/shard_map/ppermute | solution.py:33
  35.6 26.5 %all-to-all-start = ((bf16[32,10,640]{2,1,0:T(8,128)(2,1)}), bf16[32,10,640]{2,1,0:T(8,128)(2,1)}, u32[]{:S(2)}, u32[]{:S(2)}) async-start(bf16[32,10,640]{2,1,0:T(8,128)(2,1)} %reshape.104), calls=%async_computation | async-start | bytes 1310720 | tf_op jit(solution)/shard_map/all_to_all | solution.py:357
  66.8 3.3 %copy-start.4 = (bf16[9,512,256]{2,1,0:T(8,128)(2,1)S(1)}, bf16[9,512,256]{2,1,0:T(8,128)(2,1)}, u32[]{:S(2)}) copy-start(bf16[9,512,256]{2,1,0:T(8,128)(2,1)} %weights.1) | copy-start | bytes 7077892
  86.8 3.0 %copy-start.2 = (bf16[16,128,256]{2,1,0:T(8,128)(2,1)S(1)}, bf16[16,128,256]{2,1,0:T(8,128)(2,1)}, u32[]{:S(2)}) copy-start(bf16[16,128,256]{2,1,0:T(8,128)(2,1)} %copy-done.1) | copy-start | bytes 3145732
  91.2 6.3 %copy-start.5 = (bf16[16,128,512]{2,1,0:T(8,128)(2,1)}, bf16[16,128,512]{2,1,0:T(8,128)(2,1)S(1)}, u32[]{:S(2)}) copy-start(bf16[16,128,512]{2,1,0:T(8,128)(2,1)S(1)} %pad_maximum_fusion.4) | copy-start | bytes 6291460
  91.2 2.2 copy-start.11
  99.1 2.0 copy-start.7
  104.5 2.7 %copy-start.8 = (f32[2048,512]{1,0:T(8,128)S(1)}, f32[2048,512]{1,0:T(8,128)}, u32[]{:S(2)}) copy-start(f32[2048,512]{1,0:T(8,128)} %copy-done.7) | copy-start | bytes 12582916
  104.5 2.7 %slice-start = ((bf16[320,640]{1,0:T(8,128)(2,1)}), bf16[320,512]{1,0:T(8,128)(2,1)S(1)}, s32[]{:S(2)}) async-start(bf16[320,640]{1,0:T(8,128)(2,1)} %reshape.105), calls=%async_computation.2 | async-start | bytes 655360 | tf_op jit(solution)/shard_map/slice | solution.py:375
  110.9 3.5 %copy-start.6 = (bf16[16,128,512]{2,1,0:T(8,128)(2,1)S(1)}, bf16[16,128,512]{2,1,0:T(8,128)(2,1)}, u32[]{:S(2)}) copy-start(bf16[16,128,512]{2,1,0:T(8,128)(2,1)} %copy-done.5) | copy-start | bytes 6291460
  120.8 1.6 copy-start.16
  126.1 5.9 %collective-permute-start.7 = (bf16[2,256,1536]{2,1,0:T(8,128)(2,1)S(1)}, bf16[2,256,1536]{2,1,0:T(8,128)(2,1)S(1)}, u32[]{:S(2)}, u32[]{:S(2)}) collective-permute-start(bf16[2,256,1536]{2,1,0:T(8,128)(2,1)S(1)} %pad_maximum_fusion.8), channel_id=1, source_target_pairs={{0,2},{2,0},{1,3},{3,1},{4,6},{6,4},{5,7},{7,5},{8,10},{10,8},{9,1... | collective-permute-start | bytes 4718600 | tf_op jit(solution)/shard_map/ppermute | solution.py:33
  130.2 1.7 copy-start.19
  137.2 2.2 copy-start.17
  139.4 10.7 %collective-permute-start.11 = (bf16[2,256,1536]{2,1,0:T(8,128)(2,1)}, bf16[2,256,1536]{2,1,0:T(8,128)(2,1)}, u32[]{:S(2)}, u32[]{:S(2)}) collective-permute-start(bf16[2,256,1536]{2,1,0:T(8,128)(2,1)} %pad_maximum_fusion.9), channel_id=1, source_target_pairs={{0,2},{2,0},{1,3},{3,1},{4,6},{6,4},{5,7},{7,5},{8,10},{10,8},{9,1... | collective-permute-start | bytes 4718600 | tf_op jit(solution)/shard_map/ppermute | solution.py:33
  139.7 1.8 copy-start.13
  141.5 8.4 %copy-start.18 = (f32[512,1536]{1,0:T(8,128)S(1)}, f32[512,1536]{1,0:T(8,128)}, u32[]{:S(2)}) copy-start(f32[512,1536]{1,0:T(8,128)} %copy-done.17) | copy-start | bytes 9437188
  146.0 7.9 %collective-permute-start.8 = (bf16[2,64,1536]{2,1,0:T(8,128)(2,1)S(1)}, bf16[2,64,1536]{2,1,0:T(8,128)(2,1)S(1)}, u32[]{:S(2)}, u32[]{:S(2)}) collective-permute-start(bf16[2,64,1536]{2,1,0:T(8,128)(2,1)S(1)} %get-tuple-element.31), channel_id=1, source_target_pairs={{0,4},{1,5},{2,18},{3,19},{4,0},{5,1},{6,22},{7,23},{8,12},{9,13},... | collective-permute-start | bytes 1179656 | tf_op jit(solution)/shard_map/ppermute | solution.py:61
  146.1 11.4 %collective-permute-start.10 = (bf16[2,64,1536]{2,1,0:T(8,128)(2,1)S(1)}, bf16[2,64,1536]{2,1,0:T(8,128)(2,1)S(1)}, u32[]{:S(2)}, u32[]{:S(2)}) collective-permute-start(bf16[2,64,1536]{2,1,0:T(8,128)(2,1)S(1)} %get-tuple-element.32), channel_id=1, source_target_pairs={{0,8},{1,9},{2,34},{3,35},{4,12},{5,13},{6,38},{7,39},{8,0},{9,1},... | collective-permute-start | bytes 1179656 | tf_op jit(solution)/shard_map/ppermute | solution.py:61
  147.8 12.3 %collective-permute-start.9 = (bf16[2,64,1536]{2,1,0:T(8,128)(2,1)S(1)}, bf16[2,64,1536]{2,1,0:T(8,128)(2,1)S(1)}, u32[]{:S(2)}, u32[]{:S(2)}) collective-permute-start(bf16[2,64,1536]{2,1,0:T(8,128)(2,1)S(1)} %get-tuple-element.33), channel_id=1, source_target_pairs={{0,12},{1,13},{2,50},{3,51},{4,8},{5,9},{6,54},{7,55},{8,4},{9,5},... | collective-permute-start | bytes 1179656 | tf_op jit(solution)/shard_map/ppermute | solution.py:61
  152.2 9.3 %collective-permute-start.12 = (bf16[2,64,1536]{2,1,0:T(8,128)(2,1)S(1)}, bf16[2,64,1536]{2,1,0:T(8,128)(2,1)S(1)}, u32[]{:S(2)}, u32[]{:S(2)}) collective-permute-start(bf16[2,64,1536]{2,1,0:T(8,128)(2,1)S(1)} %get-tuple-element.28), channel_id=1, source_target_pairs={{0,4},{1,5},{2,18},{3,19},{4,0},{5,1},{6,22},{7,23},{8,12},{9,13},... | collective-permute-start | bytes 1179656 | tf_op jit(solution)/shard_map/ppermute | solution.py:61
  152.3 13.7 %collective-permute-start.14 = (bf16[2,64,1536]{2,1,0:T(8,128)(2,1)S(1)}, bf16[2,64,1536]{2,1,0:T(8,128)(2,1)S(1)}, u32[]{:S(2)}, u32[]{:S(2)}) collective-permute-start(bf16[2,64,1536]{2,1,0:T(8,128)(2,1)S(1)} %get-tuple-element.29), channel_id=1, source_target_pairs={{0,8},{1,9},{2,34},{3,35},{4,12},{5,13},{6,38},{7,39},{8,0},{9,1},... | collective-permute-start | bytes 1179656 | tf_op jit(solution)/shard_map/ppermute | solution.py:61
  153.9 14.6 %collective-permute-start.13 = (bf16[2,64,1536]{2,1,0:T(8,128)(2,1)S(1)}, bf16[2,64,1536]{2,1,0:T(8,128)(2,1)S(1)}, u32[]{:S(2)}, u32[]{:S(2)}) collective-permute-start(bf16[2,64,1536]{2,1,0:T(8,128)(2,1)S(1)} %get-tuple-element.30), channel_id=1, source_target_pairs={{0,12},{1,13},{2,50},{3,51},{4,8},{5,9},{6,54},{7,55},{8,4},{9,5},... | collective-permute-start | bytes 1179656 | tf_op jit(solution)/shard_map/ppermute | solution.py:61
  160.3 8.5 %copy-start.9 = (f32[2,64,1536]{2,1,0:T(8,128)}, f32[2,64,1536]{2,1,0:T(8,128)S(1)}, u32[]{:S(2)}) copy-start(f32[2,64,1536]{2,1,0:T(8,128)S(1)} %convert_add_fusion.1) | copy-start | bytes 2359300
  168.8 11.5 %copy-start.10 = (f32[2,64,1536]{2,1,0:T(8,128)S(1)}, f32[2,64,1536]{2,1,0:T(8,128)}, u32[]{:S(2)}) copy-start(f32[2,64,1536]{2,1,0:T(8,128)} %copy-done.9) | copy-start | bytes 2359300
  168.8 11.5 %collective-permute-start.15 = (bf16[4,16,1536]{2,1,0:T(8,128)(2,1)S(1)}, bf16[4,16,1536]{2,1,0:T(8,128)(2,1)S(1)}, u32[]{:S(2)}, u32[]{:S(2)}) collective-permute-start(bf16[4,16,1536]{2,1,0:T(8,128)(2,1)S(1)} %get-tuple-element.48), channel_id=1, source_target_pairs={{0,16},{1,17},{2,6},{3,7},{4,20},{5,21},{6,2},{7,3},{8,24},{9,25},... | collective-permute-start | bytes 589832 | tf_op jit(solution)/shard_map/ppermute | solution.py:61
  169.4 10.9 %collective-permute-start.16 = (bf16[4,16,1536]{2,1,0:T(8,128)(2,1)S(1)}, bf16[4,16,1536]{2,1,0:T(8,128)(2,1)S(1)}, u32[]{:S(2)}, u32[]{:S(2)}) collective-permute-start(bf16[4,16,1536]{2,1,0:T(8,128)(2,1)S(1)} %get-tuple-element.49), channel_id=1, source_target_pairs={{0,48},{1,49},{2,14},{3,15},{4,52},{5,53},{6,10},{7,11},{8,56},{9,... | collective-permute-start | bytes 589832 | tf_op jit(solution)/shard_map/ppermute | solution.py:61
  170.6 9.7 %collective-permute-start.17 = (bf16[4,16,1536]{2,1,0:T(8,128)(2,1)S(1)}, bf16[4,16,1536]{2,1,0:T(8,128)(2,1)S(1)}, u32[]{:S(2)}, u32[]{:S(2)}) collective-permute-start(bf16[4,16,1536]{2,1,0:T(8,128)(2,1)S(1)} %get-tuple-element.50), channel_id=1, source_target_pairs={{0,32},{1,33},{2,10},{3,11},{4,36},{5,37},{6,14},{7,15},{8,40},{9,... | collective-permute-start | bytes 589832 | tf_op jit(solution)/shard_map/ppermute | solution.py:61
  173.2 19.9 %all-to-all-start.1 = ((bf16[32,10,640]{2,1,0:T(8,128)(2,1)}), bf16[32,10,640]{2,1,0:T(8,128)(2,1)S(1)}, u32[]{:S(2)}, u32[]{:S(2)}) async-start(bf16[32,10,640]{2,1,0:T(8,128)(2,1)} %reshape.110), calls=%async_computation.1 | async-start | bytes 1310720 | tf_op jit(solution)/shard_map/all_to_all | solution.py:456
  180.5 12.8 %collective-permute-start.18 = (bf16[4,16,768]{2,1,0:T(8,128)(2,1)S(1)}, bf16[4,16,768]{2,1,0:T(8,128)(2,1)S(1)}, u32[]{:S(2)}, u32[]{:S(2)}) collective-permute-start(bf16[4,16,768]{2,1,0:T(8,128)(2,1)S(1)} %pad_maximum_fusion.15), channel_id=1, source_target_pairs={{0,1},{1,0},{2,3},{3,2},{4,5},{5,4},{6,7},{7,6},{8,9},{9,8},{10,11... | collective-permute-start | bytes 294920 | tf_op jit(solution)/shard_map/ppermute | solution.py:61
  182.0 11.3 %collective-permute-start.20 = (bf16[4,16,768]{2,1,0:T(8,128)(2,1)S(1)}, bf16[4,16,768]{2,1,0:T(8,128)(2,1)S(1)}, u32[]{:S(2)}, u32[]{:S(2)}) collective-permute-start(bf16[4,16,768]{2,1,0:T(8,128)(2,1)S(1)} %pad_maximum_fusion.16), channel_id=1, source_target_pairs={{0,64},{1,65},{2,66},{3,67},{4,68},{5,69},{6,70},{7,71},{8,72},{9,... | collective-permute-start | bytes 294920 | tf_op jit(solution)/shard_map/ppermute | solution.py:61
  184.5 8.8 %collective-permute-start.19 = (bf16[4,16,768]{2,1,0:T(8,128)(2,1)S(1)}, bf16[4,16,768]{2,1,0:T(8,128)(2,1)S(1)}, u32[]{:S(2)}, u32[]{:S(2)}) collective-permute-start(bf16[4,16,768]{2,1,0:T(8,128)(2,1)S(1)} %pad_maximum_fusion.16), channel_id=1, source_target_pairs={{0,65},{1,64},{2,67},{3,66},{4,69},{5,68},{6,71},{7,70},{8,73},{9,... | collective-permute-start | bytes 294920 | tf_op jit(solution)/shard_map/ppermute | solution.py:61
  193.4 5.1 %collective-permute-start.23 = (bf16[4,16,768]{2,1,0:T(8,128)(2,1)S(1)}, bf16[4,16,768]{2,1,0:T(8,128)(2,1)S(1)}, u32[]{:S(2)}, u32[]{:S(2)}) collective-permute-start(bf16[4,16,768]{2,1,0:T(8,128)(2,1)S(1)} %add_convert_fusion), channel_id=1, source_target_pairs={{0,48},{1,49},{2,14},{3,15},{4,52},{5,53},{6,10},{7,11},{8,56},{9,... | collective-permute-start | bytes 294920 | tf_op jit(solution)/shard_map/ppermute | solution.py:61
  194.8 5.3 %collective-permute-start.22 = (bf16[4,16,768]{2,1,0:T(8,128)(2,1)S(1)}, bf16[4,16,768]{2,1,0:T(8,128)(2,1)S(1)}, u32[]{:S(2)}, u32[]{:S(2)}) collective-permute-start(bf16[4,16,768]{2,1,0:T(8,128)(2,1)S(1)} %add_convert_fusion), channel_id=1, source_target_pairs={{0,32},{1,33},{2,10},{3,11},{4,36},{5,37},{6,14},{7,15},{8,40},{9,... | collective-permute-start | bytes 294920 | tf_op jit(solution)/shard_map/ppermute | solution.py:61
  195.8 4.3 %collective-permute-start.21 = (bf16[4,16,768]{2,1,0:T(8,128)(2,1)S(1)}, bf16[4,16,768]{2,1,0:T(8,128)(2,1)S(1)}, u32[]{:S(2)}, u32[]{:S(2)}) collective-permute-start(bf16[4,16,768]{2,1,0:T(8,128)(2,1)S(1)} %add_convert_fusion), channel_id=1, source_target_pairs={{0,16},{1,17},{2,6},{3,7},{4,20},{5,21},{6,2},{7,3},{8,24},{9,25},... | collective-permute-start | bytes 294920 | tf_op jit(solution)/shard_map/ppermute | solution.py:61
  200.2 8.5 %collective-permute-start.25 = (bf16[4,64,768]{2,1,0:T(8,128)(2,1)S(1)}, bf16[4,64,768]{2,1,0:T(8,128)(2,1)S(1)}, u32[]{:S(2)}, u32[]{:S(2)}) collective-permute-start(bf16[4,64,768]{2,1,0:T(8,128)(2,1)S(1)} %pad_maximum_fusion.13), channel_id=1, source_target_pairs={{0,8},{1,9},{2,34},{3,35},{4,12},{5,13},{6,38},{7,39},{8,0},{9,1},... | collective-permute-start | bytes 1179656 | tf_op jit(solution)/shard_map/ppermute | solution.py:61
  202.3 10.7 %collective-permute-start.26 = (bf16[4,64,768]{2,1,0:T(8,128)(2,1)S(1)}, bf16[4,64,768]{2,1,0:T(8,128)(2,1)S(1)}, u32[]{:S(2)}, u32[]{:S(2)}) collective-permute-start(bf16[4,64,768]{2,1,0:T(8,128)(2,1)S(1)} %pad_maximum_fusion.13), channel_id=1, source_target_pairs={{0,12},{1,13},{2,50},{3,51},{4,8},{5,9},{6,54},{7,55},{8,4},{9,5},... | collective-permute-start | bytes 1179656 | tf_op jit(solution)/shard_map/ppermute | solution.py:61
  203.1 9.8 %collective-permute-start.24 = (bf16[4,64,768]{2,1,0:T(8,128)(2,1)S(1)}, bf16[4,64,768]{2,1,0:T(8,128)(2,1)S(1)}, u32[]{:S(2)}, u32[]{:S(2)}) collective-permute-start(bf16[4,64,768]{2,1,0:T(8,128)(2,1)S(1)} %pad_maximum_fusion.13), channel_id=1, source_target_pairs={{0,4},{1,5},{2,18},{3,19},{4,0},{5,1},{6,22},{7,23},{8,12},{9,13},... | collective-permute-start | bytes 1179656 | tf_op jit(solution)/shard_map/ppermute | solution.py:61
  214.0 5.0 %copy-start.35 = (bf16[320,128]{1,0:T(8,128)(2,1)S(1)}, bf16[320,128]{1,0:T(8,128)(2,1)}, u32[]{:S(2)}) copy-start(bf16[320,128]{1,0:T(8,128)(2,1)} %get-tuple-element.18) | copy-start | bytes 245764
  216.5 12.7 %collective-permute-start.27 = (bf16[4,256,768]{2,1,0:T(8,128)(2,1)}, bf16[4,256,768]{2,1,0:T(8,128)(2,1)}, u32[]{:S(2)}, u32[]{:S(2)}) collective-permute-start(bf16[4,256,768]{2,1,0:T(8,128)(2,1)} %pad_maximum_fusion.10), channel_id=1, source_target_pairs={{0,2},{2,0},{1,3},{3,1},{4,6},{6,4},{5,7},{7,5},{8,10},{10,8},{9,1... | collective-permute-start | bytes 4718600 | tf_op jit(solution)/shard_map/ppermute | solution.py:33
  219.3 8.5 %collective-permute-start.28 = (bf16[128,640]{1,0:T(8,128)(2,1)S(1)}, bf16[128,640]{1,0:T(8,128)(2,1)S(1)}, u32[]{:S(2)}, u32[]{:S(2)}) collective-permute-start(bf16[128,640]{1,0:T(8,128)(2,1)S(1)} %pad_maximum_fusion.14), channel_id=1, source_target_pairs={{0,64},{64,0},{1,65},{65,1},{2,66},{66,2},{3,67},{67,3},{4,68},{68... | collective-permute-start | bytes 491528 | tf_op jit(solution)/shard_map/ppermute | solution.py:462
  (20 other events, 24.5 us)

commit v5 on v4

--- a/solution.py
+++ b/solution.py
@@ -155,11 +155,12 @@
     parts = [part, swap(part, "z", 0), swap(part, "z", 1), swap(part, "y", 0)]
     mine = jnp.stack(parts)
     other = swap(mine, "core", 0)
-    both = jnp.stack([mine, other])
 
     def block(half, group):
-        index = (half ^ core, group ^ color, 0, 0)
-        return lax.dynamic_slice(both, index, (1, 1, rows, 3 * cols))[0, 0]
+        first, second = (
+            lax.dynamic_index_in_dim(value, group ^ color, 0, False) for value in (mine, other)
+        )
+        return jnp.where(half == core, first, second)
 
     return block, mine, other, jnp.stack([core, color]).astype(jnp.int32)
 
@@ -366,14 +367,16 @@
         frames_in.reshape(-1, channels),
         jnp.concatenate([frames_in[:, 1:], high], axis=1).reshape(-1, channels),
     ]
+
     near_out = convolve(near_body, low, frames_in, high, (spatial_weight,))
     far_out = convolve(
         far_body, low, frames_in, high, (mine_blocks, other_blocks), (place,)
     )
-    far_out, held = lax.optimization_barrier((far_out, held))
+    far_out, slot_weight, extras = lax.optimization_barrier(
+        (far_out, held[:, :channels], held[:, channels:])
+    )
     spatial_out = jnp.concatenate([near_out, far_out], axis=2)
-    slot_weight = held[:, :channels]
-    extras = held[:, channels : channels + 8 + frames].astype(F32)
+    extras = extras[:, : 8 + frames].astype(F32)
     slot_bias = extras[:, :1]
     slot_cell = jnp.where(extras[:, 2:3] > 0.5, extras[:, 1:2].astype(jnp.int32), cells)
     slot_spikes = extras[:, 8:]

time: 240 us -> 229 us (0.954)
  other arithmetic: 30.1 us -> 24.4 us
  local copies, waits for them, and re-layouts: 34.9 us -> 29.8 us
    unnamed x83 -> x57, local copies, waits for them, and re-layouts: 12.2 us -> 8.26 us
where the time goes in v5:
time: 229 us; the launch traced here: 226 us
  starting transfers between devices  67.4 us (29%)
  waiting for transfers between devices  54.4 us (24%)
  matrix products  31.3 us (14%)
  local copies, waits for them, and re-layouts  29.8 us (13%)
  other arithmetic  24.4 us (11%)
  Pallas kernels  16.6 us (7%)
    ppermute x18, waiting for transfers between devices, permute_by_core(): return lax.ppermute(value, ALL, perm)  25.4 us
    ppermute x18, starting transfers between devices, permute_by_core(): return lax.ppermute(value, ALL, perm)  21.7 us
    dot_general x6, matrix products, contract_rows(): lax.dot_general(left, right, (((0,), (0,)), ((), ())), preferred_element_...  17.4 us
    pallas_call x2, Pallas kernels, convolve(): pl.pallas_call(body, grid_spec=pltpu.PrefetchScalarGridSpec(num_scalar_pr...  14.5 us
    ppermute x8, starting transfers between devices, swap(): return lax.ppermute(value, name, perm)  14 us
    all_to_all x1, starting transfers between devices, compute(): lax.all_to_all(packed.reshape(tile_count, capacity, PACK), TILE, split_ax...  13.6 us
    ppermute x8, waiting for transfers between devices, swap(): return lax.ppermute(value, name, perm)  8.87 us
    all_to_all x1, waiting for transfers between devices, compute(): lax.all_to_all(back.reshape(tile_count, capacity, PACK), TILE, split_axis...  8.32 us
  transfers between devices with their start and end apart: 31, of which 14 were waited for; matrix products, arithmetic and copies ran while one was open for 15% of the time, Pallas kernels for 4%

profile of v5, /device:TPU:1, one launch (start us, length us, event | category | flops | bytes accessed | tf_op | source)
XLA Modules:
  0.0 225.8 jit_solution(2041864558949468552)
XLA Ops:
  2.1 3.6 %collective-permute-start.2 = (bf16[256,768]{1,0:T(8,128)(2,1)S(1)}, bf16[256,768]{1,0:T(8,128)(2,1)S(1)}, u32[]{:S(2)}, u32[]{:S(2)}) collective-permute-start(bf16[256,768]{1,0:T(8,128)(2,1)S(1)} %pad_maximum_fusion.12), channel_id=1, source_target_pairs={{1,64},{64,1},{65,0},{0,65},{3,66},{66,3},{67,2},{2,67},{5,68},{68... | collective-permute-start | bytes 1179656 | tf_op jit(solution)/shard_map/ppermute | solution.py:33
  5.7 8.7 %collective-permute-done.2 = bf16[256,768]{1,0:T(8,128)(2,1)S(1)} collective-permute-done((bf16[256,768]{1,0:T(8,128)(2,1)S(1)}, bf16[256,768]{1,0:T(8,128)(2,1)S(1)}, u32[]{:S(2)}, u32[]{:S(2)}) %collective-permute-start.2) | collective-permute-done | bytes 393248 | tf_op jit(solution)/shard_map/ppermute | solution.py:33
  14.5 3.6 %collective-permute-start.4 = (bf16[256,768]{1,0:T(8,128)(2,1)S(1)}, bf16[256,768]{1,0:T(8,128)(2,1)S(1)}, u32[]{:S(2)}, u32[]{:S(2)}) collective-permute-start(bf16[256,768]{1,0:T(8,128)(2,1)S(1)} %collective-permute-done.2), channel_id=1, source_target_pairs={{16,32},{32,16},{48,0},{0,48},{17,33},{33,17},{49,1},{1,49},{18,34... | collective-permute-start | bytes 1179656 | tf_op jit(solution)/shard_map/ppermute | solution.py:33
  19.6 5.0 %collective-permute-start = (bf16[16,1,64,512]{3,2,1,0:T(8,128)(2,1)}, bf16[16,1,64,512]{3,2,1,0:T(8,128)(2,1)S(1)}, u32[]{:S(2)}, u32[]{:S(2)}) collective-permute-start(bf16[16,1,64,512]{3,2,1,0:T(8,128)(2,1)} %get-tuple-element.45), channel_id=1, source_target_pairs={{0,2},{2,4},{4,6},{6,8},{8,10},{10,12},{12,14},{14,16},{16,18},{18... | collective-permute-start | bytes 3145736 | tf_op jit(solution)/shard_map/ppermute | solution.py:174
  24.6 1.9 collective-permute-start.1
  26.9 3.0 %collective-permute-start.6 = (bf16[4,256,768]{2,1,0:T(8,128)(2,1)S(1)}, bf16[4,256,768]{2,1,0:T(8,128)(2,1)}, u32[]{:S(2)}, u32[]{:S(2)}) collective-permute-start(bf16[4,256,768]{2,1,0:T(8,128)(2,1)S(1)} %pad_maximum_fusion.7.mine), channel_id=1, source_target_pairs={{0,2},{2,0},{1,3},{3,1},{4,6},{6,4},{5,7},{7,5},{8,10},{10,8},{9,1... | collective-permute-start | bytes 4718600 | tf_op jit(solution)/shard_map/ppermute | solution.py:33
  29.9 2.1 pack.1
  32.0 2.0 reshape.108
  34.0 13.6 %all-to-all-start = ((bf16[32,10,640]{2,1,0:T(8,128)(2,1)}), bf16[32,10,640]{2,1,0:T(8,128)(2,1)S(1)}, u32[]{:S(2)}, u32[]{:S(2)}) async-start(bf16[32,10,640]{2,1,0:T(8,128)(2,1)} %reshape.108), calls=%async_computation | async-start | bytes 1310720 | tf_op jit(solution)/shard_map/all_to_all | solution.py:358
  47.6 1.9 fusion.103
  49.6 1.7 dynamic-slice_bitcast_fusion.9
  51.3 1.8 dynamic-slice_bitcast_fusion.5
  53.1 7.2 %all-to-all-done = bf16[32,10,640]{2,1,0:T(8,128)(2,1)S(1)} async-done(((bf16[32,10,640]{2,1,0:T(8,128)(2,1)}), bf16[32,10,640]{2,1,0:T(8,128)(2,1)S(1)}, u32[]{:S(2)}, u32[]{:S(2)}) %all-to-all-start) | async-done | bytes 409632 | tf_op jit(solution)/shard_map/all_to_all | solution.py:358
  63.3 2.9 %pad_maximum_fusion.5 = bf16[16,2,64,512]{3,2,1,0:T(8,128)(2,1)} fusion(bf16[16,1,64,512]{3,2,1,0:T(8,128)(2,1)} %get-tuple-element.44, bf16[16,1,64,512]{3,2,1,0:T(8,128)(2,1)S(1)} %collective-permute-done.low), kind=kLoop, calls=%fused_computation.37 | loop fusion | flops 1048576 | bytes 4194304 | tf_op jit(solution)/shard_map/concatenate | solution.py:366
  66.2 3.2 %pad_maximum_fusion.6 = bf16[16,2,64,512]{3,2,1,0:T(8,128)(2,1)} fusion(bf16[16,1,64,512]{3,2,1,0:T(8,128)(2,1)} %collective-permute-done.1.high, bf16[16,1,64,512]{3,2,1,0:T(8,128)(2,1)} %get-tuple-element.45), kind=kLoop, calls=%fused_computation.38 | loop fusion | flops 1048576 | bytes 4194304 | tf_op jit(solution)/shard_map/concatenate | solution.py:368
  69.4 6.6 %conv.3 = bf16[16,128,256]{2,1,0:T(8,128)(2,1)S(1)} custom-call(bf16[16,1,64,512]{3,2,1,0:T(8,128)(2,1)S(1)} %collective-permute-done.low, bf16[16,2,64,512]{3,2,1,0:T(8,128)(2,1)S(1)} %bitcast.144, bf16[16,1,64,512]{3,2,1,0:T(8,128)(2,1)} %collective-permute-done.1.high, bf16[9,512,256]{2,1,0:T(8,128)(2,1)S(1)} %copy-done.3), custom_call_target="tpu_custom_call" | custom-call | flops 4831838208 | bytes 7602176 | tf_op jit(solution)/shard_map/conv/pallas_call | solution.py:248
  76.0 8.0 %conv.2 = bf16[16,128,256]{2,1,0:T(8,128)(2,1)S(1)} custom-call(s32[2]{0:T(128)S(1)} %pad_add_fusion.place, bf16[16,1,64,512]{3,2,1,0:T(8,128)(2,1)S(1)} %collective-permute-done.low, bf16[16,2,64,512]{3,2,1,0:T(8,128)(2,1)S(1)} %bitcast.145, bf16[16,1,64,512]{3,2,1,0:T(8,128)(2,1)} %collective-permute-done.1.high, ...), custom_call_target="tpu_custom_call" | custom-call | flops 4831838208 | bytes 7602176 | tf_op jit(solution)/shard_map/conv/pallas_call | solution.py:248
  90.5 2.0 convolution_bitcast_fusion
  94.2 1.6 broadcast_select_fusion.2
  98.6 2.5 %fusion.3 = bf16[2048,512]{1,0:T(8,128)(2,1)S(1)} fusion(f32[2048,512]{1,0:T(8,128)S(1)} %copy-done.7, bf16[320,2048]{1,0:T(8,128)(2,1)S(1)} %bitcast.165, bf16[320,2048]{1,0:T(8,128)(2,1)S(1)} %bitcast.166, bf16[320,512]{1,0:T(8,128)(2,1)S(1)} %slice.251), kind=kOutput, calls=%fused_computation.8 | convolution fusion | flops 1353973760 | bytes 9240576 | tf_op jit(solution)/shard_map/dot_general | solution.py:21
  101.6 3.5 %convolution_convert_fusion = bf16[2048,512]{1,0:T(8,128)(2,1)S(1)} fusion(bf16[2048,512]{1,0:T(8,128)(2,1)S(1)} %bitcast.161, bf16[2048,512]{1,0:T(8,128)(2,1)S(1)} %bitcast.159, bf16[2048,512]{1,0:T(8,128)(2,1)S(1)} %fusion.3, bf16[256,256]{1,0:T(8,128)(2,1)S(1)} %get-tuple-element.91, bf16[256,256]{1,0:T(8,128)(2,1)S(1)} %copy-done.20, ...), kind=kOutput, calls=%fused_computation.18 | convolution fusion | flops 3260022784 | bytes 9961472 | tf_op jit(solution)/shard_map/dot_general | solution.py:441
  105.1 3.5 %fusion.7 = f32[512,1536]{1,0:T(8,128)S(1)} fusion(bf16[2048,512]{1,0:T(8,128)(2,1)S(1)} %bitcast.148, bf16[2048,512]{1,0:T(8,128)(2,1)S(1)} %bitcast.162, bf16[2048,512]{1,0:T(8,128)(2,1)S(1)} %bitcast.160, bf16[2048,512]{1,0:T(8,128)(2,1)S(1)} %fusion.3), kind=kOutput, calls=%fused_computation.23 | convolution fusion | flops 3240099840 | bytes 11534336 | tf_op jit(solution)/shard_map/dot_general | solution.py:21
  113.1 3.5 %fusion.108 = f32[512,1536]{1,0:T(8,128)S(1)} fusion(bf16[2048,512]{1,0:T(8,128)(2,1)S(1)} %bitcast.164, bf16[2048,1536]{1,0:T(8,128)(2,1)S(1)} %pad_maximum_fusion.1), kind=kOutput, calls=%fused_computation.219 | convolution fusion | flops 3221225472 | bytes 11534336 | tf_op jit(solution)/shard_map/dot_general | solution.py:21
  118.2 3.5 %fusion.109 = f32[1536,512]{0,1:T(8,128)S(1)} fusion(bf16[2048,1536]{1,0:T(8,128)(2,1)S(1)} %pad_maximum_fusion.1, bf16[2048,512]{1,0:T(8,128)(2,1)S(1)} %bitcast.146), kind=kOutput, calls=%fused_computation.220 | convolution fusion | flops 3221225472 | bytes 11534336 | tf_op jit(solution)/shard_map/dot_general | solution.py:21
  121.6 1.7 copy-done.16
  125.2 3.5 %fusion.110 = f32[512,1536]{1,0:T(8,128)S(1)} fusion(bf16[2048,512]{1,0:T(8,128)(2,1)S(1)} %bitcast.163, bf16[2048,1536]{1,0:T(8,128)(2,1)S(1)} %pad_maximum_fusion.1), kind=kOutput, calls=%fused_computation.221 | convolution fusion | flops 3221225472 | bytes 11534336 | tf_op jit(solution)/shard_map/dot_general | solution.py:21
  131.8 1.6 dynamic-slice_bitcast_fusion.1
  133.4 4.3 %convolution_convert_fusion.1 = bf16[320,512]{1,0:T(8,128)(2,1)S(1)} fusion(bf16[40,8,16,128]{3,2,1,0:T(8,128)(2,1)S(1)} %bitcast.156, f32[2048,512]{1,0:T(8,128)} %copy-done.6), kind=kOutput, calls=%fused_computation.81 | convolution fusion | flops 675446784 | bytes 5832704 | tf_op jit(solution)/shard_map/dot_general | solution.py:433
  139.6 2.2 collective-permute-start.9
  142.0 1.9 maximum_add_fusion.1
  145.7 2.2 collective-permute-start.13
  149.3 2.6 %collective-permute-done.9 = bf16[2,64,1536]{2,1,0:T(8,128)(2,1)S(1)} collective-permute-done((bf16[2,64,1536]{2,1,0:T(8,128)(2,1)S(1)}, bf16[2,64,1536]{2,1,0:T(8,128)(2,1)S(1)}, u32[]{:S(2)}, u32[]{:S(2)}) %collective-permute-start.9) | collective-permute-done | bytes 393248 | tf_op jit(solution)/shard_map/ppermute | solution.py:61
  153.4 4.4 %collective-permute-done.14 = bf16[2,64,1536]{2,1,0:T(8,128)(2,1)S(1)} collective-permute-done((bf16[2,64,1536]{2,1,0:T(8,128)(2,1)S(1)}, bf16[2,64,1536]{2,1,0:T(8,128)(2,1)S(1)}, u32[]{:S(2)}, u32[]{:S(2)}) %collective-permute-start.14) | collective-permute-done | bytes 393248 | tf_op jit(solution)/shard_map/ppermute | solution.py:61
  157.8 2.6 %collective-permute-done.13 = bf16[2,64,1536]{2,1,0:T(8,128)(2,1)S(1)} collective-permute-done((bf16[2,64,1536]{2,1,0:T(8,128)(2,1)S(1)}, bf16[2,64,1536]{2,1,0:T(8,128)(2,1)S(1)}, u32[]{:S(2)}, u32[]{:S(2)}) %collective-permute-start.13) | collective-permute-done | bytes 393248 | tf_op jit(solution)/shard_map/ppermute | solution.py:61
  162.2 1.7 collective-permute-start.17
  165.0 7.2 %all-to-all-start.1 = ((bf16[32,10,640]{2,1,0:T(8,128)(2,1)}), bf16[32,10,640]{2,1,0:T(8,128)(2,1)S(1)}, u32[]{:S(2)}, u32[]{:S(2)}) async-start(bf16[32,10,640]{2,1,0:T(8,128)(2,1)} %reshape.114), calls=%async_computation.1 | async-start | bytes 1310720 | tf_op jit(solution)/shard_map/all_to_all | solution.py:459
  173.9 2.4 %collective-permute-start.20 = (bf16[4,16,768]{2,1,0:T(8,128)(2,1)S(1)}, bf16[4,16,768]{2,1,0:T(8,128)(2,1)S(1)}, u32[]{:S(2)}, u32[]{:S(2)}) collective-permute-start(bf16[4,16,768]{2,1,0:T(8,128)(2,1)S(1)} %pad_maximum_fusion.16), channel_id=1, source_target_pairs={{0,64},{1,65},{2,66},{3,67},{4,68},{5,69},{6,70},{7,71},{8,72},{9,... | collective-permute-start | bytes 294920 | tf_op jit(solution)/shard_map/ppermute | solution.py:61
  176.7 8.3 %all-to-all-done.1 = bf16[32,10,640]{2,1,0:T(8,128)(2,1)S(1)} async-done(((bf16[32,10,640]{2,1,0:T(8,128)(2,1)}), bf16[32,10,640]{2,1,0:T(8,128)(2,1)S(1)}, u32[]{:S(2)}, u32[]{:S(2)}) %all-to-all-start.1) | async-done | bytes 409632 | tf_op jit(solution)/shard_map/all_to_all | solution.py:459
  188.6 1.7 collective-permute-done.23
  190.3 1.7 collective-permute-done.22
  192.1 2.0 collective-permute-start.25
  195.0 5.7 %collective-permute-done.25 = bf16[4,64,768]{2,1,0:T(8,128)(2,1)S(1)} collective-permute-done((bf16[4,64,768]{2,1,0:T(8,128)(2,1)S(1)}, bf16[4,64,768]{2,1,0:T(8,128)(2,1)S(1)}, u32[]{:S(2)}, u32[]{:S(2)}) %collective-permute-start.25) | collective-permute-done | bytes 393248 | tf_op jit(solution)/shard_map/ppermute | solution.py:61
  200.7 4.2 %collective-permute-done.26 = bf16[4,64,768]{2,1,0:T(8,128)(2,1)S(1)} collective-permute-done((bf16[4,64,768]{2,1,0:T(8,128)(2,1)S(1)}, bf16[4,64,768]{2,1,0:T(8,128)(2,1)S(1)}, u32[]{:S(2)}, u32[]{:S(2)}) %collective-permute-start.26) | collective-permute-done | bytes 393248 | tf_op jit(solution)/shard_map/ppermute | solution.py:61
  205.5 2.5 %collective-permute-start.27 = (bf16[4,256,768]{2,1,0:T(8,128)(2,1)S(1)}, bf16[4,256,768]{2,1,0:T(8,128)(2,1)}, u32[]{:S(2)}, u32[]{:S(2)}) collective-permute-start(bf16[4,256,768]{2,1,0:T(8,128)(2,1)S(1)} %pad_maximum_fusion.10), channel_id=1, source_target_pairs={{0,2},{2,0},{1,3},{3,1},{4,6},{6,4},{5,7},{7,5},{8,10},{10,8},{9,1... | collective-permute-start | bytes 4718600 | tf_op jit(solution)/shard_map/ppermute | solution.py:33
  209.3 3.9 %collective-permute-start.28 = (bf16[128,640]{1,0:T(8,128)(2,1)S(1)}, bf16[128,640]{1,0:T(8,128)(2,1)S(1)}, u32[]{:S(2)}, u32[]{:S(2)}) collective-permute-start(bf16[128,640]{1,0:T(8,128)(2,1)S(1)} %pad_maximum_fusion.14), channel_id=1, source_target_pairs={{0,64},{64,0},{1,65},{65,1},{2,66},{66,2},{3,67},{67,3},{4,68},{68... | collective-permute-start | bytes 491528 | tf_op jit(solution)/shard_map/ppermute | solution.py:465
  213.2 4.6 %collective-permute-done.28 = bf16[128,640]{1,0:T(8,128)(2,1)S(1)} collective-permute-done((bf16[128,640]{1,0:T(8,128)(2,1)S(1)}, bf16[128,640]{1,0:T(8,128)(2,1)S(1)}, u32[]{:S(2)}, u32[]{:S(2)}) %collective-permute-start.28) | collective-permute-done | bytes 163872 | tf_op jit(solution)/shard_map/ppermute | solution.py:465
  219.1 2.0 broadcast_select_fusion
  221.6 2.6 %stack.156 = f32[9,512,256]{2,1,0:T(8,128)} convert(bf16[9,512,256]{2,1,0:T(8,128)(2,1)S(1)} %fusion.80) | non-fusion elementwise | flops 1179648 | bytes 7077888 | tf_op jit(solution)/shard_map/stack | solution.py:475
  (168 shorter events, 49.4 us)
Async XLA Ops:
  0.6 17.5 %copy-start = (bf16[1,1,16,2,64,512]{5,4,3,2,1,0:T(8,128)(2,1)S(1)}, bf16[1,1,16,2,64,512]{5,4,3,2,1,0:T(8,128)(2,1)}, u32[]{:S(2)}) copy-start(bf16[1,1,16,2,64,512]{5,4,3,2,1,0:T(8,128)(2,1)} %param.9) | copy-start | bytes 6291460
  2.1 12.3 %collective-permute-start.2 = (bf16[256,768]{1,0:T(8,128)(2,1)S(1)}, bf16[256,768]{1,0:T(8,128)(2,1)S(1)}, u32[]{:S(2)}, u32[]{:S(2)}) collective-permute-start(bf16[256,768]{1,0:T(8,128)(2,1)S(1)} %pad_maximum_fusion.12), channel_id=1, source_target_pairs={{1,64},{64,1},{65,0},{0,65},{3,66},{66,3},{67,2},{2,67},{5,68},{68... | collective-permute-start | bytes 1179656 | tf_op jit(solution)/shard_map/ppermute | solution.py:33
  14.5 12.1 %collective-permute-start.5 = (bf16[256,768]{1,0:T(8,128)(2,1)S(1)}, bf16[256,768]{1,0:T(8,128)(2,1)S(1)}, u32[]{:S(2)}, u32[]{:S(2)}) collective-permute-start(bf16[256,768]{1,0:T(8,128)(2,1)S(1)} %collective-permute-done.2), channel_id=1, source_target_pairs={{0,1},{1,0},{64,65},{65,64},{2,3},{3,2},{66,67},{67,66},{4,5},{5,4... | collective-permute-start | bytes 1179656 | tf_op jit(solution)/shard_map/ppermute | solution.py:33
  14.5 12.1 %collective-permute-start.4 = (bf16[256,768]{1,0:T(8,128)(2,1)S(1)}, bf16[256,768]{1,0:T(8,128)(2,1)S(1)}, u32[]{:S(2)}, u32[]{:S(2)}) collective-permute-start(bf16[256,768]{1,0:T(8,128)(2,1)S(1)} %collective-permute-done.2), channel_id=1, source_target_pairs={{16,32},{32,16},{48,0},{0,48},{17,33},{33,17},{49,1},{1,49},{18,34... | collective-permute-start | bytes 1179656 | tf_op jit(solution)/shard_map/ppermute | solution.py:33
  18.1 8.6 %collective-permute-start.3 = (bf16[256,768]{1,0:T(8,128)(2,1)S(1)}, bf16[256,768]{1,0:T(8,128)(2,1)S(1)}, u32[]{:S(2)}, u32[]{:S(2)}) collective-permute-start(bf16[256,768]{1,0:T(8,128)(2,1)S(1)} %collective-permute-done.2), channel_id=1, source_target_pairs={{0,16},{16,0},{32,48},{48,32},{1,17},{17,1},{33,49},{49,33},{2,18}... | collective-permute-start | bytes 1179656 | tf_op jit(solution)/shard_map/ppermute | solution.py:33
  19.6 43.7 %collective-permute-start = (bf16[16,1,64,512]{3,2,1,0:T(8,128)(2,1)}, bf16[16,1,64,512]{3,2,1,0:T(8,128)(2,1)S(1)}, u32[]{:S(2)}, u32[]{:S(2)}) collective-permute-start(bf16[16,1,64,512]{3,2,1,0:T(8,128)(2,1)} %get-tuple-element.45), channel_id=1, source_target_pairs={{0,2},{2,4},{4,6},{6,8},{8,10},{10,12},{12,14},{14,16},{16,18},{18... | collective-permute-start | bytes 3145736 | tf_op jit(solution)/shard_map/ppermute | solution.py:174
  24.6 41.6 %collective-permute-start.1 = (bf16[16,1,64,512]{3,2,1,0:T(8,128)(2,1)}, bf16[16,1,64,512]{3,2,1,0:T(8,128)(2,1)}, u32[]{:S(2)}, u32[]{:S(2)}) collective-permute-start(bf16[16,1,64,512]{3,2,1,0:T(8,128)(2,1)} %get-tuple-element.44), channel_id=1, source_target_pairs={{2,0},{4,2},{6,4},{8,6},{10,8},{12,10},{14,12},{16,14},{18,16},{20... | collective-permute-start | bytes 3145736 | tf_op jit(solution)/shard_map/ppermute | solution.py:175
  26.9 49.1 %collective-permute-start.6 = (bf16[4,256,768]{2,1,0:T(8,128)(2,1)S(1)}, bf16[4,256,768]{2,1,0:T(8,128)(2,1)}, u32[]{:S(2)}, u32[]{:S(2)}) collective-permute-start(bf16[4,256,768]{2,1,0:T(8,128)(2,1)S(1)} %pad_maximum_fusion.7.mine), channel_id=1, source_target_pairs={{0,2},{2,0},{1,3},{3,1},{4,6},{6,4},{5,7},{7,5},{8,10},{10,8},{9,1... | collective-permute-start | bytes 4718600 | tf_op jit(solution)/shard_map/ppermute | solution.py:33
  34.0 26.4 %all-to-all-start = ((bf16[32,10,640]{2,1,0:T(8,128)(2,1)}), bf16[32,10,640]{2,1,0:T(8,128)(2,1)S(1)}, u32[]{:S(2)}, u32[]{:S(2)}) async-start(bf16[32,10,640]{2,1,0:T(8,128)(2,1)} %reshape.108), calls=%async_computation | async-start | bytes 1310720 | tf_op jit(solution)/shard_map/all_to_all | solution.py:358
  63.3 6.2 %copy-start.3 = (bf16[9,512,256]{2,1,0:T(8,128)(2,1)S(1)}, bf16[9,512,256]{2,1,0:T(8,128)(2,1)}, u32[]{:S(2)}) copy-start(bf16[9,512,256]{2,1,0:T(8,128)(2,1)} %weights.1) | copy-start | bytes 7077892
  66.2 3.2 %copy-start.1 = (bf16[1,1,16,2,64,512]{5,4,3,2,1,0:T(8,128)(2,1)S(1)}, bf16[1,1,16,2,64,512]{5,4,3,2,1,0:T(8,128)(2,1)}, u32[]{:S(2)}) copy-start(bf16[1,1,16,2,64,512]{5,4,3,2,1,0:T(8,128)(2,1)} %param.9) | copy-start | bytes 6291460
  84.4 4.6 %copy-start.4 = (bf16[16,128,512]{2,1,0:T(8,128)(2,1)}, bf16[16,128,512]{2,1,0:T(8,128)(2,1)S(1)}, u32[]{:S(2)}) copy-start(bf16[16,128,512]{2,1,0:T(8,128)(2,1)S(1)} %pad_maximum_fusion.4) | copy-start | bytes 6291460
  84.9 1.4 copy-start.19
  90.5 2.0 copy-start.6
  95.9 2.7 %copy-start.7 = (f32[2048,512]{1,0:T(8,128)S(1)}, f32[2048,512]{1,0:T(8,128)}, u32[]{:S(2)}) copy-start(f32[2048,512]{1,0:T(8,128)} %copy-done.6) | copy-start | bytes 12582916
  101.6 3.5 %copy-start.5 = (bf16[16,128,512]{2,1,0:T(8,128)(2,1)S(1)}, bf16[16,128,512]{2,1,0:T(8,128)(2,1)}, u32[]{:S(2)}) copy-start(bf16[16,128,512]{2,1,0:T(8,128)(2,1)} %copy-done.4) | copy-start | bytes 6291460
  111.5 1.6 copy-start.13
  116.6 1.6 copy-start.2
  116.8 6.8 %collective-permute-start.7 = (bf16[2,256,1536]{2,1,0:T(8,128)(2,1)S(1)}, bf16[2,256,1536]{2,1,0:T(8,128)(2,1)S(1)}, u32[]{:S(2)}, u32[]{:S(2)}) collective-permute-start(bf16[2,256,1536]{2,1,0:T(8,128)(2,1)S(1)} %pad_maximum_fusion.8), channel_id=1, source_target_pairs={{0,2},{2,0},{1,3},{3,1},{4,6},{6,4},{5,7},{7,5},{8,10},{10,8},{9,1... | collective-permute-start | bytes 4718600 | tf_op jit(solution)/shard_map/ppermute | solution.py:33
  121.6 1.7 copy-start.16
  123.6 1.6 copy-start.12
  128.7 2.2 copy-start.14
  130.9 11.1 %collective-permute-start.11 = (bf16[2,256,1536]{2,1,0:T(8,128)(2,1)}, bf16[2,256,1536]{2,1,0:T(8,128)(2,1)}, u32[]{:S(2)}, u32[]{:S(2)}) collective-permute-start(bf16[2,256,1536]{2,1,0:T(8,128)(2,1)} %pad_maximum_fusion.9), channel_id=1, source_target_pairs={{0,2},{2,0},{1,3},{3,1},{4,6},{6,4},{5,7},{7,5},{8,10},{10,8},{9,1... | collective-permute-start | bytes 4718600 | tf_op jit(solution)/shard_map/ppermute | solution.py:33
  131.6 1.8 copy-start.11
  133.4 8.4 %copy-start.15 = (f32[512,1536]{1,0:T(8,128)S(1)}, f32[512,1536]{1,0:T(8,128)}, u32[]{:S(2)}) copy-start(f32[512,1536]{1,0:T(8,128)} %copy-done.14) | copy-start | bytes 9437188
  137.9 7.9 %collective-permute-start.8 = (bf16[2,64,1536]{2,1,0:T(8,128)(2,1)S(1)}, bf16[2,64,1536]{2,1,0:T(8,128)(2,1)S(1)}, u32[]{:S(2)}, u32[]{:S(2)}) collective-permute-start(bf16[2,64,1536]{2,1,0:T(8,128)(2,1)S(1)} %get-tuple-element.33), channel_id=1, source_target_pairs={{0,4},{1,5},{2,18},{3,19},{4,0},{5,1},{6,22},{7,23},{8,12},{9,13},... | collective-permute-start | bytes 1179656 | tf_op jit(solution)/shard_map/ppermute | solution.py:61
  138.0 11.3 %collective-permute-start.10 = (bf16[2,64,1536]{2,1,0:T(8,128)(2,1)S(1)}, bf16[2,64,1536]{2,1,0:T(8,128)(2,1)S(1)}, u32[]{:S(2)}, u32[]{:S(2)}) collective-permute-start(bf16[2,64,1536]{2,1,0:T(8,128)(2,1)S(1)} %get-tuple-element.34), channel_id=1, source_target_pairs={{0,8},{1,9},{2,34},{3,35},{4,12},{5,13},{6,38},{7,39},{8,0},{9,1},... | collective-permute-start | bytes 1179656 | tf_op jit(solution)/shard_map/ppermute | solution.py:61
  139.6 12.3 %collective-permute-start.9 = (bf16[2,64,1536]{2,1,0:T(8,128)(2,1)S(1)}, bf16[2,64,1536]{2,1,0:T(8,128)(2,1)S(1)}, u32[]{:S(2)}, u32[]{:S(2)}) collective-permute-start(bf16[2,64,1536]{2,1,0:T(8,128)(2,1)S(1)} %get-tuple-element.35), channel_id=1, source_target_pairs={{0,12},{1,13},{2,50},{3,51},{4,8},{5,9},{6,54},{7,55},{8,4},{9,5},... | collective-permute-start | bytes 1179656 | tf_op jit(solution)/shard_map/ppermute | solution.py:61
  144.0 9.3 %collective-permute-start.12 = (bf16[2,64,1536]{2,1,0:T(8,128)(2,1)S(1)}, bf16[2,64,1536]{2,1,0:T(8,128)(2,1)S(1)}, u32[]{:S(2)}, u32[]{:S(2)}) collective-permute-start(bf16[2,64,1536]{2,1,0:T(8,128)(2,1)S(1)} %get-tuple-element.30), channel_id=1, source_target_pairs={{0,4},{1,5},{2,18},{3,19},{4,0},{5,1},{6,22},{7,23},{8,12},{9,13},... | collective-permute-start | bytes 1179656 | tf_op jit(solution)/shard_map/ppermute | solution.py:61
  144.1 13.6 %collective-permute-start.14 = (bf16[2,64,1536]{2,1,0:T(8,128)(2,1)S(1)}, bf16[2,64,1536]{2,1,0:T(8,128)(2,1)S(1)}, u32[]{:S(2)}, u32[]{:S(2)}) collective-permute-start(bf16[2,64,1536]{2,1,0:T(8,128)(2,1)S(1)} %get-tuple-element.31), channel_id=1, source_target_pairs={{0,8},{1,9},{2,34},{3,35},{4,12},{5,13},{6,38},{7,39},{8,0},{9,1},... | collective-permute-start | bytes 1179656 | tf_op jit(solution)/shard_map/ppermute | solution.py:61
  145.7 14.6 %collective-permute-start.13 = (bf16[2,64,1536]{2,1,0:T(8,128)(2,1)S(1)}, bf16[2,64,1536]{2,1,0:T(8,128)(2,1)S(1)}, u32[]{:S(2)}, u32[]{:S(2)}) collective-permute-start(bf16[2,64,1536]{2,1,0:T(8,128)(2,1)S(1)} %get-tuple-element.32), channel_id=1, source_target_pairs={{0,12},{1,13},{2,50},{3,51},{4,8},{5,9},{6,54},{7,55},{8,4},{9,5},... | collective-permute-start | bytes 1179656 | tf_op jit(solution)/shard_map/ppermute | solution.py:61
  152.1 8.5 %copy-start.8 = (f32[2,64,1536]{2,1,0:T(8,128)}, f32[2,64,1536]{2,1,0:T(8,128)S(1)}, u32[]{:S(2)}) copy-start(f32[2,64,1536]{2,1,0:T(8,128)S(1)} %convert_add_fusion.1) | copy-start | bytes 2359300
  160.6 11.6 %copy-start.9 = (f32[2,64,1536]{2,1,0:T(8,128)S(1)}, f32[2,64,1536]{2,1,0:T(8,128)}, u32[]{:S(2)}) copy-start(f32[2,64,1536]{2,1,0:T(8,128)} %copy-done.8) | copy-start | bytes 2359300
  160.6 11.6 %collective-permute-start.15 = (bf16[4,16,1536]{2,1,0:T(8,128)(2,1)S(1)}, bf16[4,16,1536]{2,1,0:T(8,128)(2,1)S(1)}, u32[]{:S(2)}, u32[]{:S(2)}) collective-permute-start(bf16[4,16,1536]{2,1,0:T(8,128)(2,1)S(1)} %get-tuple-element.50), channel_id=1, source_target_pairs={{0,16},{1,17},{2,6},{3,7},{4,20},{5,21},{6,2},{7,3},{8,24},{9,25},... | collective-permute-start | bytes 589832 | tf_op jit(solution)/shard_map/ppermute | solution.py:61
  161.0 11.2 %collective-permute-start.16 = (bf16[4,16,1536]{2,1,0:T(8,128)(2,1)S(1)}, bf16[4,16,1536]{2,1,0:T(8,128)(2,1)S(1)}, u32[]{:S(2)}, u32[]{:S(2)}) collective-permute-start(bf16[4,16,1536]{2,1,0:T(8,128)(2,1)S(1)} %get-tuple-element.51), channel_id=1, source_target_pairs={{0,48},{1,49},{2,14},{3,15},{4,52},{5,53},{6,10},{7,11},{8,56},{9,... | collective-permute-start | bytes 589832 | tf_op jit(solution)/shard_map/ppermute | solution.py:61
  162.2 10.0 %collective-permute-start.17 = (bf16[4,16,1536]{2,1,0:T(8,128)(2,1)S(1)}, bf16[4,16,1536]{2,1,0:T(8,128)(2,1)S(1)}, u32[]{:S(2)}, u32[]{:S(2)}) collective-permute-start(bf16[4,16,1536]{2,1,0:T(8,128)(2,1)S(1)} %get-tuple-element.52), channel_id=1, source_target_pairs={{0,32},{1,33},{2,10},{3,11},{4,36},{5,37},{6,14},{7,15},{8,40},{9,... | collective-permute-start | bytes 589832 | tf_op jit(solution)/shard_map/ppermute | solution.py:61
  165.0 20.0 %all-to-all-start.1 = ((bf16[32,10,640]{2,1,0:T(8,128)(2,1)}), bf16[32,10,640]{2,1,0:T(8,128)(2,1)S(1)}, u32[]{:S(2)}, u32[]{:S(2)}) async-start(bf16[32,10,640]{2,1,0:T(8,128)(2,1)} %reshape.114), calls=%async_computation.1 | async-start | bytes 1310720 | tf_op jit(solution)/shard_map/all_to_all | solution.py:459
  172.4 12.8 %collective-permute-start.18 = (bf16[4,16,768]{2,1,0:T(8,128)(2,1)S(1)}, bf16[4,16,768]{2,1,0:T(8,128)(2,1)S(1)}, u32[]{:S(2)}, u32[]{:S(2)}) collective-permute-start(bf16[4,16,768]{2,1,0:T(8,128)(2,1)S(1)} %pad_maximum_fusion.15), channel_id=1, source_target_pairs={{0,1},{1,0},{2,3},{3,2},{4,5},{5,4},{6,7},{7,6},{8,9},{9,8},{10,11... | collective-permute-start | bytes 294920 | tf_op jit(solution)/shard_map/ppermute | solution.py:61
  173.9 11.3 %collective-permute-start.20 = (bf16[4,16,768]{2,1,0:T(8,128)(2,1)S(1)}, bf16[4,16,768]{2,1,0:T(8,128)(2,1)S(1)}, u32[]{:S(2)}, u32[]{:S(2)}) collective-permute-start(bf16[4,16,768]{2,1,0:T(8,128)(2,1)S(1)} %pad_maximum_fusion.16), channel_id=1, source_target_pairs={{0,64},{1,65},{2,66},{3,67},{4,68},{5,69},{6,70},{7,71},{8,72},{9,... | collective-permute-start | bytes 294920 | tf_op jit(solution)/shard_map/ppermute | solution.py:61
  176.4 8.8 %collective-permute-start.19 = (bf16[4,16,768]{2,1,0:T(8,128)(2,1)S(1)}, bf16[4,16,768]{2,1,0:T(8,128)(2,1)S(1)}, u32[]{:S(2)}, u32[]{:S(2)}) collective-permute-start(bf16[4,16,768]{2,1,0:T(8,128)(2,1)S(1)} %pad_maximum_fusion.16), channel_id=1, source_target_pairs={{0,65},{1,64},{2,67},{3,66},{4,69},{5,68},{6,71},{7,70},{8,73},{9,... | collective-permute-start | bytes 294920 | tf_op jit(solution)/shard_map/ppermute | solution.py:61
  185.3 5.1 %collective-permute-start.23 = (bf16[4,16,768]{2,1,0:T(8,128)(2,1)S(1)}, bf16[4,16,768]{2,1,0:T(8,128)(2,1)S(1)}, u32[]{:S(2)}, u32[]{:S(2)}) collective-permute-start(bf16[4,16,768]{2,1,0:T(8,128)(2,1)S(1)} %add_convert_fusion), channel_id=1, source_target_pairs={{0,48},{1,49},{2,14},{3,15},{4,52},{5,53},{6,10},{7,11},{8,56},{9,... | collective-permute-start | bytes 294920 | tf_op jit(solution)/shard_map/ppermute | solution.py:61
  186.8 5.3 %collective-permute-start.22 = (bf16[4,16,768]{2,1,0:T(8,128)(2,1)S(1)}, bf16[4,16,768]{2,1,0:T(8,128)(2,1)S(1)}, u32[]{:S(2)}, u32[]{:S(2)}) collective-permute-start(bf16[4,16,768]{2,1,0:T(8,128)(2,1)S(1)} %add_convert_fusion), channel_id=1, source_target_pairs={{0,32},{1,33},{2,10},{3,11},{4,36},{5,37},{6,14},{7,15},{8,40},{9,... | collective-permute-start | bytes 294920 | tf_op jit(solution)/shard_map/ppermute | solution.py:61
  187.8 4.3 %collective-permute-start.21 = (bf16[4,16,768]{2,1,0:T(8,128)(2,1)S(1)}, bf16[4,16,768]{2,1,0:T(8,128)(2,1)S(1)}, u32[]{:S(2)}, u32[]{:S(2)}) collective-permute-start(bf16[4,16,768]{2,1,0:T(8,128)(2,1)S(1)} %add_convert_fusion), channel_id=1, source_target_pairs={{0,16},{1,17},{2,6},{3,7},{4,20},{5,21},{6,2},{7,3},{8,24},{9,25},... | collective-permute-start | bytes 294920 | tf_op jit(solution)/shard_map/ppermute | solution.py:61
  192.1 8.5 %collective-permute-start.25 = (bf16[4,64,768]{2,1,0:T(8,128)(2,1)S(1)}, bf16[4,64,768]{2,1,0:T(8,128)(2,1)S(1)}, u32[]{:S(2)}, u32[]{:S(2)}) collective-permute-start(bf16[4,64,768]{2,1,0:T(8,128)(2,1)S(1)} %pad_maximum_fusion.13), channel_id=1, source_target_pairs={{0,8},{1,9},{2,34},{3,35},{4,12},{5,13},{6,38},{7,39},{8,0},{9,1},... | collective-permute-start | bytes 1179656 | tf_op jit(solution)/shard_map/ppermute | solution.py:61
  194.1 10.7 %collective-permute-start.26 = (bf16[4,64,768]{2,1,0:T(8,128)(2,1)S(1)}, bf16[4,64,768]{2,1,0:T(8,128)(2,1)S(1)}, u32[]{:S(2)}, u32[]{:S(2)}) collective-permute-start(bf16[4,64,768]{2,1,0:T(8,128)(2,1)S(1)} %pad_maximum_fusion.13), channel_id=1, source_target_pairs={{0,12},{1,13},{2,50},{3,51},{4,8},{5,9},{6,54},{7,55},{8,4},{9,5},... | collective-permute-start | bytes 1179656 | tf_op jit(solution)/shard_map/ppermute | solution.py:61
  195.0 9.9 %collective-permute-start.24 = (bf16[4,64,768]{2,1,0:T(8,128)(2,1)S(1)}, bf16[4,64,768]{2,1,0:T(8,128)(2,1)S(1)}, u32[]{:S(2)}, u32[]{:S(2)}) collective-permute-start(bf16[4,64,768]{2,1,0:T(8,128)(2,1)S(1)} %pad_maximum_fusion.13), channel_id=1, source_target_pairs={{0,4},{1,5},{2,18},{3,19},{4,0},{5,1},{6,22},{7,23},{8,12},{9,13},... | collective-permute-start | bytes 1179656 | tf_op jit(solution)/shard_map/ppermute | solution.py:61
  205.5 13.6 %collective-permute-start.27 = (bf16[4,256,768]{2,1,0:T(8,128)(2,1)S(1)}, bf16[4,256,768]{2,1,0:T(8,128)(2,1)}, u32[]{:S(2)}, u32[]{:S(2)}) collective-permute-start(bf16[4,256,768]{2,1,0:T(8,128)(2,1)S(1)} %pad_maximum_fusion.10), channel_id=1, source_target_pairs={{0,2},{2,0},{1,3},{3,1},{4,6},{6,4},{5,7},{7,5},{8,10},{10,8},{9,1... | collective-permute-start | bytes 4718600 | tf_op jit(solution)/shard_map/ppermute | solution.py:33
  209.3 8.4 %collective-permute-start.28 = (bf16[128,640]{1,0:T(8,128)(2,1)S(1)}, bf16[128,640]{1,0:T(8,128)(2,1)S(1)}, u32[]{:S(2)}, u32[]{:S(2)}) collective-permute-start(bf16[128,640]{1,0:T(8,128)(2,1)S(1)} %pad_maximum_fusion.14), channel_id=1, source_target_pairs={{0,64},{64,0},{1,65},{65,1},{2,66},{66,2},{3,67},{67,3},{4,68},{68... | collective-permute-start | bytes 491528 | tf_op jit(solution)/shard_map/ppermute | solution.py:465
  (6 other events, 7.7 us)
